TPU v7x, 32 devices: a whole 2x2x4 slice. The times are simulated.
32 devices in a mesh: gx: 4 (over z), gy: 8 (over y, x, core).
Axes of the slice: x: 2, y: 2, z: 4, core: 2. Of those that a mesh axis runs over, the one named last changes fastest.
Arguments:
- velocity: float32 [3, 64, 256, 512], P(None, None, 'gy', 'gx'), may hold values from -6 to 6
- pressure: float32 [64, 256, 512], P(None, 'gy', 'gx'), may hold values from -6 to 6
- memory: float32 [64, 256, 512], P(None, 'gy', 'gx'), may hold values from -4 to 4
- buoyancy: float32 [64, 256, 512], P(None, 'gy', 'gx'), may hold values from 0.1 to 0.4
- modulus: float32 [64, 256, 512], P(None, 'gy', 'gx'), may hold values from 0.1 to 0.4
- relax: float32 [64, 256, 512], P(None, 'gy', 'gx'), may hold values from 0.05 to 0.5
- strength: float32 [64, 256, 512], P(None, 'gy', 'gx'), may hold values from 0.2 to 1
- spectra: float32 [2048, 256], P(('gx', 'gy')), may hold values from -6 to 6
- patch_cell: int32 [2048], P(('gx', 'gy')), may hold values from 0 to 262143
- rupture_patches: int32 [32, 64], replicated, may hold values from -1 to 2047, as said below
- slip_weights: bfloat16 [32, 64, 512], P('gx', 'gy'), may hold values from -1 to 1
Outputs:
- velocity_out: float32 [3, 64, 256, 512], P(None, None, 'gy', 'gx')
- pressure_out: float32 [64, 256, 512], P(None, 'gy', 'gx')
- memory_out: float32 [64, 256, 512], P(None, 'gy', 'gx')
- spectra_out: float32 [2048, 256], P(('gx', 'gy'))
- slip_response: float32 [32, 512, 256], P('gx', 'gy')
Inputs may be any that keep to these rules, and one draw needn't show every extreme that they name: `patch_cell`: the cell of a patch is a flat index (z * 32 + y) * 128 + x within its brick. `rupture_patches`: each patch is listed in at most one slot. Slot (r, s) belongs to the owner at index r // 8 of gx and s // 8 of gy; of the 64 patches of one block, at most 2 are listed in the slots of any one owner, and some pairs of block and owner reach 2.
All inputs are finite; a program needn't handle non-finite values.
Results may differ from a plain program's by a relative error of at most 0.0029.
Values may be sent and summed in bfloat16 or wider, within the bound.
A program may use at most 128 MiB of HBM per device.

v0:
```python
import functools

import jax
import jax.numpy as jnp
import numpy as np
from jax import lax
from jax.experimental import pallas as pl
from jax.experimental.pallas import tpu as pltpu
from jax.sharding import PartitionSpec as P

STEPS = 4
CAP = 2
BATCH = 8


def phase_rows(freqs):
    angle = np.pi * (np.arange(freqs) + 0.5) / freqs
    rows = [np.concatenate([np.cos(angle * n), -np.sin(angle * n)]) for n in range(1, STEPS + 1)]
    return jnp.asarray(np.stack(rows).astype(np.float32))


Y_ROWS = [4] + [3] * (STEPS - 1) + [1]
X_PACKS = [3] + [2] * (STEPS - 1) + [1]


def quotient(value, size):
    if size & (size - 1):
        return lax.div(value, jnp.full_like(value, size))
    return lax.shift_right_logical(value, jnp.full_like(value, size.bit_length() - 1))


def remainder(value, size):
    if size & (size - 1):
        return lax.rem(value, jnp.full_like(value, size))
    return value & (size - 1)


def step_kernel(dims, *refs):
    nz, ny, nx, chunks, zc, per_dev, ngx, ngy = dims
    refs = list(refs)
    take = lambda count: [refs.pop(0) for _ in range(count)]
    vel_in, p_in, m_in, b_in, mod_in, rel_in, str_in, spectra, cell, cell_row, phase = take(11)
    listed, weights = take(2)
    vx, vy, vz, p, m, spectra_out, weights_got, rows_out, group_out = take(9)
    b, mod, rel, stg = take(4)
    ysend, yrecv = (take(STEPS + 1), take(STEPS + 1))
    xsend, xrecv = (take(STEPS + 1), take(STEPS + 1))
    vxh, bxh, hx, vyh, rows_got, samples = take(6)
    placing, rows_send, rows_group = take(3)
    in_sem, send_sem, recv_sem, far_send, far_recv = take(5)

    gx, gy = (lax.axis_index("gx"), lax.axis_index("gy"))
    has = [gy > 0, gy < ngy - 1, gx > 0, gx < ngx - 1]
    peer = [{"gy": gy - 1}, {"gy": gy + 1}, {"gx": gx - 1}, {"gx": gx + 1}]

    loads = [
        pltpu.make_async_copy(src, dst, in_sem.at[i])
        for i, (src, dst) in enumerate(
            [
                (p_in, p.at[pl.ds(1, nz)]),
                (b_in, b.at[pl.ds(0, nz)]),
                (vel_in.at[0], vx),
                (vel_in.at[1], vy),
                (vel_in.at[2], vz.at[pl.ds(1, nz)]),
                (rel_in, rel),
                (m_in, m),
                (str_in, stg),
                (mod_in, mod),
            ]
        )
    ]
    for load in loads:
        load.start()

    along_gx = [lax.rem(gx + k, ngx) for k in range(1, ngx)]
    along_gy = [lax.rem(gy + k, ngy) for k in range(1, ngy)]
    peers = [{"gx": other} for other in along_gx] + [{"gy": other} for other in along_gy]
    barrier = pltpu.get_barrier_semaphore()
    for other in peers:
        pl.semaphore_signal(
            barrier, inc=1, device_id=other, device_id_type=pl.DeviceIdType.MESH
        )

    plane = jnp.zeros((ny, nx), jnp.float32)
    p[0] = plane
    p[nz + 1] = plane
    p[nz + 2] = plane
    vz[0] = plane
    vz[nz + 1] = plane
    b[nz] = plane
    for side in range(4):

        @pl.when(jnp.logical_not(has[side]))
        def _():
            for r in range(STEPS + 1):
                if side < 2:
                    yrecv[r][side] = jnp.zeros(yrecv[r].shape[1:], jnp.float32)
                else:
                    xrecv[r][side - 2] = jnp.zeros(xrecv[r].shape[1:], jnp.float32)

    def copy_to(r, c, side):
        slot = side % 2
        if side < 2:
            src, dst = (ysend[r].at[slot, c], yrecv[r].at[1 - slot, c])
        else:
            src, dst = (xsend[r].at[c], xrecv[r].at[1 - slot, c])
        return pltpu.make_async_remote_copy(
            src_ref=src,
            dst_ref=dst,
            send_sem=send_sem.at[r, c, side],
            recv_sem=recv_sem.at[r, c, side - side % 2 + 1 - slot],
            device_id=peer[side],
            device_id_type=pl.DeviceIdType.MESH,
        )

    def copy_from(r, c, side):
        slot = side % 2
        if side < 2:
            src, dst = (ysend[r].at[slot, c], yrecv[r].at[slot, c])
        else:
            src, dst = (xsend[r].at[c], xrecv[r].at[slot, c])
        return pltpu.make_async_remote_copy(
            src_ref=src,
            dst_ref=dst,
            send_sem=send_sem.at[r, c, side],
            recv_sem=recv_sem.at[r, c, side],
            device_id=peer[side],
            device_id_type=pl.DeviceIdType.MESH,
        )

    def send(r, c):
        for side in range(4):

            @pl.when(has[side])
            def _():
                copy_to(r, c, side).start()

    def receive(r, c):
        for side in range(4):

            @pl.when(has[side])
            def _():
                copy_from(r, c, side).wait_recv()

    lane = lax.broadcasted_iota(jnp.int32, (ny, nx), 1)
    row = lax.broadcasted_iota(jnp.int32, (ny, nx), 0)
    quad, lane4 = (quotient(lane, 4), remainder(lane, 4))
    last_lane, first_lane = (lane == nx - 1, lane == 0)
    last_row, first_row = (row == ny - 1, row == 0)

    def pack(total, slab, zl):
        return jnp.where(quad == zl, pltpu.roll(slab, 4 * zl + 2, 1), total)

    def d_x(slab, halo, zl):
        ends = pltpu.roll(halo, nx - 2 - 4 * zl, 1)
        after = jnp.where(last_lane, ends, pltpu.roll(slab, nx - 1, 1))
        before = jnp.where(first_lane, ends, pltpu.roll(slab, 1, 1))
        return after - before

    def d_y(slab, south, north):
        after = jnp.where(last_row, north, pltpu.roll(slab, ny - 1, 0))
        before = jnp.where(first_row, south, pltpu.roll(slab, 1, 0))
        return after - before

    for load in loads[:4]:
        load.wait()
    for c in range(chunks):

        def edges(i, totals):
            pt, vt, bt = totals
            for j in range(BATCH):
                zl = i * BATCH + j
                z = c * zc + zl
                ps, vs, ws, bs = (p[z + 1], vx[z], vy[z], b[z])
                pt, vt, bt = (pack(pt, ps, zl), pack(vt, vs, zl), pack(bt, bs, zl))
                at = pl.ds(zl, 1)
                ysend[0][0, c, 0, at, :] = ps[0:1]
                ysend[0][0, c, 1, at, :] = ps[1:2]
                ysend[0][0, c, 2, at, :] = ws[0:1]
                ysend[0][0, c, 3, at, :] = bs[0:1]
                ysend[0][1, c, 0, at, :] = ps[ny - 2 : ny - 1]
                ysend[0][1, c, 1, at, :] = ps[ny - 1 : ny]
                ysend[0][1, c, 2, at, :] = ws[ny - 1 : ny]
                ysend[0][1, c, 3, at, :] = bs[ny - 1 : ny]
            return pt, vt, bt

        totals = lax.fori_loop(0, zc // BATCH, edges, (plane, plane, plane))
        for i, total in enumerate(totals):
            xsend[0][c, i] = total
        if c == 0:
            pl.semaphore_wait(barrier, len(peers))
        send(0, c)
    for load in loads[4:]:
        load.wait()

    rup_group, slot_dev, variations = weights.shape
    lanes = weights_got.shape[3]
    group_rows = ngy * CAP
    all_rows = ngx * group_rows

    def weight_block(other):
        block = other * (variations // ngy) // lanes
        return weights.at[:, :, pl.ds(pl.multiple_of(block * lanes, lanes), lanes)]

    def far(kind, k, src, dst):
        axis, size = ("gx", ngx) if kind == 1 else ("gy", ngy)
        return pltpu.make_async_remote_copy(
            src_ref=src,
            dst_ref=dst,
            send_sem=far_send.at[kind, k],
            recv_sem=far_recv.at[kind, k],
            device_id={axis: lax.rem(lax.axis_index(axis) + k, size)},
            device_id_type=pl.DeviceIdType.MESH,
        )

    def rows_of(ref, index, count):
        return ref.at[pl.ds(pl.multiple_of(index * count, count), count)]

    def weights_to(k):
        return far(0, k, weight_block(lax.rem(gy + k, ngy)), weights_got.at[gy])

    def weights_from(k):
        return far(0, k, weight_block(gy), weights_got.at[lax.rem(gy + ngy - k, ngy)])

    def first_to(k):
        src = rows_of(rows_send, lax.rem(gx + k, ngx), group_rows)
        return far(1, k, src, rows_of(rows_group, gx, group_rows))

    def first_from(k):
        src = rows_of(rows_send, gx, group_rows)
        return far(1, k, src, rows_of(rows_group, lax.rem(gx + ngx - k, ngx), group_rows))

    def second_to(k):
        return far(2, k, rows_group, rows_of(rows_out, gy, all_rows))

    def second_from(k):
        return far(2, k, rows_group, rows_of(rows_out, lax.rem(gy + ngy - k, ngy), all_rows))

    for k in range(1, ngy):
        weights_to(k).start()
    own_weights = pltpu.make_async_copy(weight_block(gy), weights_got.at[gy], far_send.at[0, 0])
    own_weights.start()

    square = (per_dev, per_dev)
    eye = lax.broadcasted_iota(jnp.int32, square, 0) == lax.broadcasted_iota(jnp.int32, square, 1)

    def to_row(column):
        return jnp.sum(jnp.where(eye, column, 0.0), axis=0, keepdims=True)

    def to_column(line):
        return jnp.sum(jnp.where(eye, line, 0.0), axis=1, keepdims=True)

    def fill_placing():
        ruptures, slots = listed.shape
        shape = (per_dev, slots)
        own_ids = lax.broadcasted_iota(jnp.int32, shape, 0) + (gx * ngy + gy) * per_dev
        slot_owner = quotient(lax.broadcasted_iota(jnp.int32, shape, 1), slot_dev)

        def body(r, best):
            owner = quotient(r, rup_group) * ngy + slot_owner
            return jnp.where(listed[pl.ds(r, 1), :] == own_ids, owner, best)

        best = lax.fori_loop(0, ruptures, body, jnp.full(shape, -1, jnp.int32))
        target = jnp.max(best.astype(jnp.float32), axis=1, keepdims=True)
        before = lax.broadcasted_iota(jnp.int32, square, 1) < lax.broadcasted_iota(
            jnp.int32, square, 0
        )
        same = (to_row(target) == target) & before
        rank = jnp.sum(jnp.where(same, 1.0, 0.0), axis=1, keepdims=True)
        bucket = to_row(jnp.where(target >= 0.0, target * CAP + rank, -1.0))
        place = lax.broadcasted_iota(jnp.int32, placing.shape, 0).astype(jnp.float32)
        placing[...] = jnp.where(place == bucket, 1.0, 0.0).astype(jnp.bfloat16)

    def halos(r, c):
        def joined(i):
            return jnp.where(lane4 < 2, xrecv[r][0, c, i], xrecv[r][1, c, i])

        def swapped(halo):
            return jnp.where(lane4 == 1, pltpu.roll(halo, nx - 1, 1), pltpu.roll(halo, 1, 1))

        outer, own = (joined(0), xsend[r][c, 0])
        if r == 0:
            vh, bh = (joined(1), joined(2))
            bxh[c] = bh
            vyh[0, c] = yrecv[0][0, c, 2]
            vyh[1, c] = yrecv[0][1, c, 2]
        else:
            vh, bh = (vxh[c], bxh[c])
        slope = jnp.where(
            lane4 == 1,
            pltpu.roll(own, nx - 1, 1) - pltpu.roll(outer, 1, 1),
            pltpu.roll(outer, nx - 1, 1) - pltpu.roll(own, 1, 1),
        )
        vh = vh - bh * slope
        vxh[c] = vh
        hx[0, c] = swapped(outer)
        hx[1, c] = swapped(vh)
        vyh[0, c] = vyh[0, c] - yrecv[0][0, c, 3] * (ysend[r][0, c, 0] - yrecv[r][0, c, 0])
        vyh[1, c] = vyh[1, c] - yrecv[0][1, c, 3] * (yrecv[r][1, c, 1] - ysend[r][1, c, 1])

    def sweep(r, c):
        last = r == STEPS - 1
        n = r + 1

        def body(i, totals):
            pt, wt = totals
            base = i * BATCH
            z0 = c * zc + base
            ps = [p[z0 + 1 + j] for j in range(BATCH + 2)]
            bs = [b[z0 + j] for j in range(BATCH + 1)]
            zs = [vz[z0], vz[z0 + 1]]
            vs, ws, new_p = ([], [], [])
            for j in range(BATCH):
                zl = base + j
                at = pl.ds(zl, 1)
                zs.append(vz[z0 + j + 2] - bs[j + 1] * (ps[j + 2] - ps[j]))
                vs.append(vx[z0 + j] - bs[j] * d_x(ps[j], hx[0, c], zl))
                south, north = (yrecv[r][0, c, 1, at, :], yrecv[r][1, c, 0, at, :])
                ws.append(vy[z0 + j] - bs[j] * d_y(ps[j], south, north))
            for j in range(BATCH):
                zl = base + j
                at = pl.ds(zl, 1)
                spread = d_x(vs[j], hx[1, c], zl) + d_y(ws[j], vyh[0, c, at, :], vyh[1, c, at, :])
                spread = spread + (zs[j + 2] - zs[j])
                mem = m[z0 + j]
                mem = mem - rel[z0 + j] * (mem + stg[z0 + j] * spread)
                m[z0 + j] = mem
                new_p.append(ps[j] - mod[z0 + j] * (spread + mem))
            for j in range(BATCH):
                zl = base + j
                at = pl.ds(zl, 1)
                vz[z0 + j + 2] = zs[j + 2]
                vx[z0 + j] = vs[j]
                vy[z0 + j] = ws[j]
                p[z0 + j + 1] = new_p[j]
                wt = pack(wt, ws[j], zl)
                ysend[n][0, c, 0 if last else 2, at, :] = vs[j][0:1]
                ysend[n][1, c, 0 if last else 2, at, :] = vs[j][ny - 1 : ny]
                if not last:
                    pt = pack(pt, new_p[j], zl)
                    ysend[n][0, c, 0, at, :] = new_p[j][0:1]
                    ysend[n][0, c, 1, at, :] = new_p[j][1:2]
                    ysend[n][1, c, 0, at, :] = new_p[j][ny - 2 : ny - 1]
                    ysend[n][1, c, 1, at, :] = new_p[j][ny - 1 : ny]
            return pt, wt

        pt, wt = lax.fori_loop(0, zc // BATCH, body, (plane, plane))
        if last:
            xsend[n][c, 0] = wt
        else:
            xsend[n][c, 0] = pt
            xsend[n][c, 1] = wt

    fill_placing()
    cells = to_column(cell_row[...].astype(jnp.float32)).astype(jnp.int32)
    cell_z, cell_x = (quotient(cells, ny * nx), remainder(cells, nx))
    cell_y = remainder(quotient(cells, nx), ny)
    patch_lane = lax.broadcasted_iota(jnp.int32, (per_dev, nx), 1)

    def masked(keep, values):
        return jnp.where(keep, values, 0.0)

    def sample_own(n):
        def body(i, carry):
            at = cell[i]
            z, y = (quotient(at, ny * nx), remainder(quotient(at, nx), ny))
            out = pl.ds(i, 1)
            rows_got[0, out, :] = vx[z, pl.ds(jnp.minimum(y + 1, ny - 1), 1), :]
            rows_got[1, out, :] = vx[z, pl.ds(jnp.maximum(y - 1, 0), 1), :]
            rows_got[2, out, :] = vy[z, pl.ds(y, 1), :]
            return carry

        lax.fori_loop(0, per_dev, body, 0, unroll=8)
        along = masked(cell_y < ny - 1, rows_got[0]) - masked(cell_y > 0, rows_got[1])
        across = rows_got[2]
        total = masked(patch_lane == cell_x, along)
        total = total + masked(patch_lane == cell_x + 1, across)
        samples[n - 1] = total - masked(patch_lane == cell_x - 1, across)

    def sample_halo(n):
        which_row, which_pack = (Y_ROWS[n] - 1, X_PACKS[n] - 1)

        def body(i, carry):
            at = cell[i]
            z, y = (quotient(at, ny * nx), remainder(quotient(at, nx), ny))
            c, zl = (quotient(z, zc), remainder(z, zc))
            out = pl.ds(i, 1)
            rows_got[0, out, :] = yrecv[n][0, c, which_row, pl.ds(zl, 1), :]
            rows_got[1, out, :] = yrecv[n][1, c, which_row, pl.ds(zl, 1), :]
            rows_got[2, out, :] = xrecv[n][0, c, which_pack, pl.ds(y, 1), :]
            rows_got[3, out, :] = xrecv[n][1, c, which_pack, pl.ds(y, 1), :]
            return carry

        lax.fori_loop(0, per_dev, body, 0, unroll=8)
        start = 4 * remainder(cell_z, zc)
        here = patch_lane == cell_x
        total = samples[n - 1]
        total = total + masked(here & (cell_y == ny - 1), rows_got[1])
        total = total - masked(here & (cell_y == 0), rows_got[0])
        total = total + masked((patch_lane == start + 2) & (cell_x == nx - 1), rows_got[3])
        total = total - masked((patch_lane == start + 1) & (cell_x == 0), rows_got[2])
        value = jnp.sum(total, axis=1, keepdims=True)
        spectra_out[...] = spectra_out[...] + value * phase[n - 1 : n, :]

    spectra_out[...] = spectra[...]
    rup = pl.ds(pl.multiple_of(gx * rup_group, rup_group), rup_group)
    group_out[...] = listed[rup, :]
    for r in range(STEPS):
        vz[1] = vz[1] - b[0] * (p[2] - p[0])
        for c in range(chunks):
            receive(r, c)
            halos(r, c)
            sweep(r, c)
            send(r + 1, c)
        sample_own(r + 1)
        if r > 0:
            sample_halo(r)
    for c in range(chunks):
        receive(STEPS, c)
    sample_halo(STEPS)
    rows_send[...] = jnp.dot(
        placing[...], spectra_out[...].astype(jnp.bfloat16), preferred_element_type=jnp.float32
    ).astype(jnp.bfloat16)
    for k in range(1, ngx):
        first_to(k).start()
    at = pl.ds(pl.multiple_of(gx * group_rows, group_rows), group_rows)
    rows_group[at, :] = rows_send[at, :]
    for k in range(1, ngx):
        first_from(k).wait_recv()
    for k in range(1, ngy):
        second_to(k).start()
    at = pl.ds(pl.multiple_of(gy * all_rows, all_rows), all_rows)
    rows_out[at, :] = rows_group[...]
    own_weights.wait()
    for k in range(1, ngy):
        weights_from(k).wait_recv()
        weights_to(k).wait_send()
    for k in range(1, ngy):
        second_from(k).wait_recv()
        second_to(k).wait_send()
    for k in range(1, ngx):
        first_to(k).wait_send()
    for r in range(STEPS + 1):
        for c in range(chunks):
            for side in range(4):

                @pl.when(has[side])
                def _():
                    copy_to(r, c, side).wait_send()


def finish_kernel(dims, *refs):
    nz, per_dev, ngx, ngy, slot_dev = dims
    refs = list(refs)
    take = lambda count: [refs.pop(0) for _ in range(count)]
    vx, vy, vz, p, m, spectra, weights, rows, group = take(9)
    vel_out, p_out, m_out, spectra_out, slip_out = take(5)
    table, slots, wide, slip, out_sem, slip_sem = take(6)
    rup_group, slot_count = group.shape
    share, lanes = (slip.shape[1], weights.shape[3])
    inner = pl.ds(1, nz)
    pairs = [
        (vx, vel_out.at[0]),
        (vy, vel_out.at[1]),
        (vz.at[inner], vel_out.at[2]),
        (p.at[inner], p_out),
        (m, m_out),
        (spectra, spectra_out),
    ]
    stores = [
        pltpu.make_async_copy(src, dst, out_sem.at[i]) for i, (src, dst) in enumerate(pairs)
    ]
    for store in stores:
        store.start()

    shape = (rup_group, table.shape[1])
    lane = lax.broadcasted_iota(jnp.int32, shape, 1)
    owner, place = (quotient(lane, slot_dev), remainder(lane, slot_dev))
    table[...] = jnp.full(shape, -1, jnp.int32)
    table[:, :slot_count] = group[...]
    ids = table[...]
    source = quotient(ids, per_dev)
    turned = [ids] + [pltpu.roll(ids, k, 0) for k in range(1, rup_group)]

    def earlier(i, rank):
        shift = i - (slot_dev - 1)
        inside = (place >= shift) & (place < shift + slot_dev)
        turn = jnp.where(shift < 0, shift + shape[1], shift)
        for other in turned:
            other = pltpu.roll(other, turn, 1)
            found = inside & (other < ids) & (quotient(other, per_dev) == source)
            rank = jnp.where(found, 1, rank)
        return rank

    rank = lax.fori_loop(0, 2 * slot_dev - 1, earlier, jnp.zeros(shape, jnp.int32))
    block = remainder(source, ngy) * ngx + quotient(source, ngy)
    table[...] = jnp.where(ids >= 0, (block * ngy + owner) * CAP + rank, -1)

    size = min(slot_count, 128)
    square = (size, size)
    eye = lax.broadcasted_iota(jnp.int32, square, 0) == lax.broadcasted_iota(jnp.int32, square, 1)
    row_at = lax.broadcasted_iota(jnp.int32, (size, rows.shape[0]), 1)
    start = pl.multiple_of(remainder(lax.axis_index("gy") * share, lanes), share)

    def respond(r, carry):
        lines = table[pl.ds(r, 1), :].astype(jnp.float32)
        for k in range(slot_count // size):
            line = lines[:, k * size : (k + 1) * size]
            column = jnp.sum(jnp.where(eye, line, 0.0), axis=1, keepdims=True).astype(jnp.int32)
            chosen = jnp.where(row_at == column, 1.0, 0.0).astype(jnp.bfloat16)
            picked = jnp.dot(chosen, rows[...], preferred_element_type=jnp.float32)
            slots[pl.ds(k * size, size), :] = picked.astype(jnp.bfloat16)
        own = weights[:, r].astype(jnp.float32).reshape(slot_count, lanes).astype(jnp.bfloat16)
        wide[...] = lax.dot_general(
            own, slots[...], (((0,), (0,)), ((), ())), preferred_element_type=jnp.float32
        )
        slip[r] = wide[pl.ds(start, share), :]
        pltpu.make_async_copy(slip.at[r], slip_out.at[r], slip_sem.at[r]).start()
        return carry

    lax.fori_loop(0, rup_group, respond, 0)
    for store in stores:
        store.wait()
    for r in range(rup_group):
        pltpu.make_async_copy(slip.at[r], slip_out.at[r], slip_sem.at[r]).wait()


VMEM_LIMIT = 40 * 1024 * 1024


def in_hbm(x):
    return pltpu.with_memory_space_constraint(x, pltpu.HBM)


def advance(
    velocity, pressure, memory, buoyancy, modulus, relax, strength, spectra, patch_cell, listed, weights
):
    nz, ny, nx = pressure.shape
    per_dev, width = spectra.shape
    zc = nx // 4
    chunks = nz // zc
    ngx, ngy = (lax.axis_size("gx"), lax.axis_size("gy"))
    dims = (nz, ny, nx, chunks, zc, per_dev, ngx, ngy)
    rup_group, slot_dev, variations = weights.shape
    lanes = max(variations // ngy, 128)
    all_rows = ngx * ngy * CAP
    f32 = jnp.float32
    field = lambda planes: pltpu.VMEM((planes, ny, nx), f32)
    rounds = range(STEPS + 1)
    any_spec = pl.BlockSpec(memory_space=pl.ANY)
    vmem_spec = pl.BlockSpec(memory_space=pltpu.VMEM)
    return pl.pallas_call(
        functools.partial(step_kernel, dims),
        out_shape=[
            field(nz),
            field(nz),
            field(nz + 2),
            field(nz + 3),
            field(nz),
            pltpu.VMEM(spectra.shape, f32),
            pltpu.VMEM((ngy, rup_group, slot_dev, lanes), jnp.bfloat16),
            pltpu.VMEM((ngy * all_rows, width), jnp.bfloat16),
            pltpu.VMEM((rup_group, listed.shape[1]), jnp.int32),
        ],
        in_specs=[any_spec] * 7
        + [vmem_spec, pl.BlockSpec(memory_space=pltpu.SMEM)]
        + [vmem_spec] * 4,
        out_specs=[vmem_spec] * 9,
        scratch_shapes=[field(nz + 1), field(nz), field(nz), field(nz)]
        + [pltpu.VMEM((2, chunks, Y_ROWS[r], zc, nx), f32) for r in rounds]
        + [pltpu.VMEM((2, chunks, Y_ROWS[r], zc, nx), f32) for r in rounds]
        + [pltpu.VMEM((chunks, X_PACKS[r], ny, nx), f32) for r in rounds]
        + [pltpu.VMEM((2, chunks, X_PACKS[r], ny, nx), f32) for r in rounds]
        + [
            pltpu.VMEM((chunks, ny, nx), f32),
            pltpu.VMEM((chunks, ny, nx), f32),
            pltpu.VMEM((2, chunks, ny, nx), f32),
            pltpu.VMEM((2, chunks, zc, nx), f32),
            pltpu.VMEM((4, per_dev, nx), f32),
            pltpu.VMEM((STEPS, per_dev, nx), f32),
            pltpu.VMEM((all_rows, per_dev), jnp.bfloat16),
            pltpu.VMEM((all_rows, width), jnp.bfloat16),
            pltpu.VMEM((all_rows, width), jnp.bfloat16),
            pltpu.SemaphoreType.DMA((9,)),
            pltpu.SemaphoreType.DMA((STEPS + 1, chunks, 4)),
            pltpu.SemaphoreType.DMA((STEPS + 1, chunks, 4)),
            pltpu.SemaphoreType.DMA((3, max(ngx, ngy))),
            pltpu.SemaphoreType.DMA((3, max(ngx, ngy))),
        ],
        compiler_params=pltpu.CompilerParams(
            collective_id=0, has_side_effects=True, vmem_limit_bytes=VMEM_LIMIT
        ),
    )(
        *[in_hbm(x) for x in (velocity, pressure, memory, buoyancy, modulus, relax, strength)],
        in_hbm(spectra),
        patch_cell,
        in_hbm(patch_cell.reshape(1, -1)),
        in_hbm(phase_rows(width // 2)),
        in_hbm(listed),
        in_hbm(weights),
    )


def finish(state, velocity, pressure, memory, spectra, weights):
    nz = pressure.shape[0]
    per_dev, width = spectra.shape
    ngx, ngy = (lax.axis_size("gx"), lax.axis_size("gy"))
    rup_group, slot_dev, variations = weights.shape
    slot_count = slot_dev * ngy
    share = variations // ngy
    lanes = max(share, 128)
    f32 = jnp.float32
    any_spec = pl.BlockSpec(memory_space=pl.ANY)
    vmem_spec = pl.BlockSpec(memory_space=pltpu.VMEM)
    return pl.pallas_call(
        functools.partial(finish_kernel, (nz, per_dev, ngx, ngy, slot_dev)),
        out_shape=[
            jax.ShapeDtypeStruct(velocity.shape, f32),
            jax.ShapeDtypeStruct(pressure.shape, f32),
            jax.ShapeDtypeStruct(memory.shape, f32),
            jax.ShapeDtypeStruct(spectra.shape, f32),
            jax.ShapeDtypeStruct((rup_group, share, width), f32),
        ],
        in_specs=[vmem_spec] * len(state),
        out_specs=[any_spec] * 5,
        scratch_shapes=[
            pltpu.VMEM((rup_group, max(slot_count, 128)), jnp.int32),
            pltpu.VMEM((slot_count, width), jnp.bfloat16),
            pltpu.VMEM((lanes, width), f32),
            pltpu.VMEM((rup_group, share, width), f32),
            pltpu.SemaphoreType.DMA((6,)),
            pltpu.SemaphoreType.DMA((rup_group,)),
        ],
        compiler_params=pltpu.CompilerParams(vmem_limit_bytes=VMEM_LIMIT),
    )(*[pltpu.with_memory_space_constraint(x, pltpu.VMEM) for x in state])


def per_device(
    velocity,
    pressure,
    memory,
    buoyancy,
    modulus,
    relax,
    strength,
    spectra,
    patch_cell,
    rupture_patches,
    slip_weights,
):
    state = advance(
        velocity,
        pressure,
        memory,
        buoyancy,
        modulus,
        relax,
        strength,
        spectra,
        patch_cell,
        rupture_patches,
        slip_weights,
    )
    return tuple(finish(state, velocity, pressure, memory, spectra, slip_weights))


def solution(mesh):
    in_specs = (
        P(None, None, "gy", "gx"),
        P(None, "gy", "gx"),
        P(None, "gy", "gx"),
        P(None, "gy", "gx"),
        P(None, "gy", "gx"),
        P(None, "gy", "gx"),
        P(None, "gy", "gx"),
        P(("gx", "gy"), None),
        P(("gx", "gy")),
        P(),
        P("gx", "gy", None),
    )
    out_specs = (
        P(None, None, "gy", "gx"),
        P(None, "gy", "gx"),
        P(None, "gy", "gx"),
        P(("gx", "gy"), None),
        P("gx", "gy", None),
    )
    return jax.shard_map(
        per_device, mesh=mesh, in_specs=in_specs, out_specs=out_specs, check_vma=False
    )
```

profile of v0, /device:TPU:0, one launch (start us, length us, event | category | flops | bytes accessed | tf_op | source)
XLA Modules:
  0.0 45.8 jit_solution(16146322179501745522)
XLA Ops:
  0.6 39.9 %shard_map.155 = (f32[64,32,128]{2,1,0:T(8,128)S(1)}, f32[64,32,128]{2,1,0:T(8,128)S(1)}, f32[66,32,128]{2,1,0:T(8,128)S(1)}, f32[67,32,128]{2,1,0:T(8,128)S(1)}...) custom-call(f32[3,64,32,128]{3,2,1,0:T(8,128)} %refs_0_.1, ...), custom_call_target="tpu_custom_call" | custom-call | tf_op jit(solution)/shard_map/pallas_call | solution.py:552
  40.5 5.3 %shard_map.156 = (f32[3,64,32,128]{3,2,1,0:T(8,128)}, f32[64,32,128]{2,1,0:T(8,128)}, f32[64,32,128]{2,1,0:T(8,128)}, f32[64,256]{1,0:T(8,128)}, f32[8,64,256]{2,1,0:T(8,128)}) custom-call(f32[64,32,128]{2,1,0:T(8,128)S(1)} %get-tuple-element.14.refs_0_, f32[64,32,128]{2,1,0:T(8,128)S(1)} %get-tuple-element.15.refs_1_, ...), custom_call_target="tpu_custom_call" | custom-call | tf_op jit(solution)/shard_map/pallas_call | solution.py:615
where the time goes:
time: 46 us; the launch traced here: 45.8 us
  Pallas kernels  45.2 us (98%)
  between operations  0.64 us (1%)
    pallas_call x1, Pallas kernels, advance(): pl.pallas_call(functools.partial(step_kernel, dims), out_shape=[field(nz)...  39.9 us
    pallas_call x1, Pallas kernels, finish(): pl.pallas_call(functools.partial(finish_kernel, (nz, per_dev, ngx, ngy, s...  5.3 us

commit v1 on v0

v1 whole, which is shorter than its diff:
```python
import functools

import jax
import jax.numpy as jnp
import numpy as np
from jax import lax
from jax.experimental import pallas as pl
from jax.experimental.pallas import tpu as pltpu
from jax.sharding import PartitionSpec as P

STEPS = 4
CAP = 2
BATCH = 8


def phase_rows(freqs):
    angle = np.pi * (np.arange(freqs) + 0.5) / freqs
    rows = [np.concatenate([np.cos(angle * n), -np.sin(angle * n)]) for n in range(1, STEPS + 1)]
    return jnp.asarray(np.stack(rows).astype(np.float32))


Y_ROWS = [4, 3] + [2] * (STEPS - 2)
X_PACKS = [3, 2] + [1] * (STEPS - 2)


def quotient(value, size):
    if size & (size - 1):
        return lax.div(value, jnp.full_like(value, size))
    return lax.shift_right_logical(value, jnp.full_like(value, size.bit_length() - 1))


def remainder(value, size):
    if size & (size - 1):
        return lax.rem(value, jnp.full_like(value, size))
    return value & (size - 1)


def step_kernel(dims, *refs):
    nz, ny, nx, chunks, zc, per_dev, ngx, ngy = dims
    refs = list(refs)
    take = lambda count: [refs.pop(0) for _ in range(count)]
    vel_in, p_in, m_in, b_in, mod_in, rel_in, str_in = take(7)
    spectra_in, cell_in, cell_row_in, phase_in, listed_in, weights = take(6)
    vx, vy, vz, p, m, spectra_out, weights_got, rows_out, table = take(9)
    b, mod, rel, stg = take(4)
    ysend, yrecv = (take(STEPS), take(STEPS))
    xsend, xrecv = (take(STEPS), take(STEPS))
    csend, crecv = (take(STEPS - 1), take(STEPS - 1))
    cell, cell_row, phase, listed = take(4)
    vxh, bxh, hx, vyh, vyx, xj, got, shear, factors = take(9)
    placing, rows_send, rows_group = take(3)
    in_sem, small_sem, send_sem, recv_sem, far_send, far_recv = take(6)

    gx, gy = (lax.axis_index("gx"), lax.axis_index("gy"))
    has = [gy > 0, gy < ngy - 1, gx > 0, gx < ngx - 1]
    has = has + [has[k // 2] & has[2 + k % 2] for k in range(4)]
    peer = [{"gy": gy - 1}, {"gy": gy + 1}, {"gx": gx - 1}, {"gx": gx + 1}]
    peer = peer + [{**peer[k // 2], **peer[2 + k % 2]} for k in range(4)]

    def load(i, c):
        at = pl.ds(c * zc, zc)
        moved = pl.ds(c * zc + 1, zc)
        src, dst = [
            (p_in.at[at], p.at[moved]),
            (b_in.at[at], b.at[at]),
            (vel_in.at[0, at], vx.at[at]),
            (vel_in.at[1, at], vy.at[at]),
            (vel_in.at[2, at], vz.at[moved]),
            (rel_in.at[at], rel.at[at]),
            (m_in.at[at], m.at[at]),
            (str_in.at[at], stg.at[at]),
            (mod_in.at[at], mod.at[at]),
        ][i]
        return pltpu.make_async_copy(src, dst, in_sem.at[i, c])

    smalls = [
        pltpu.make_async_copy(src, dst, small_sem.at[i])
        for i, (src, dst) in enumerate(
            [
                (cell_in, cell),
                (cell_row_in, cell_row),
                (listed_in, listed),
                (phase_in, phase),
                (spectra_in, spectra_out),
            ]
        )
    ]
    for c in range(chunks):
        for i in range(4):
            load(i, c).start()
    for c in range(chunks):
        for i in range(4, 9):
            load(i, c).start()
    for small in smalls:
        small.start()

    along_gx = [lax.rem(gx + k, ngx) for k in range(1, ngx)]
    along_gy = [lax.rem(gy + k, ngy) for k in range(1, ngy)]
    peers = [{"gx": other} for other in along_gx] + [{"gy": other} for other in along_gy]
    peers = peers + [
        {"gy": lax.rem(gy + ngy + dy, ngy), "gx": lax.rem(gx + ngx + dx, ngx)}
        for dy in (-1, 1)
        for dx in (-1, 1)
    ]
    barrier = pltpu.get_barrier_semaphore()
    for other in peers:
        pl.semaphore_signal(
            barrier, inc=1, device_id=other, device_id_type=pl.DeviceIdType.MESH
        )

    plane = jnp.zeros((ny, nx), jnp.float32)
    p[0] = plane
    p[nz + 1] = plane
    p[nz + 2] = plane
    vz[0] = plane
    vz[nz + 1] = plane
    b[nz] = plane
    for side in range(8):

        @pl.when(jnp.logical_not(has[side]))
        def _():
            for r in range(STEPS):
                if side < 2:
                    yrecv[r][side] = jnp.zeros(yrecv[r].shape[1:], jnp.float32)
                elif side < 4:
                    xrecv[r][side - 2] = jnp.zeros(xrecv[r].shape[1:], jnp.float32)
                elif r > 0:
                    for c in range(chunks):
                        crecv[r - 1][c, side - 4] = jnp.zeros((1, nx), jnp.float32)

    def ends(r, c, side, coming):
        k = side % 4
        if side < 2:
            there = side if coming else 1 - side
            src, dst = (ysend[r].at[side, c], yrecv[r].at[there, c])
            arrives = there
        elif side < 4:
            there = k - 2 if coming else 3 - k
            src, dst = (xsend[r].at[c], xrecv[r].at[there, c])
            arrives = 2 + there
        else:
            there = k if coming else 3 - k
            src, dst = (csend[r - 1].at[c, k // 2], crecv[r - 1].at[c, there])
            arrives = 4 + there
        return pltpu.make_async_remote_copy(
            src_ref=src,
            dst_ref=dst,
            send_sem=send_sem.at[r, c, side],
            recv_sem=recv_sem.at[r, c, arrives],
            device_id=peer[side],
            device_id_type=pl.DeviceIdType.MESH,
        )

    def sides(r):
        return range(4) if r == 0 else range(8)

    def send(r, c):
        for side in sides(r):

            @pl.when(has[side])
            def _():
                ends(r, c, side, False).start()

    def receive(r, c):
        for side in sides(r):

            @pl.when(has[side])
            def _():
                ends(r, c, side, True).wait_recv()

    lane = lax.broadcasted_iota(jnp.int32, (ny, nx), 1)
    row = lax.broadcasted_iota(jnp.int32, (ny, nx), 0)
    quad, lane4 = (quotient(lane, 4), remainder(lane, 4))
    last_lane, first_lane = (lane == nx - 1, lane == 0)
    last_row, first_row = (row == ny - 1, row == 0)
    west_half = remainder(lax.broadcasted_iota(jnp.int32, (1, nx), 1), 4) < 2

    def pack(total, slab, zl):
        return jnp.where(quad == zl, pltpu.roll(slab, 4 * zl + 2, 1), total)

    def d_x(slab, halo, zl):
        ends = pltpu.roll(halo, nx - 2 - 4 * zl, 1)
        after = jnp.where(last_lane, ends, pltpu.roll(slab, nx - 1, 1))
        before = jnp.where(first_lane, ends, pltpu.roll(slab, 1, 1))
        return after - before

    def d_y(slab, south, north):
        after = jnp.where(last_row, north, pltpu.roll(slab, ny - 1, 0))
        before = jnp.where(first_row, south, pltpu.roll(slab, 1, 0))
        return after - before

    for c in range(chunks):
        for i in range(4):
            load(i, c).wait()

        def edges(i, totals):
            pt, vt, bt = totals
            for j in range(BATCH):
                zl = i * BATCH + j
                z = c * zc + zl
                ps, vs, ws, bs = (p[z + 1], vx[z], vy[z], b[z])
                pt, vt, bt = (pack(pt, ps, zl), pack(vt, vs, zl), pack(bt, bs, zl))
                at = pl.ds(zl, 1)
                ysend[0][0, c, 0, at, :] = ps[0:1]
                ysend[0][0, c, 1, at, :] = ps[1:2]
                ysend[0][0, c, 2, at, :] = ws[0:1]
                ysend[0][0, c, 3, at, :] = bs[0:1]
                ysend[0][1, c, 0, at, :] = ps[ny - 2 : ny - 1]
                ysend[0][1, c, 1, at, :] = ps[ny - 1 : ny]
                ysend[0][1, c, 2, at, :] = ws[ny - 1 : ny]
                ysend[0][1, c, 3, at, :] = bs[ny - 1 : ny]
            return pt, vt, bt

        totals = lax.fori_loop(0, zc // BATCH, edges, (plane, plane, plane))
        for i, total in enumerate(totals):
            xsend[0][c, i] = total
        if c == 0:
            pl.semaphore_wait(barrier, len(peers))
        send(0, c)

    rup_group, slot_dev, variations = weights.shape
    lanes = weights_got.shape[3]
    group_rows = ngy * CAP
    all_rows = ngx * group_rows

    def weight_block(other):
        block = other * (variations // ngy) // lanes
        return weights.at[:, :, pl.ds(pl.multiple_of(block * lanes, lanes), lanes)]

    def far(kind, k, src, dst):
        axis, size = ("gx", ngx) if kind == 1 else ("gy", ngy)
        return pltpu.make_async_remote_copy(
            src_ref=src,
            dst_ref=dst,
            send_sem=far_send.at[kind, k],
            recv_sem=far_recv.at[kind, k],
            device_id={axis: lax.rem(lax.axis_index(axis) + k, size)},
            device_id_type=pl.DeviceIdType.MESH,
        )

    def rows_of(ref, index, count):
        return ref.at[pl.ds(pl.multiple_of(index * count, count), count)]

    def weights_to(k):
        return far(0, k, weight_block(lax.rem(gy + k, ngy)), weights_got.at[gy])

    def weights_from(k):
        return far(0, k, weight_block(gy), weights_got.at[lax.rem(gy + ngy - k, ngy)])

    def first_to(k):
        src = rows_of(rows_send, lax.rem(gx + k, ngx), group_rows)
        return far(1, k, src, rows_of(rows_group, gx, group_rows))

    def first_from(k):
        src = rows_of(rows_send, gx, group_rows)
        return far(1, k, src, rows_of(rows_group, lax.rem(gx + ngx - k, ngx), group_rows))

    def second_to(k):
        return far(2, k, rows_group, rows_of(rows_out, gy, all_rows))

    def second_from(k):
        return far(2, k, rows_group, rows_of(rows_out, lax.rem(gy + ngy - k, ngy), all_rows))

    for k in range(1, ngy):
        weights_to(k).start()
    own_weights = pltpu.make_async_copy(weight_block(gy), weights_got.at[gy], far_send.at[0, 0])
    own_weights.start()

    square = (per_dev, per_dev)
    eye = lax.broadcasted_iota(jnp.int32, square, 0) == lax.broadcasted_iota(jnp.int32, square, 1)

    def to_row(column):
        return jnp.sum(jnp.where(eye, column, 0.0), axis=0, keepdims=True)

    def to_column(line):
        return jnp.sum(jnp.where(eye, line, 0.0), axis=1, keepdims=True)

    def fill_placing():
        ruptures, slots = listed.shape
        shape = (per_dev, slots)
        own_ids = lax.broadcasted_iota(jnp.int32, shape, 0) + (gx * ngy + gy) * per_dev
        slot_owner = quotient(lax.broadcasted_iota(jnp.int32, shape, 1), slot_dev)

        def body(r, best):
            owner = quotient(r, rup_group) * ngy + slot_owner
            return jnp.where(listed[pl.ds(r, 1), :] == own_ids, owner, best)

        best = lax.fori_loop(0, ruptures, body, jnp.full(shape, -1, jnp.int32))
        target = jnp.max(best.astype(jnp.float32), axis=1, keepdims=True)
        before = lax.broadcasted_iota(jnp.int32, square, 1) < lax.broadcasted_iota(
            jnp.int32, square, 0
        )
        same = (to_row(target) == target) & before
        rank = jnp.sum(jnp.where(same, 1.0, 0.0), axis=1, keepdims=True)
        bucket = to_row(jnp.where(target >= 0.0, target * CAP + rank, -1.0))
        place = lax.broadcasted_iota(jnp.int32, placing.shape, 0).astype(jnp.float32)
        placing[...] = jnp.where(place == bucket, 1.0, 0.0).astype(jnp.bfloat16)

    def fill_table():
        slot_count = listed.shape[1]
        shape = table.shape
        spot = lax.broadcasted_iota(jnp.int32, shape, 1)
        owner, place = (quotient(spot, slot_dev), remainder(spot, slot_dev))
        table[...] = jnp.full(shape, -1, jnp.int32)
        group = pl.ds(pl.multiple_of(gx * rup_group, rup_group), rup_group)
        table[:, :slot_count] = listed[group, :]
        ids = table[...]
        source = quotient(ids, per_dev)

        def earlier(i, rank):
            shift = i - (slot_dev - 1)
            inside = (place >= shift) & (place < shift + slot_dev)
            turned = pltpu.roll(ids, jnp.where(shift < 0, shift + shape[1], shift), 1)
            for k in range(rup_group):
                other = pltpu.roll(turned, k, 0) if k else turned
                found = inside & (other < ids) & (quotient(other, per_dev) == source)
                rank = jnp.where(found, 1, rank)
            return rank

        shifts = 2 * slot_dev - 1
        unroll = max(k for k in range(1, 16) if shifts % k == 0)
        rank = lax.fori_loop(0, shifts, earlier, jnp.zeros(shape, jnp.int32), unroll=unroll)
        block = remainder(source, ngy) * ngx + quotient(source, ngy)
        table[...] = jnp.where(ids >= 0, (block * ngy + owner) * CAP + rank, -1)

    def halos(r, c):
        def joined(i):
            return jnp.where(lane4 < 2, xrecv[r][0, c, i], xrecv[r][1, c, i])

        def swapped(halo):
            return jnp.where(lane4 == 1, pltpu.roll(halo, nx - 1, 1), pltpu.roll(halo, 1, 1))

        outer, own = (joined(0), xsend[r][c, 0])
        if r == 0:
            vh, bh = (joined(1), joined(2))
            bxh[c] = bh
            vyh[0, c] = yrecv[0][0, c, 2]
            vyh[1, c] = yrecv[0][1, c, 2]
        else:
            vh, bh = (vxh[c], bxh[c])
            corner = crecv[r - 1]
            xj[c, 7:8, :] = jnp.where(west_half, corner[c, 0], corner[c, 1])
            xj[c, 8 : 8 + ny, :] = outer
            xj[c, 8 + ny : 9 + ny, :] = jnp.where(west_half, corner[c, 2], corner[c, 3])
            if r == 1:
                vyx[c] = joined(1)
        slope = jnp.where(
            lane4 == 1,
            pltpu.roll(own, nx - 1, 1) - pltpu.roll(outer, 1, 1),
            pltpu.roll(outer, nx - 1, 1) - pltpu.roll(own, 1, 1),
        )
        vh = vh - bh * slope
        vxh[c] = vh
        hx[0, c] = swapped(outer)
        hx[1, c] = swapped(vh)
        vyh[0, c] = vyh[0, c] - yrecv[0][0, c, 3] * (ysend[r][0, c, 0] - yrecv[r][0, c, 0])
        vyh[1, c] = vyh[1, c] - yrecv[0][1, c, 3] * (yrecv[r][1, c, 1] - ysend[r][1, c, 1])

    def sweep(r, c):
        last, first = (r == STEPS - 1, r == 0)
        n = r + 1

        def body(i, totals):
            totals = list(totals)
            base = i * BATCH
            z0 = c * zc + base
            ps = [p[z0 + 1 + j] for j in range(BATCH + 2)]
            bs = [b[z0 + j] for j in range(BATCH + 1)]
            zs = [vz[z0], vz[z0 + 1]]
            vs, ws, new_p = ([], [], [])
            for j in range(BATCH):
                zl = base + j
                at = pl.ds(zl, 1)
                zs.append(vz[z0 + j + 2] - bs[j + 1] * (ps[j + 2] - ps[j]))
                vs.append(vx[z0 + j] - bs[j] * d_x(ps[j], hx[0, c], zl))
                south, north = (yrecv[r][0, c, 1, at, :], yrecv[r][1, c, 0, at, :])
                ws.append(vy[z0 + j] - bs[j] * d_y(ps[j], south, north))
            for j in range(BATCH):
                zl = base + j
                at = pl.ds(zl, 1)
                spread = d_x(vs[j], hx[1, c], zl) + d_y(ws[j], vyh[0, c, at, :], vyh[1, c, at, :])
                spread = spread + (zs[j + 2] - zs[j])
                mem = m[z0 + j]
                mem = mem - rel[z0 + j] * (mem + stg[z0 + j] * spread)
                m[z0 + j] = mem
                new_p.append(ps[j] - mod[z0 + j] * (spread + mem))
            for j in range(BATCH):
                zl = base + j
                at = pl.ds(zl, 1)
                vz[z0 + j + 2] = zs[j + 2]
                vx[z0 + j] = vs[j]
                vy[z0 + j] = ws[j]
                p[z0 + j + 1] = new_p[j]
                if not last:
                    totals[0] = pack(totals[0], new_p[j], zl)
                    ysend[n][0, c, 0, at, :] = new_p[j][0:1]
                    ysend[n][0, c, 1, at, :] = new_p[j][1:2]
                    ysend[n][1, c, 0, at, :] = new_p[j][ny - 2 : ny - 1]
                    ysend[n][1, c, 1, at, :] = new_p[j][ny - 1 : ny]
                if first:
                    totals[1] = pack(totals[1], ws[j], zl)
                    ysend[n][0, c, 2, at, :] = vs[j][0:1]
                    ysend[n][1, c, 2, at, :] = vs[j][ny - 1 : ny]
            return tuple(totals)

        count = 0 if last else X_PACKS[n]
        totals = lax.fori_loop(0, zc // BATCH, body, (plane,) * count)
        for i, total in enumerate(totals):
            xsend[n][c, i] = total
        if not last:
            csend[n - 1][c, 0] = totals[0][0:1]
            csend[n - 1][c, 1] = totals[0][ny - 1 : ny]

    patch_lane = lax.broadcasted_iota(jnp.int32, (per_dev, nx), 1)

    def masked(keep, values):
        return jnp.where(keep, values, 0.0)

    def gather(first_slot, rows):
        def body(i, carry):
            at = cell[i]
            z, y = (quotient(at, ny * nx), remainder(quotient(at, nx), ny))
            out = pl.ds(i, 1)
            for k, row in enumerate(rows):
                got[first_slot + k, out, :] = row(z, y)
            return carry

        lax.fori_loop(0, per_dev, body, 0, unroll=8)

    def row_up(ref, z, y):
        return ref[z, pl.ds(jnp.minimum(y + 1, ny - 1), 1), :]

    def row_down(ref, z, y):
        return ref[z, pl.ds(jnp.maximum(y - 1, 0), 1), :]

    def row_halo(ref, index, z, y):
        side = jnp.where(y == 0, 0, 1)
        which = 1 - side if index is None else index
        return ref[side, quotient(z, zc), which, pl.ds(remainder(z, zc), 1), :]

    def row_pack(ref, shift, z, y):
        return ref[quotient(z, zc), pl.ds(y + shift, 1), :]

    def own_rows(ref, lift):
        return [lambda z, y: row_up(ref, z + lift, y), lambda z, y: row_down(ref, z + lift, y)]

    def halo_rows(n):
        return [
            lambda z, y: row_halo(yrecv[n], None, z, y),
            lambda z, y: row_pack(xj, 9, z, y),
            lambda z, y: row_pack(xj, 7, z, y),
        ]

    B_OWN, P_OWN, V_OWN, P_HALO, V_HALO, B_HALO = (0, 3, 5, 8, 11, 13)

    def places():
        cells = to_column(cell_row[...].astype(jnp.float32)).astype(jnp.int32)
        cell_z, cell_x = (quotient(cells, ny * nx), remainder(cells, nx))
        return cell_x, remainder(quotient(cells, nx), ny), 4 * remainder(cell_z, zc)

    def along(values):
        return jnp.sum(values, axis=1, keepdims=True)

    def note(n, value):
        shear[...] = jnp.broadcast_to(value, shear.shape)
        spectra_out[...] = spectra_out[...] + value * phase[n - 1 : n, :]

    def first_shear():
        cell_x, cell_y, start = places()
        here = patch_lane == cell_x
        up, down = (cell_y < ny - 1, cell_y > 0)
        ahead, behind = (patch_lane == cell_x + 1, patch_lane == cell_x - 1)
        ahead_out = (patch_lane == start + 2) & (cell_x == nx - 1)
        behind_out = (patch_lane == start + 1) & (cell_x == 0)
        total = masked(here, jnp.where(up, got[V_OWN], got[V_HALO]))
        total = total - masked(here, jnp.where(down, got[V_OWN + 1], got[V_HALO]))
        total = total + masked(ahead, got[V_OWN + 2]) - masked(behind, got[V_OWN + 2])
        total = total + masked(ahead_out, got[V_HALO + 1]) - masked(behind_out, got[V_HALO + 1])
        note(1, along(total))
        b_up = along(masked(here, jnp.where(up, got[B_OWN], got[B_HALO])))
        b_down = along(masked(here, jnp.where(down, got[B_OWN + 1], got[B_HALO])))
        b_mid, b_out = (got[B_OWN + 2], got[B_HALO + 1])
        b_ahead = along(masked(ahead, b_mid) + masked(ahead_out, b_out))
        b_behind = along(masked(behind, b_mid) + masked(behind_out, b_out))
        at_up = masked(behind, b_up + b_behind) - masked(ahead, b_up + b_ahead)
        at_down = masked(ahead, b_down + b_ahead) - masked(behind, b_down + b_behind)
        factors[0] = masked(up, at_up)
        factors[1] = masked(down, at_down)
        factors[2] = jnp.where(up, masked(jnp.logical_not(down), at_down), at_up)
        factors[3] = masked(behind_out, b_up + b_behind) - masked(ahead_out, b_up + b_ahead)
        factors[4] = masked(ahead_out, b_down + b_ahead) - masked(behind_out, b_down + b_behind)

    def next_shear(n):
        rows = [P_OWN, P_OWN + 1, P_HALO, P_HALO + 1, P_HALO + 2]
        total = factors[0] * got[rows[0]]
        for k in range(1, 5):
            total = total + factors[k] * got[rows[k]]
        note(n, shear[:, 0:1] + along(total))

    for small in smalls:
        small.wait()
    fill_placing()
    gather(B_OWN, own_rows(b, 0) + [lambda z, y: b[z, pl.ds(y, 1), :]])
    for c in range(chunks):
        for i in range(4, 9):
            load(i, c).wait()

    def work_after(r):
        if r == 0:
            v_rows = own_rows(vx, 0) + [lambda z, y: vy[z, pl.ds(y, 1), :]]
            gather(P_OWN, own_rows(p, 1) + v_rows)
        elif r == 1:
            gather(
                P_HALO,
                halo_rows(1)
                + [
                    lambda z, y: row_halo(yrecv[1], 2, z, y),
                    lambda z, y: row_pack(vyx, 0, z, y),
                    lambda z, y: row_halo(yrecv[0], 3, z, y),
                    lambda z, y: row_pack(bxh, 0, z, y),
                ],
            )
            first_shear()
            next_shear(2)
            gather(P_OWN, own_rows(p, 1))
        elif r < STEPS - 1:
            gather(P_HALO, halo_rows(r))
            next_shear(r + 1)
            gather(P_OWN, own_rows(p, 1))

    def exchange_first():
        gather(P_HALO, halo_rows(STEPS - 1))
        next_shear(STEPS)
        rows_send[...] = jnp.dot(
            placing[...], spectra_out[...].astype(jnp.bfloat16), preferred_element_type=jnp.float32
        ).astype(jnp.bfloat16)
        for k in range(1, ngx):
            first_to(k).start()
        at = pl.ds(pl.multiple_of(gx * group_rows, group_rows), group_rows)
        rows_group[at, :] = rows_send[at, :]

    for r in range(STEPS):
        vz[1] = vz[1] - b[0] * (p[2] - p[0])
        for c in range(chunks):
            receive(r, c)
            halos(r, c)
            if r == STEPS - 1 and c == chunks - 1:
                exchange_first()
            sweep(r, c)
            if r < STEPS - 1:
                send(r + 1, c)
        work_after(r)
    for k in range(1, ngx):
        first_from(k).wait_recv()
    for k in range(1, ngy):
        second_to(k).start()
    at = pl.ds(pl.multiple_of(gy * all_rows, all_rows), all_rows)
    rows_out[at, :] = rows_group[...]
    fill_table()
    for side in range(8):

        @pl.when(has[side])
        def _():
            for r in range(STEPS):
                if side in sides(r):
                    for c in range(chunks):
                        ends(r, c, side, False).wait_send()

    own_weights.wait()
    for k in range(1, ngy):
        weights_from(k).wait_recv()
        weights_to(k).wait_send()
    for k in range(1, ngx):
        first_to(k).wait_send()
    for k in range(1, ngy):
        second_from(k).wait_recv()
        second_to(k).wait_send()


def finish_kernel(dims, *refs):
    nz, slot_count, share = dims
    refs = list(refs)
    take = lambda count: [refs.pop(0) for _ in range(count)]
    vx, vy, vz, p, m, spectra, weights, rows, table = take(9)
    vel_out, p_out, m_out, spectra_out, slip_out = take(5)
    columns, slots, wide, out_sem, slip_sem = take(5)
    rup_group, lanes = (weights.shape[1], weights.shape[3])
    inner = pl.ds(1, nz)
    pairs = [
        (vx, vel_out.at[0]),
        (vy, vel_out.at[1]),
        (vz.at[inner], vel_out.at[2]),
        (p.at[inner], p_out),
        (m, m_out),
        (spectra, spectra_out),
    ]
    stores = [
        pltpu.make_async_copy(src, dst, out_sem.at[i]) for i, (src, dst) in enumerate(pairs)
    ]
    for store in stores:
        store.start()

    size, depth = (min(rup_group * slot_count, 512), min(rows.shape[0], 512))
    lines = min(slot_count, 128)
    square = (lines, lines)
    eye = lax.broadcasted_iota(jnp.int32, square, 0) == lax.broadcasted_iota(jnp.int32, square, 1)
    row_at = lax.broadcasted_iota(jnp.int32, (size, depth), 1)
    start = pl.multiple_of(remainder(lax.axis_index("gy") * share, lanes), share)

    for r in range(rup_group):
        for k in range(slot_count // lines):
            line = table[r : r + 1, k * lines : (k + 1) * lines].astype(jnp.float32)
            column = jnp.sum(jnp.where(eye, line, 0.0), axis=1, keepdims=True).astype(jnp.int32)
            at = pl.ds(r * slot_count + k * lines, lines)
            columns[at, :] = jnp.broadcast_to(column, (lines, columns.shape[1]))

    def choose(i, carry):
        at = pl.ds(pl.multiple_of(i * size, size), size)
        column = columns[at, 0:1]

        def part(k, total):
            base = pl.multiple_of(k * depth, depth)
            chosen = jnp.where(row_at + base == column, 1.0, 0.0).astype(jnp.bfloat16)
            return total + jnp.dot(
                chosen, rows[pl.ds(base, depth), :], preferred_element_type=jnp.float32
            )

        total = jnp.zeros((size, rows.shape[1]), jnp.float32)
        if rows.shape[0] == depth:
            total = part(0, total)
        else:
            total = lax.fori_loop(0, rows.shape[0] // depth, part, total)
        slots[at, :] = total.astype(jnp.bfloat16)
        return carry

    if slots.shape[0] == size:
        choose(0, 0)
    else:
        lax.fori_loop(0, slots.shape[0] // size, choose, 0)
    for r in range(rup_group):
        own = weights[:, r].astype(jnp.float32).reshape(slot_count, lanes).astype(jnp.bfloat16)
        wide[r] = lax.dot_general(
            own,
            slots[pl.ds(r * slot_count, slot_count), :],
            (((0,), (0,)), ((), ())),
            preferred_element_type=jnp.float32,
        )
        pltpu.make_async_copy(
            wide.at[r, pl.ds(start, share)], slip_out.at[r], slip_sem.at[r]
        ).start()
    for store in stores:
        store.wait()
    for r in range(rup_group):
        pltpu.make_async_copy(
            wide.at[r, pl.ds(start, share)], slip_out.at[r], slip_sem.at[r]
        ).wait()


VMEM_LIMIT = 40 * 1024 * 1024


def in_hbm(x):
    return pltpu.with_memory_space_constraint(x, pltpu.HBM)


def advance(
    velocity, pressure, memory, buoyancy, modulus, relax, strength, spectra, patch_cell, listed, weights
):
    nz, ny, nx = pressure.shape
    per_dev, width = spectra.shape
    zc = nx // 4
    chunks = nz // zc
    ngx, ngy = (lax.axis_size("gx"), lax.axis_size("gy"))
    dims = (nz, ny, nx, chunks, zc, per_dev, ngx, ngy)
    rup_group, slot_dev, variations = weights.shape
    lanes = max(variations // ngy, 128)
    all_rows = ngx * ngy * CAP
    f32 = jnp.float32
    field = lambda planes: pltpu.VMEM((planes, ny, nx), f32)
    rounds = range(STEPS)
    any_spec = pl.BlockSpec(memory_space=pl.ANY)
    vmem_spec = pl.BlockSpec(memory_space=pltpu.VMEM)
    return pl.pallas_call(
        functools.partial(step_kernel, dims),
        out_shape=[
            field(nz),
            field(nz),
            field(nz + 2),
            field(nz + 3),
            field(nz),
            pltpu.VMEM(spectra.shape, f32),
            pltpu.VMEM((ngy, rup_group, slot_dev, lanes), jnp.bfloat16),
            pltpu.VMEM((ngy * all_rows, width), jnp.bfloat16),
            pltpu.VMEM((rup_group, max(listed.shape[1], 128)), jnp.int32),
        ],
        in_specs=[any_spec] * 13,
        out_specs=[vmem_spec] * 9,
        scratch_shapes=[field(nz + 1), field(nz), field(nz), field(nz)]
        + [pltpu.VMEM((2, chunks, Y_ROWS[r], zc, nx), f32) for r in rounds]
        + [pltpu.VMEM((2, chunks, Y_ROWS[r], zc, nx), f32) for r in rounds]
        + [pltpu.VMEM((chunks, X_PACKS[r], ny, nx), f32) for r in rounds]
        + [pltpu.VMEM((2, chunks, X_PACKS[r], ny, nx), f32) for r in rounds]
        + [pltpu.VMEM((chunks, 2, 1, nx), f32) for r in rounds[1:]]
        + [pltpu.VMEM((chunks, 4, 1, nx), f32) for r in rounds[1:]]
        + [
            pltpu.SMEM((per_dev,), jnp.int32),
            pltpu.VMEM((1, per_dev), jnp.int32),
            pltpu.VMEM((STEPS, width), f32),
            pltpu.VMEM(listed.shape, jnp.int32),
            pltpu.VMEM((chunks, ny, nx), f32),
            pltpu.VMEM((chunks, ny, nx), f32),
            pltpu.VMEM((2, chunks, ny, nx), f32),
            pltpu.VMEM((2, chunks, zc, nx), f32),
            pltpu.VMEM((chunks, ny, nx), f32),
            pltpu.VMEM((chunks, ny + 16, nx), f32),
            pltpu.VMEM((15, per_dev, nx), f32),
            pltpu.VMEM((per_dev, nx), f32),
            pltpu.VMEM((5, per_dev, nx), f32),
            pltpu.VMEM((all_rows, per_dev), jnp.bfloat16),
            pltpu.VMEM((all_rows, width), jnp.bfloat16),
            pltpu.VMEM((all_rows, width), jnp.bfloat16),
            pltpu.SemaphoreType.DMA((9, chunks)),
            pltpu.SemaphoreType.DMA((5,)),
            pltpu.SemaphoreType.DMA((STEPS, chunks, 8)),
            pltpu.SemaphoreType.DMA((STEPS, chunks, 8)),
            pltpu.SemaphoreType.DMA((3, max(ngx, ngy))),
            pltpu.SemaphoreType.DMA((3, max(ngx, ngy))),
        ],
        compiler_params=pltpu.CompilerParams(
            collective_id=0, has_side_effects=True, vmem_limit_bytes=VMEM_LIMIT
        ),
    )(
        *[in_hbm(x) for x in (velocity, pressure, memory, buoyancy, modulus, relax, strength)],
        in_hbm(spectra),
        in_hbm(patch_cell),
        in_hbm(patch_cell.reshape(1, -1)),
        in_hbm(phase_rows(width // 2)),
        in_hbm(listed),
        in_hbm(weights),
    )


def finish(state, velocity, pressure, memory, spectra, weights):
    nz = pressure.shape[0]
    width = spectra.shape[1]
    ngy = lax.axis_size("gy")
    rup_group, slot_dev, variations = weights.shape
    slot_count = slot_dev * ngy
    share = variations // ngy
    lanes = max(share, 128)
    f32 = jnp.float32
    any_spec = pl.BlockSpec(memory_space=pl.ANY)
    vmem_spec = pl.BlockSpec(memory_space=pltpu.VMEM)
    return pl.pallas_call(
        functools.partial(finish_kernel, (nz, slot_count, share)),
        out_shape=[
            jax.ShapeDtypeStruct(velocity.shape, f32),
            jax.ShapeDtypeStruct(pressure.shape, f32),
            jax.ShapeDtypeStruct(memory.shape, f32),
            jax.ShapeDtypeStruct(spectra.shape, f32),
            jax.ShapeDtypeStruct((rup_group, share, width), f32),
        ],
        in_specs=[vmem_spec] * len(state),
        out_specs=[any_spec] * 5,
        scratch_shapes=[
            pltpu.VMEM((rup_group * slot_count, 128), jnp.int32),
            pltpu.VMEM((rup_group * slot_count, width), jnp.bfloat16),
            pltpu.VMEM((rup_group, lanes, width), f32),
            pltpu.SemaphoreType.DMA((6,)),
            pltpu.SemaphoreType.DMA((rup_group,)),
        ],
        compiler_params=pltpu.CompilerParams(vmem_limit_bytes=VMEM_LIMIT),
    )(*[pltpu.with_memory_space_constraint(x, pltpu.VMEM) for x in state])


def per_device(
    velocity,
    pressure,
    memory,
    buoyancy,
    modulus,
    relax,
    strength,
    spectra,
    patch_cell,
    rupture_patches,
    slip_weights,
):
    state = advance(
        velocity,
        pressure,
        memory,
        buoyancy,
        modulus,
        relax,
        strength,
        spectra,
        patch_cell,
        rupture_patches,
        slip_weights,
    )
    return tuple(finish(state, velocity, pressure, memory, spectra, slip_weights))


def solution(mesh):
    in_specs = (
        P(None, None, "gy", "gx"),
        P(None, "gy", "gx"),
        P(None, "gy", "gx"),
        P(None, "gy", "gx"),
        P(None, "gy", "gx"),
        P(None, "gy", "gx"),
        P(None, "gy", "gx"),
        P(("gx", "gy"), None),
        P(("gx", "gy")),
        P(),
        P("gx", "gy", None),
    )
    out_specs = (
        P(None, None, "gy", "gx"),
        P(None, "gy", "gx"),
        P(None, "gy", "gx"),
        P(("gx", "gy"), None),
        P("gx", "gy", None),
    )
    return jax.shard_map(
        per_device, mesh=mesh, in_specs=in_specs, out_specs=out_specs, check_vma=False
    )
```

time: 46 us -> 40.3 us (0.88)
  Pallas kernels: 45.2 us -> 39.5 us
    pallas_call x1, Pallas kernels: 39.9 us -> 36.2 us  [advance(): pl.pallas_call(functools.partial(step_kernel, dims), out_shape=[field(nz)...]
    pallas_call x1, Pallas kernels: 5.3 us -> 3.27 us  [finish(): pl.pallas_call(functools.partial(finish_kernel, (nz, slot_count, share)),...]
where the time goes in v1:
time: 40.3 us; the launch traced here: 40.1 us
  Pallas kernels  39.5 us (98%)
  between operations  0.64 us (2%)
    pallas_call x1, Pallas kernels, advance(): pl.pallas_call(functools.partial(step_kernel, dims), out_shape=[field(nz)...  36.2 us
    pallas_call x1, Pallas kernels, finish(): pl.pallas_call(functools.partial(finish_kernel, (nz, slot_count, share)),...  3.27 us

profile of v1, /device:TPU:0, one launch (start us, length us, event | category | flops | bytes accessed | tf_op | source)
XLA Modules:
  0.0 40.1 jit_solution(1466582344819694180)
XLA Ops:
  0.6 36.2 %shard_map.155 = (f32[64,32,128]{2,1,0:T(8,128)S(1)}, f32[64,32,128]{2,1,0:T(8,128)S(1)}, f32[66,32,128]{2,1,0:T(8,128)S(1)}, f32[67,32,128]{2,1,0:T(8,128)S(1)}...) custom-call(f32[3,64,32,128]{3,2,1,0:T(8,128)} %refs_0_.1, ...), custom_call_target="tpu_custom_call" | custom-call | tf_op jit(solution)/shard_map/pallas_call | solution.py:683
  36.9 3.3 %shard_map.156 = (f32[3,64,32,128]{3,2,1,0:T(8,128)}, f32[64,32,128]{2,1,0:T(8,128)}, f32[64,32,128]{2,1,0:T(8,128)}, f32[64,256]{1,0:T(8,128)}, f32[8,64,256]{2,1,0:T(8,128)}) custom-call(f32[64,32,128]{2,1,0:T(8,128)S(1)} %get-tuple-element.14.refs_0_, f32[64,32,128]{2,1,0:T(8,128)S(1)} %get-tuple-element.15.refs_1_, ...), custom_call_target="tpu_custom_call" | custom-call | tf_op jit(solution)/shard_map/pallas_call | solution.py:754

commit v2 on v1

--- a/solution.py
+++ b/solution.py
@@ -16,6 +16,7 @@
 def phase_rows(freqs):
     angle = np.pi * (np.arange(freqs) + 0.5) / freqs
     rows = [np.concatenate([np.cos(angle * n), -np.sin(angle * n)]) for n in range(1, STEPS + 1)]
+    rows = rows + [np.zeros(2 * freqs)] * (8 - STEPS)
     return jnp.asarray(np.stack(rows).astype(np.float32))
 
 
@@ -41,15 +42,16 @@
     take = lambda count: [refs.pop(0) for _ in range(count)]
     vel_in, p_in, m_in, b_in, mod_in, rel_in, str_in = take(7)
     spectra_in, cell_in, cell_row_in, phase_in, listed_in, weights = take(6)
-    vx, vy, vz, p, m, spectra_out, weights_got, rows_out, table = take(9)
+    vx, vy, vz, p, m, spectra_out, weights_got, rows_out, table, heard, phase = take(11)
     b, mod, rel, stg = take(4)
     ysend, yrecv = (take(STEPS), take(STEPS))
     xsend, xrecv = (take(STEPS), take(STEPS))
     csend, crecv = (take(STEPS - 1), take(STEPS - 1))
-    cell, cell_row, phase, listed = take(4)
+    cell, cell_row, listed = take(3)
     vxh, bxh, hx, vyh, vyx, xj, got, shear, factors = take(9)
-    placing, rows_send, rows_group = take(3)
+    placing, placed, rows_send, rows_group, told = take(5)
     in_sem, small_sem, send_sem, recv_sem, far_send, far_recv = take(6)
+    pass_send, pass_recv, tell_sem, hear_sem = take(4)
 
     gx, gy = (lax.axis_index("gx"), lax.axis_index("gy"))
     has = [gy > 0, gy < ngy - 1, gx > 0, gx < ngx - 1]
@@ -94,19 +96,31 @@
     for small in smalls:
         small.start()
 
-    along_gx = [lax.rem(gx + k, ngx) for k in range(1, ngx)]
-    along_gy = [lax.rem(gy + k, ngy) for k in range(1, ngy)]
-    peers = [{"gx": other} for other in along_gx] + [{"gy": other} for other in along_gy]
-    peers = peers + [
-        {"gy": lax.rem(gy + ngy + dy, ngy), "gx": lax.rem(gx + ngx + dx, ngx)}
-        for dy in (-1, 1)
-        for dx in (-1, 1)
-    ]
+    devices = ngx * ngy
+    me = gx * ngy + gy
+    mine = gy * ngx + gx
+
+    def other_device(k):
+        other = lax.rem(me + k, devices)
+        return {"gx": lax.div(other, ngy), "gy": lax.rem(other, ngy)}
+
+    def flip(j):
+        index = gy
+        for bit in range(j.bit_length()):
+            if (j >> bit) & 1:
+                step = 2**bit
+                index = index + step * (1 - 2 * lax.rem(lax.div(index, step), 2))
+        return index
+
     barrier = pltpu.get_barrier_semaphore()
-    for other in peers:
+
+    def greet(k, carry):
         pl.semaphore_signal(
-            barrier, inc=1, device_id=other, device_id_type=pl.DeviceIdType.MESH
-        )
+            barrier, inc=1, device_id=other_device(k), device_id_type=pl.DeviceIdType.MESH
+        )
+        return carry
+
+    lax.fori_loop(1, devices, greet, 0)
 
     plane = jnp.zeros((ny, nx), jnp.float32)
     p[0] = plane
@@ -215,7 +229,7 @@
         for i, total in enumerate(totals):
             xsend[0][c, i] = total
         if c == 0:
-            pl.semaphore_wait(barrier, len(peers))
+            pl.semaphore_wait(barrier, devices - 1)
         send(0, c)
 
     rup_group, slot_dev, variations = weights.shape
@@ -255,16 +269,48 @@
         src = rows_of(rows_send, gx, group_rows)
         return far(1, k, src, rows_of(rows_group, lax.rem(gx + ngx - k, ngx), group_rows))
 
-    def second_to(k):
-        return far(2, k, rows_group, rows_of(rows_out, gy, all_rows))
-
-    def second_from(k):
-        return far(2, k, rows_group, rows_of(rows_out, lax.rem(gy + ngy - k, ngy), all_rows))
-
-    for k in range(1, ngy):
-        weights_to(k).start()
+    half = all_rows // 2
+
+    def block_rows(owner, h):
+        at = pl.multiple_of(owner * all_rows + h * half, half)
+        return rows_out.at[pl.ds(at, half)]
+
+    def carry_over(j, h, src, dst, partner):
+        return pltpu.make_async_remote_copy(
+            src_ref=src,
+            dst_ref=dst,
+            send_sem=pass_send.at[j, h],
+            recv_sem=pass_recv.at[j, h],
+            device_id={"gy": partner},
+            device_id_type=pl.DeviceIdType.MESH,
+        )
+
+    def direct_to(j, h):
+        return carry_over(
+            j, h, rows_group.at[pl.ds(h * half, half)], block_rows(gy, h), flip(j)
+        )
+
+    def pass_on(j, h):
+        block = block_rows(flip(j), h)
+        return carry_over(j + 1, h, block, block, flip(1))
+
+    def block_from(j, h):
+        block = block_rows(flip(j), h)
+        return carry_over(j, h, block, block, flip(1 if j % 2 else j))
+
+    def tell(k):
+        where = other_device(k)
+        return pltpu.make_async_remote_copy(
+            src_ref=told.at[where["gx"]],
+            dst_ref=heard.at[mine],
+            send_sem=tell_sem.at[0],
+            recv_sem=hear_sem.at[0],
+            device_id=where,
+            device_id_type=pl.DeviceIdType.MESH,
+        )
+
     own_weights = pltpu.make_async_copy(weight_block(gy), weights_got.at[gy], far_send.at[0, 0])
-    own_weights.start()
+    own_told = pltpu.make_async_copy(told.at[gx], heard.at[mine], hear_sem.at[0])
 
     square = (per_dev, per_dev)
     eye = lax.broadcasted_iota(jnp.int32, square, 0) == lax.broadcasted_iota(jnp.int32, square, 1)
@@ -292,9 +338,11 @@
         )
         same = (to_row(target) == target) & before
         rank = jnp.sum(jnp.where(same, 1.0, 0.0), axis=1, keepdims=True)
-        bucket = to_row(jnp.where(target >= 0.0, target * CAP + rank, -1.0))
+        bucket = jnp.where(target >= 0.0, target * CAP + rank, -1.0)
+        spot = lax.broadcasted_iota(jnp.int32, placed.shape, 1).astype(jnp.float32)
+        placed[...] = jnp.where(spot == bucket, 1.0, 0.0)
         place = lax.broadcasted_iota(jnp.int32, placing.shape, 0).astype(jnp.float32)
-        placing[...] = jnp.where(place == bucket, 1.0, 0.0).astype(jnp.bfloat16)
+        placing[...] = jnp.where(place == to_row(bucket), 1.0, 0.0)
 
     def fill_table():
         slot_count = listed.shape[1]
@@ -411,6 +459,8 @@
             csend[n - 1][c, 0] = totals[0][0:1]
             csend[n - 1][c, 1] = totals[0][ny - 1 : ny]
 
+    told_lane = lax.broadcasted_iota(jnp.int32, (1, 128), 1)
+    in_place = quotient(told_lane, group_rows) == remainder(mine, 128 // group_rows)
     patch_lane = lax.broadcasted_iota(jnp.int32, (per_dev, nx), 1)
 
     def masked(keep, values):
@@ -463,6 +513,13 @@
 
     def note(n, value):
         shear[...] = jnp.broadcast_to(value, shear.shape)
+        line = jnp.sum(placed[...] * value, axis=0, keepdims=True)
+        for k in range(ngx):
+            begin = k * group_rows
+            tile = begin - begin % 128
+            piece = line[:, tile : tile + 128]
+            spread = pltpu.roll(piece, remainder(mine * group_rows + (128 - begin % 128), 128), 1)
+            told[k, n - 1 : n, :] = jnp.where(in_place, spread, 0.0)
         spectra_out[...] = spectra_out[...] + value * phase[n - 1 : n, :]
 
     def first_shear():
@@ -499,7 +556,18 @@
 
     for small in smalls:
         small.wait()
+    told[...] = jnp.zeros(told.shape, jnp.float32)
     fill_placing()
+    rows_send[...] = jnp.dot(
+        placing[...],
+        spectra_out[...],
+        preferred_element_type=jnp.float32,
+        precision=lax.Precision.HIGHEST,
+    )
+    for k in range(1, ngx):
+        first_to(k).start()
+    at = pl.ds(pl.multiple_of(gx * group_rows, group_rows), group_rows)
+    rows_group[at, :] = rows_send[at, :]
     gather(B_OWN, own_rows(b, 0) + [lambda z, y: b[z, pl.ds(y, 1), :]])
     for c in range(chunks):
         for i in range(4, 9):
@@ -528,16 +596,47 @@
             next_shear(r + 1)
             gather(P_OWN, own_rows(p, 1))
 
-    def exchange_first():
+    def last_shear():
         gather(P_HALO, halo_rows(STEPS - 1))
         next_shear(STEPS)
-        rows_send[...] = jnp.dot(
-            placing[...], spectra_out[...].astype(jnp.bfloat16), preferred_element_type=jnp.float32
-        ).astype(jnp.bfloat16)
+        own_told.start()
+
+        def start(k, carry):
+            tell(k).start()
+            return carry
+
+        lax.fori_loop(1, devices, start, 0)
+
+    gaps = [(r, c) for r in range(STEPS - 1) for c in range(chunks)][1:]
+    jobs = {gap: [] for gap in gaps + [(STEPS - 1, 0), None]}
+    order = list(jobs)
+    pieces = [(j, h) for j in range(2, ngy, 2) for h in range(2)]
+
+    def enter_rows():
         for k in range(1, ngx):
-            first_to(k).start()
-        at = pl.ds(pl.multiple_of(gx * group_rows, group_rows), group_rows)
-        rows_group[at, :] = rows_send[at, :]
+            first_from(k).wait_recv()
+        at = pl.ds(pl.multiple_of(gy * all_rows, all_rows), all_rows)
+        rows_out[at, :] = rows_group[...]
+        for h in range(2):
+            direct_to(1, h).start()
+        own_weights.start()
+
+    def leave(j, h):
+        direct_to(j, h).start()
+
+    def forward(j, h):
+        block_from(j, h).wait_recv()
+        pass_on(j, h).start()
+
+    jobs[order[0]].append(enter_rows)
+    for i, (j, h) in enumerate(pieces):
+        place = i * len(gaps) // len(pieces)
+        jobs[order[place]].append(functools.partial(leave, j, h))
+        after = order[min(place + 2, len(order) - 1)]
+        jobs[after].append(functools.partial(forward, j, h))
+    for k in range(1, ngy):
+        place = (k - 1) * len(gaps) // (ngy - 1)
+        jobs[order[place]].append(lambda k=k: weights_to(k).start())
 
     for r in range(STEPS):
         vz[1] = vz[1] - b[0] * (p[2] - p[0])
@@ -545,17 +644,15 @@
             receive(r, c)
             halos(r, c)
             if r == STEPS - 1 and c == chunks - 1:
-                exchange_first()
+                last_shear()
             sweep(r, c)
             if r < STEPS - 1:
                 send(r + 1, c)
+            for job in jobs.get((r, c), []):
+                job()
         work_after(r)
-    for k in range(1, ngx):
-        first_from(k).wait_recv()
-    for k in range(1, ngy):
-        second_to(k).start()
-    at = pl.ds(pl.multiple_of(gy * all_rows, all_rows), all_rows)
-    rows_out[at, :] = rows_group[...]
+    for job in jobs[None]:
+        job()
     fill_table()
     for side in range(8):
 
@@ -572,18 +669,26 @@
         weights_to(k).wait_send()
     for k in range(1, ngx):
         first_to(k).wait_send()
-    for k in range(1, ngy):
-        second_from(k).wait_recv()
-        second_to(k).wait_send()
+    for h in range(2):
+        for j in [1] + list(range(2, ngy, 2)):
+            direct_to(j, h).wait_send()
+        for j in range(2, ngy, 2):
+            pass_on(j, h).wait_send()
+        for j in range(1, ngy, 2):
+            block_from(j, h).wait_recv()
+    pltpu.make_async_copy(
+        heard.at[pl.ds(1, devices - 1)], heard.at[pl.ds(1, devices - 1)], tell_sem.at[0]
+    ).wait()
+    pltpu.make_async_copy(heard, heard, hear_sem.at[0]).wait()
 
 
 def finish_kernel(dims, *refs):
     nz, slot_count, share = dims
     refs = list(refs)
     take = lambda count: [refs.pop(0) for _ in range(count)]
-    vx, vy, vz, p, m, spectra, weights, rows, table = take(9)
+    vx, vy, vz, p, m, spectra, weights, rows, table, heard, phase = take(11)
     vel_out, p_out, m_out, spectra_out, slip_out = take(5)
-    columns, slots, wide, out_sem, slip_sem = take(5)
+    columns, slots, wide, exact, out_sem, slip_sem = take(6)
     rup_group, lanes = (weights.shape[1], weights.shape[3])
     inner = pl.ds(1, nz)
     pairs = [
@@ -614,6 +719,23 @@
             at = pl.ds(r * slot_count + k * lines, lines)
             columns[at, :] = jnp.broadcast_to(column, (lines, columns.shape[1]))
 
+    count = heard.shape[0]
+    per_tile = count * 128 // rows.shape[0]
+    tiles = [
+        functools.reduce(jnp.add, [heard[t * per_tile + k] for k in range(per_tile)])
+        for t in range(count // per_tile)
+    ]
+    for t, tile in enumerate(tiles):
+        at = pl.ds(t * 128, 128)
+        change = lax.dot_general(
+            tile,
+            phase[...],
+            (((0,), (0,)), ((), ())),
+            preferred_element_type=jnp.float32,
+            precision=lax.Precision.HIGHEST,
+        )
+        exact[at, :] = (rows[at, :] + change).astype(jnp.bfloat16)
+
     def choose(i, carry):
         at = pl.ds(pl.multiple_of(i * size, size), size)
         column = columns[at, 0:1]
@@ -622,7 +744,7 @@
             base = pl.multiple_of(k * depth, depth)
             chosen = jnp.where(row_at + base == column, 1.0, 0.0).astype(jnp.bfloat16)
             return total + jnp.dot(
-                chosen, rows[pl.ds(base, depth), :], preferred_element_type=jnp.float32
+                chosen, exact[pl.ds(base, depth), :], preferred_element_type=jnp.float32
             )
 
         total = jnp.zeros((size, rows.shape[1]), jnp.float32)
@@ -690,11 +812,13 @@
             field(nz),
             pltpu.VMEM(spectra.shape, f32),
             pltpu.VMEM((ngy, rup_group, slot_dev, lanes), jnp.bfloat16),
-            pltpu.VMEM((ngy * all_rows, width), jnp.bfloat16),
+            pltpu.VMEM((ngy * all_rows, width), f32),
             pltpu.VMEM((rup_group, max(listed.shape[1], 128)), jnp.int32),
+            pltpu.VMEM((ngx * ngy, 8, 128), f32),
+            pltpu.VMEM((8, width), f32),
         ],
         in_specs=[any_spec] * 13,
-        out_specs=[vmem_spec] * 9,
+        out_specs=[vmem_spec] * 11,
         scratch_shapes=[field(nz + 1), field(nz), field(nz), field(nz)]
         + [pltpu.VMEM((2, chunks, Y_ROWS[r], zc, nx), f32) for r in rounds]
         + [pltpu.VMEM((2, chunks, Y_ROWS[r], zc, nx), f32) for r in rounds]
@@ -705,7 +829,6 @@
         + [
             pltpu.SMEM((per_dev,), jnp.int32),
             pltpu.VMEM((1, per_dev), jnp.int32),
-            pltpu.VMEM((STEPS, width), f32),
             pltpu.VMEM(listed.shape, jnp.int32),
             pltpu.VMEM((chunks, ny, nx), f32),
             pltpu.VMEM((chunks, ny, nx), f32),
@@ -716,15 +839,21 @@
             pltpu.VMEM((15, per_dev, nx), f32),
             pltpu.VMEM((per_dev, nx), f32),
             pltpu.VMEM((5, per_dev, nx), f32),
-            pltpu.VMEM((all_rows, per_dev), jnp.bfloat16),
-            pltpu.VMEM((all_rows, width), jnp.bfloat16),
-            pltpu.VMEM((all_rows, width), jnp.bfloat16),
+            pltpu.VMEM((all_rows, per_dev), f32),
+            pltpu.VMEM((per_dev, max(all_rows, 128)), f32),
+            pltpu.VMEM((all_rows, width), f32),
+            pltpu.VMEM((all_rows, width), f32),
+            pltpu.VMEM((ngx, 8, 128), f32),
             pltpu.SemaphoreType.DMA((9, chunks)),
             pltpu.SemaphoreType.DMA((5,)),
             pltpu.SemaphoreType.DMA((STEPS, chunks, 8)),
             pltpu.SemaphoreType.DMA((STEPS, chunks, 8)),
-            pltpu.SemaphoreType.DMA((3, max(ngx, ngy))),
-            pltpu.SemaphoreType.DMA((3, max(ngx, ngy))),
+            pltpu.SemaphoreType.DMA((2, max(ngx, ngy))),
+            pltpu.SemaphoreType.DMA((2, max(ngx, ngy))),
+            pltpu.SemaphoreType.DMA((ngy, 2)),
+            pltpu.SemaphoreType.DMA((ngy, 2)),
+            pltpu.SemaphoreType.DMA((1,)),
+            pltpu.SemaphoreType.DMA((1,)),
         ],
         compiler_params=pltpu.CompilerParams(
             collective_id=0, has_side_effects=True, vmem_limit_bytes=VMEM_LIMIT
@@ -766,6 +895,7 @@
             pltpu.VMEM((rup_group * slot_count, 128), jnp.int32),
             pltpu.VMEM((rup_group * slot_count, width), jnp.bfloat16),
             pltpu.VMEM((rup_group, lanes, width), f32),
+            pltpu.VMEM(state[7].shape, jnp.bfloat16),
             pltpu.SemaphoreType.DMA((6,)),
             pltpu.SemaphoreType.DMA((rup_group,)),
         ],

time: 40.3 us -> 37.6 us (0.933)
  Pallas kernels: 39.5 us -> 36.8 us
    pallas_call x1, Pallas kernels: 36.2 us -> 33.5 us  [advance(): pl.pallas_call(functools.partial(step_kernel, dims), out_shape=[field(nz)...]
where the time goes in v2:
time: 37.6 us; the launch traced here: 37.5 us
  Pallas kernels  36.8 us (98%)
  between operations  0.64 us (2%)
    pallas_call x1, Pallas kernels, advance(): pl.pallas_call(functools.partial(step_kernel, dims), out_shape=[field(nz)...  33.5 us
    pallas_call x1, Pallas kernels, finish(): pl.pallas_call(functools.partial(finish_kernel, (nz, slot_count, share)),...  3.32 us

profile of v2, /device:TPU:0, one launch (start us, length us, event | category | flops | bytes accessed | tf_op | source)
XLA Modules:
  0.0 37.5 jit_solution(8020523769450103406)
XLA Ops:
  0.6 33.5 %shard_map.155 = (f32[64,32,128]{2,1,0:T(8,128)S(1)}, f32[64,32,128]{2,1,0:T(8,128)S(1)}, f32[66,32,128]{2,1,0:T(8,128)S(1)}, f32[67,32,128]{2,1,0:T(8,128)S(1)}...) custom-call(f32[3,64,32,128]{3,2,1,0:T(8,128)} %refs_0_.1, ...), custom_call_target="tpu_custom_call" | custom-call | tf_op jit(solution)/shard_map/pallas_call | solution.py:805
  34.2 3.3 %shard_map.156 = (f32[3,64,32,128]{3,2,1,0:T(8,128)}, f32[64,32,128]{2,1,0:T(8,128)}, f32[64,32,128]{2,1,0:T(8,128)}, f32[64,256]{1,0:T(8,128)}, f32[8,64,256]{2,1,0:T(8,128)}) custom-call(f32[64,32,128]{2,1,0:T(8,128)S(1)} %get-tuple-element.16.refs_0_, f32[64,32,128]{2,1,0:T(8,128)S(1)} %get-tuple-element.17.refs_1_, ...), custom_call_target="tpu_custom_call" | custom-call | tf_op jit(solution)/shard_map/pallas_call | solution.py:883

commit v3 on v2

--- a/solution.py
+++ b/solution.py
@@ -42,16 +42,14 @@
     take = lambda count: [refs.pop(0) for _ in range(count)]
     vel_in, p_in, m_in, b_in, mod_in, rel_in, str_in = take(7)
     spectra_in, cell_in, cell_row_in, phase_in, listed_in, weights = take(6)
-    vx, vy, vz, p, m, spectra_out, weights_got, rows_out, table, heard, phase = take(11)
+    vx, vy, vz, p, m, spectra_out, weights_got, rows_out, table, heard, heard_last, phase = take(12)
     b, mod, rel, stg = take(4)
-    ysend, yrecv = (take(STEPS), take(STEPS))
-    xsend, xrecv = (take(STEPS), take(STEPS))
-    csend, crecv = (take(STEPS - 1), take(STEPS - 1))
+    ysend, xsend, csend = take(3)
+    yrecv, xrecv, crecv = (take(STEPS), take(STEPS), take(STEPS - 1))
     cell, cell_row, listed = take(3)
     vxh, bxh, hx, vyh, vyx, xj, got, shear, factors = take(9)
-    placing, placed, rows_send, rows_group, told = take(5)
-    in_sem, small_sem, send_sem, recv_sem, far_send, far_recv = take(6)
-    pass_send, pass_recv, tell_sem, hear_sem = take(4)
+    placing, placed, rows_send, rows_group, told, told_last = take(6)
+    in_sem, small_sem, send_sem, recv_sem, far_sem, block_sem, tell_sem, hear_sem = take(8)
 
     gx, gy = (lax.axis_index("gx"), lax.axis_index("gy"))
     has = [gy > 0, gy < ngy - 1, gx > 0, gx < ngx - 1]
@@ -75,6 +73,9 @@
         ][i]
         return pltpu.make_async_copy(src, dst, in_sem.at[i, c])
 
+    y_row = lambda r, k: sum(Y_ROWS[:r]) + k
+    x_row = lambda r, k: sum(X_PACKS[:r]) + k
+
     smalls = [
         pltpu.make_async_copy(src, dst, small_sem.at[i])
         for i, (src, dst) in enumerate(
@@ -87,15 +88,14 @@
             ]
         )
     ]
+    for small in smalls:
+        small.start()
     for c in range(chunks):
         for i in range(4):
             load(i, c).start()
     for c in range(chunks):
         for i in range(4, 9):
             load(i, c).start()
-    for small in smalls:
-        small.start()
-
     devices = ngx * ngy
     me = gx * ngy + gy
     mine = gy * ngx + gx
@@ -146,21 +146,24 @@
         k = side % 4
         if side < 2:
             there = side if coming else 1 - side
-            src, dst = (ysend[r].at[side, c], yrecv[r].at[there, c])
+            src = ysend.at[side, c, pl.ds(y_row(r, 0), Y_ROWS[r])]
+            dst = yrecv[r].at[there, c]
             arrives = there
         elif side < 4:
             there = k - 2 if coming else 3 - k
-            src, dst = (xsend[r].at[c], xrecv[r].at[there, c])
+            src = xsend.at[c, pl.ds(x_row(r, 0), X_PACKS[r])]
+            dst = xrecv[r].at[there, c]
             arrives = 2 + there
         else:
             there = k if coming else 3 - k
-            src, dst = (csend[r - 1].at[c, k // 2], crecv[r - 1].at[c, there])
+            src = csend.at[k // 2, (r - 1) * chunks + c]
+            dst = crecv[r - 1].at[c, there]
             arrives = 4 + there
         return pltpu.make_async_remote_copy(
             src_ref=src,
             dst_ref=dst,
-            send_sem=send_sem.at[r, c, side],
-            recv_sem=recv_sem.at[r, c, arrives],
+            send_sem=send_sem.at[side],
+            recv_sem=recv_sem.at[r % 2, c, arrives],
             device_id=peer[side],
             device_id_type=pl.DeviceIdType.MESH,
         )
@@ -215,19 +218,19 @@
                 ps, vs, ws, bs = (p[z + 1], vx[z], vy[z], b[z])
                 pt, vt, bt = (pack(pt, ps, zl), pack(vt, vs, zl), pack(bt, bs, zl))
                 at = pl.ds(zl, 1)
-                ysend[0][0, c, 0, at, :] = ps[0:1]
-                ysend[0][0, c, 1, at, :] = ps[1:2]
-                ysend[0][0, c, 2, at, :] = ws[0:1]
-                ysend[0][0, c, 3, at, :] = bs[0:1]
-                ysend[0][1, c, 0, at, :] = ps[ny - 2 : ny - 1]
-                ysend[0][1, c, 1, at, :] = ps[ny - 1 : ny]
-                ysend[0][1, c, 2, at, :] = ws[ny - 1 : ny]
-                ysend[0][1, c, 3, at, :] = bs[ny - 1 : ny]
+                ysend[0, c, y_row(0, 0), at, :] = ps[0:1]
+                ysend[0, c, y_row(0, 1), at, :] = ps[1:2]
+                ysend[0, c, y_row(0, 2), at, :] = ws[0:1]
+                ysend[0, c, y_row(0, 3), at, :] = bs[0:1]
+                ysend[1, c, y_row(0, 0), at, :] = ps[ny - 2 : ny - 1]
+                ysend[1, c, y_row(0, 1), at, :] = ps[ny - 1 : ny]
+                ysend[1, c, y_row(0, 2), at, :] = ws[ny - 1 : ny]
+                ysend[1, c, y_row(0, 3), at, :] = bs[ny - 1 : ny]
             return pt, vt, bt
 
         totals = lax.fori_loop(0, zc // BATCH, edges, (plane, plane, plane))
         for i, total in enumerate(totals):
-            xsend[0][c, i] = total
+            xsend[c, x_row(0, i)] = total
         if c == 0:
             pl.semaphore_wait(barrier, devices - 1)
         send(0, c)
@@ -246,28 +249,24 @@
         return pltpu.make_async_remote_copy(
             src_ref=src,
             dst_ref=dst,
-            send_sem=far_send.at[kind, k],
-            recv_sem=far_recv.at[kind, k],
+            send_sem=far_sem.at[kind, 0],
+            recv_sem=far_sem.at[kind, 1],
             device_id={axis: lax.rem(lax.axis_index(axis) + k, size)},
             device_id_type=pl.DeviceIdType.MESH,
         )
 
+    def settle(ref, sem):
+        pltpu.make_async_copy(ref, ref, sem).wait()
+
     def rows_of(ref, index, count):
         return ref.at[pl.ds(pl.multiple_of(index * count, count), count)]
 
     def weights_to(k):
         return far(0, k, weight_block(lax.rem(gy + k, ngy)), weights_got.at[gy])
-
-    def weights_from(k):
-        return far(0, k, weight_block(gy), weights_got.at[lax.rem(gy + ngy - k, ngy)])
 
     def first_to(k):
         src = rows_of(rows_send, lax.rem(gx + k, ngx), group_rows)
         return far(1, k, src, rows_of(rows_group, gx, group_rows))
-
-    def first_from(k):
-        src = rows_of(rows_send, gx, group_rows)
-        return far(1, k, src, rows_of(rows_group, lax.rem(gx + ngx - k, ngx), group_rows))
 
     half = all_rows // 2
 
@@ -279,8 +278,8 @@
         return pltpu.make_async_remote_copy(
             src_ref=src,
             dst_ref=dst,
-            send_sem=pass_send.at[j, h],
-            recv_sem=pass_recv.at[j, h],
+            send_sem=block_sem.at[0, 1],
+            recv_sem=block_sem.at[0, 0] if j % 2 else block_sem.at[j // 2, h],
             device_id={"gy": partner},
             device_id_type=pl.DeviceIdType.MESH,
         )
@@ -298,19 +297,27 @@
         block = block_rows(flip(j), h)
         return carry_over(j, h, block, block, flip(1 if j % 2 else j))
 
-    def tell(k):
+    def tell(k, src, dst, i):
         where = other_device(k)
         return pltpu.make_async_remote_copy(
-            src_ref=told.at[where["gx"]],
-            dst_ref=heard.at[mine],
-            send_sem=tell_sem.at[0],
-            recv_sem=hear_sem.at[0],
+            src_ref=src.at[where["gx"]],
+            dst_ref=dst.at[mine],
+            send_sem=tell_sem.at[i],
+            recv_sem=hear_sem.at[i],
             device_id=where,
             device_id_type=pl.DeviceIdType.MESH,
         )
 
-    own_weights = pltpu.make_async_copy(weight_block(gy), weights_got.at[gy], far_send.at[0, 0])
-    own_told = pltpu.make_async_copy(told.at[gx], heard.at[mine], hear_sem.at[0])
+    def tell_all(src, dst, i):
+        pltpu.make_async_copy(src.at[gx], dst.at[mine], hear_sem.at[i]).start()
+
+        def start(k, carry):
+            tell(k, src, dst, i).start()
+            return carry
+
+        lax.fori_loop(1, devices, start, 0)
+
+    own_weights = pltpu.make_async_copy(weight_block(gy), weights_got.at[gy], far_sem.at[0, 1])
 
     square = (per_dev, per_dev)
     eye = lax.broadcasted_iota(jnp.int32, square, 0) == lax.broadcasted_iota(jnp.int32, square, 1)
@@ -378,7 +385,7 @@
         def swapped(halo):
             return jnp.where(lane4 == 1, pltpu.roll(halo, nx - 1, 1), pltpu.roll(halo, 1, 1))
 
-        outer, own = (joined(0), xsend[r][c, 0])
+        outer, own = (joined(0), xsend[c, x_row(r, 0)])
         if r == 0:
             vh, bh = (joined(1), joined(2))
             bxh[c] = bh
@@ -401,8 +408,8 @@
         vxh[c] = vh
         hx[0, c] = swapped(outer)
         hx[1, c] = swapped(vh)
-        vyh[0, c] = vyh[0, c] - yrecv[0][0, c, 3] * (ysend[r][0, c, 0] - yrecv[r][0, c, 0])
-        vyh[1, c] = vyh[1, c] - yrecv[0][1, c, 3] * (yrecv[r][1, c, 1] - ysend[r][1, c, 1])
+        vyh[0, c] = vyh[0, c] - yrecv[0][0, c, 3] * (ysend[0, c, y_row(r, 0)] - yrecv[r][0, c, 0])
+        vyh[1, c] = vyh[1, c] - yrecv[0][1, c, 3] * (yrecv[r][1, c, 1] - ysend[1, c, y_row(r, 1)])
 
     def sweep(r, c):
         last, first = (r == STEPS - 1, r == 0)
@@ -441,23 +448,23 @@
                 p[z0 + j + 1] = new_p[j]
                 if not last:
                     totals[0] = pack(totals[0], new_p[j], zl)
-                    ysend[n][0, c, 0, at, :] = new_p[j][0:1]
-                    ysend[n][0, c, 1, at, :] = new_p[j][1:2]
-                    ysend[n][1, c, 0, at, :] = new_p[j][ny - 2 : ny - 1]
-                    ysend[n][1, c, 1, at, :] = new_p[j][ny - 1 : ny]
+                    ysend[0, c, y_row(n, 0), at, :] = new_p[j][0:1]
+                    ysend[0, c, y_row(n, 1), at, :] = new_p[j][1:2]
+                    ysend[1, c, y_row(n, 0), at, :] = new_p[j][ny - 2 : ny - 1]
+                    ysend[1, c, y_row(n, 1), at, :] = new_p[j][ny - 1 : ny]
                 if first:
                     totals[1] = pack(totals[1], ws[j], zl)
-                    ysend[n][0, c, 2, at, :] = vs[j][0:1]
-                    ysend[n][1, c, 2, at, :] = vs[j][ny - 1 : ny]
+                    ysend[0, c, y_row(n, 2), at, :] = vs[j][0:1]
+                    ysend[1, c, y_row(n, 2), at, :] = vs[j][ny - 1 : ny]
             return tuple(totals)
 
         count = 0 if last else X_PACKS[n]
         totals = lax.fori_loop(0, zc // BATCH, body, (plane,) * count)
         for i, total in enumerate(totals):
-            xsend[n][c, i] = total
+            xsend[c, x_row(n, i)] = total
         if not last:
-            csend[n - 1][c, 0] = totals[0][0:1]
-            csend[n - 1][c, 1] = totals[0][ny - 1 : ny]
+            csend[0, (n - 1) * chunks + c] = totals[0][0:1]
+            csend[1, (n - 1) * chunks + c] = totals[0][ny - 1 : ny]
 
     told_lane = lax.broadcasted_iota(jnp.int32, (1, 128), 1)
     in_place = quotient(told_lane, group_rows) == remainder(mine, 128 // group_rows)
@@ -519,7 +526,11 @@
             tile = begin - begin % 128
             piece = line[:, tile : tile + 128]
             spread = pltpu.roll(piece, remainder(mine * group_rows + (128 - begin % 128), 128), 1)
-            told[k, n - 1 : n, :] = jnp.where(in_place, spread, 0.0)
+            spread = jnp.where(in_place, spread, 0.0)
+            if n < STEPS:
+                told[k, n - 1] = spread
+            else:
+                told_last[k] = spread
         spectra_out[...] = spectra_out[...] + value * phase[n - 1 : n, :]
 
     def first_shear():
@@ -554,29 +565,31 @@
             total = total + factors[k] * got[rows[k]]
         note(n, shear[:, 0:1] + along(total))
 
-    for small in smalls:
-        small.wait()
-    told[...] = jnp.zeros(told.shape, jnp.float32)
-    fill_placing()
-    rows_send[...] = jnp.dot(
-        placing[...],
-        spectra_out[...],
-        preferred_element_type=jnp.float32,
-        precision=lax.Precision.HIGHEST,
-    )
-    for k in range(1, ngx):
-        first_to(k).start()
-    at = pl.ds(pl.multiple_of(gx * group_rows, group_rows), group_rows)
-    rows_group[at, :] = rows_send[at, :]
-    gather(B_OWN, own_rows(b, 0) + [lambda z, y: b[z, pl.ds(y, 1), :]])
     for c in range(chunks):
         for i in range(4, 9):
             load(i, c).wait()
 
+    def send_rows():
+        fill_placing()
+        rows_send[...] = jnp.dot(
+            placing[...],
+            spectra_out[...],
+            preferred_element_type=jnp.float32,
+            precision=lax.Precision.HIGHEST,
+        )
+        for k in range(1, ngx):
+            first_to(k).start()
+        at = pl.ds(pl.multiple_of(gx * group_rows, group_rows), group_rows)
+        rows_group[at, :] = rows_send[at, :]
+
     def work_after(r):
         if r == 0:
+            for small in smalls:
+                small.wait()
+            send_rows()
+            b_rows = own_rows(b, 0) + [lambda z, y: b[z, pl.ds(y, 1), :]]
             v_rows = own_rows(vx, 0) + [lambda z, y: vy[z, pl.ds(y, 1), :]]
-            gather(P_OWN, own_rows(p, 1) + v_rows)
+            gather(B_OWN, b_rows + own_rows(p, 1) + v_rows)
         elif r == 1:
             gather(
                 P_HALO,
@@ -599,22 +612,15 @@
     def last_shear():
         gather(P_HALO, halo_rows(STEPS - 1))
         next_shear(STEPS)
-        own_told.start()
-
-        def start(k, carry):
-            tell(k).start()
-            return carry
-
-        lax.fori_loop(1, devices, start, 0)
-
-    gaps = [(r, c) for r in range(STEPS - 1) for c in range(chunks)][1:]
+        tell_all(told_last, heard_last, 1)
+
+    gaps = [(r, c) for r in range(STEPS - 1) for c in range(chunks)][chunks:]
     jobs = {gap: [] for gap in gaps + [(STEPS - 1, 0), None]}
     order = list(jobs)
     pieces = [(j, h) for j in range(2, ngy, 2) for h in range(2)]
 
     def enter_rows():
-        for k in range(1, ngx):
-            first_from(k).wait_recv()
+        settle(rows_group.at[pl.ds(0, (ngx - 1) * group_rows)], far_sem.at[1, 1])
         at = pl.ds(pl.multiple_of(gy * all_rows, all_rows), all_rows)
         rows_out[at, :] = rows_group[...]
         for h in range(2):
@@ -629,6 +635,7 @@
         pass_on(j, h).start()
 
     jobs[order[0]].append(enter_rows)
+    jobs[STEPS - 1, 0].append(lambda: tell_all(told, heard, 0))
     for i, (j, h) in enumerate(pieces):
         place = i * len(gaps) // len(pieces)
         jobs[order[place]].append(functools.partial(leave, j, h))
@@ -658,37 +665,26 @@
 
         @pl.when(has[side])
         def _():
-            for r in range(STEPS):
-                if side in sides(r):
-                    for c in range(chunks):
-                        ends(r, c, side, False).wait_send()
-
-    own_weights.wait()
-    for k in range(1, ngy):
-        weights_from(k).wait_recv()
-        weights_to(k).wait_send()
-    for k in range(1, ngx):
-        first_to(k).wait_send()
-    for h in range(2):
-        for j in [1] + list(range(2, ngy, 2)):
-            direct_to(j, h).wait_send()
-        for j in range(2, ngy, 2):
-            pass_on(j, h).wait_send()
-        for j in range(1, ngy, 2):
-            block_from(j, h).wait_recv()
-    pltpu.make_async_copy(
-        heard.at[pl.ds(1, devices - 1)], heard.at[pl.ds(1, devices - 1)], tell_sem.at[0]
-    ).wait()
-    pltpu.make_async_copy(heard, heard, hear_sem.at[0]).wait()
+            sent = ysend.at[side] if side < 2 else xsend if side < 4 else csend.at[side // 2 - 2]
+            settle(sent, send_sem.at[side])
+
+    settle(weights_got.at[pl.ds(0, ngy - 1)], far_sem.at[0, 0])
+    settle(weights_got, far_sem.at[0, 1])
+    settle(rows_group.at[pl.ds(0, (ngx - 1) * group_rows)], far_sem.at[1, 0])
+    settle(rows_out.at[pl.ds(0, (ngy - 1) * all_rows)], block_sem.at[0, 1])
+    settle(rows_out.at[pl.ds(0, ngy // 2 * all_rows)], block_sem.at[0, 0])
+    for i, ref in enumerate([heard, heard_last]):
+        settle(ref.at[pl.ds(1, devices - 1)], tell_sem.at[i])
+        settle(ref, hear_sem.at[i])
 
 
 def finish_kernel(dims, *refs):
     nz, slot_count, share = dims
     refs = list(refs)
     take = lambda count: [refs.pop(0) for _ in range(count)]
-    vx, vy, vz, p, m, spectra, weights, rows, table, heard, phase = take(11)
+    vx, vy, vz, p, m, spectra, weights, rows, table, heard, heard_last, phase = take(12)
     vel_out, p_out, m_out, spectra_out, slip_out = take(5)
-    columns, slots, wide, exact, out_sem, slip_sem = take(6)
+    columns, slots, wide, exact, lines_in, out_sem, slip_sem = take(7)
     rup_group, lanes = (weights.shape[1], weights.shape[3])
     inner = pl.ds(1, nz)
     pairs = [
@@ -721,14 +717,14 @@
 
     count = heard.shape[0]
     per_tile = count * 128 // rows.shape[0]
-    tiles = [
-        functools.reduce(jnp.add, [heard[t * per_tile + k] for k in range(per_tile)])
-        for t in range(count // per_tile)
-    ]
-    for t, tile in enumerate(tiles):
-        at = pl.ds(t * 128, 128)
+    lines_in[...] = jnp.zeros(lines_in.shape, jnp.float32)
+    for t in range(count // per_tile):
+        at, of = (pl.ds(t * 128, 128), pl.ds(t * per_tile, per_tile))
+        for n in range(STEPS):
+            told = heard[of, n] if n < STEPS - 1 else heard_last[of]
+            lines_in[n : n + 1, :] = jnp.sum(told, axis=0)
         change = lax.dot_general(
-            tile,
+            lines_in[...],
             phase[...],
             (((0,), (0,)), ((), ())),
             preferred_element_type=jnp.float32,
@@ -814,17 +810,20 @@
             pltpu.VMEM((ngy, rup_group, slot_dev, lanes), jnp.bfloat16),
             pltpu.VMEM((ngy * all_rows, width), f32),
             pltpu.VMEM((rup_group, max(listed.shape[1], 128)), jnp.int32),
-            pltpu.VMEM((ngx * ngy, 8, 128), f32),
+            pltpu.VMEM((ngx * ngy, STEPS - 1, 1, 128), f32),
+            pltpu.VMEM((ngx * ngy, 1, 128), f32),
             pltpu.VMEM((8, width), f32),
         ],
         in_specs=[any_spec] * 13,
-        out_specs=[vmem_spec] * 11,
+        out_specs=[vmem_spec] * 12,
         scratch_shapes=[field(nz + 1), field(nz), field(nz), field(nz)]
+        + [
+            pltpu.VMEM((2, chunks, sum(Y_ROWS), zc, nx), f32),
+            pltpu.VMEM((chunks, sum(X_PACKS), ny, nx), f32),
+            pltpu.VMEM((2, (STEPS - 1) * chunks, 1, nx), f32),
+        ]
         + [pltpu.VMEM((2, chunks, Y_ROWS[r], zc, nx), f32) for r in rounds]
-        + [pltpu.VMEM((2, chunks, Y_ROWS[r], zc, nx), f32) for r in rounds]
-        + [pltpu.VMEM((chunks, X_PACKS[r], ny, nx), f32) for r in rounds]
         + [pltpu.VMEM((2, chunks, X_PACKS[r], ny, nx), f32) for r in rounds]
-        + [pltpu.VMEM((chunks, 2, 1, nx), f32) for r in rounds[1:]]
         + [pltpu.VMEM((chunks, 4, 1, nx), f32) for r in rounds[1:]]
         + [
             pltpu.SMEM((per_dev,), jnp.int32),
@@ -843,17 +842,16 @@
             pltpu.VMEM((per_dev, max(all_rows, 128)), f32),
             pltpu.VMEM((all_rows, width), f32),
             pltpu.VMEM((all_rows, width), f32),
-            pltpu.VMEM((ngx, 8, 128), f32),
+            pltpu.VMEM((ngx, STEPS - 1, 1, 128), f32),
+            pltpu.VMEM((ngx, 1, 128), f32),
             pltpu.SemaphoreType.DMA((9, chunks)),
             pltpu.SemaphoreType.DMA((5,)),
-            pltpu.SemaphoreType.DMA((STEPS, chunks, 8)),
-            pltpu.SemaphoreType.DMA((STEPS, chunks, 8)),
-            pltpu.SemaphoreType.DMA((2, max(ngx, ngy))),
-            pltpu.SemaphoreType.DMA((2, max(ngx, ngy))),
-            pltpu.SemaphoreType.DMA((ngy, 2)),
-            pltpu.SemaphoreType.DMA((ngy, 2)),
-            pltpu.SemaphoreType.DMA((1,)),
-            pltpu.SemaphoreType.DMA((1,)),
+            pltpu.SemaphoreType.DMA((8,)),
+            pltpu.SemaphoreType.DMA((2, chunks, 8)),
+            pltpu.SemaphoreType.DMA((2, 2)),
+            pltpu.SemaphoreType.DMA((ngy // 2, 2)),
+            pltpu.SemaphoreType.DMA((2,)),
+            pltpu.SemaphoreType.DMA((2,)),
         ],
         compiler_params=pltpu.CompilerParams(
             collective_id=0, has_side_effects=True, vmem_limit_bytes=VMEM_LIMIT
@@ -896,6 +894,7 @@
             pltpu.VMEM((rup_group * slot_count, width), jnp.bfloat16),
             pltpu.VMEM((rup_group, lanes, width), f32),
             pltpu.VMEM(state[7].shape, jnp.bfloat16),
+            pltpu.VMEM((8, 128), f32),
             pltpu.SemaphoreType.DMA((6,)),
             pltpu.SemaphoreType.DMA((rup_group,)),
         ],

time: 37.6 us -> 36.8 us (0.979)
  Pallas kernels: 36.8 us -> 36 us
    pallas_call x1, Pallas kernels: 33.5 us -> 32.7 us  [advance(): pl.pallas_call(functools.partial(step_kernel, dims), out_shape=[field(nz)...]
where the time goes in v3:
time: 36.8 us; the launch traced here: 36.7 us
  Pallas kernels  36 us (98%)
  between operations  0.64 us (2%)
    pallas_call x1, Pallas kernels, advance(): pl.pallas_call(functools.partial(step_kernel, dims), out_shape=[field(nz)...  32.7 us
    pallas_call x1, Pallas kernels, finish(): pl.pallas_call(functools.partial(finish_kernel, (nz, slot_count, share)),...  3.32 us

profile of v3, /device:TPU:0, one launch (start us, length us, event | category | flops | bytes accessed | tf_op | source)
XLA Modules:
  0.0 36.7 jit_solution(7849026611294200105)
XLA Ops:
  0.6 32.7 %shard_map.155 = (f32[64,32,128]{2,1,0:T(8,128)S(1)}, f32[64,32,128]{2,1,0:T(8,128)S(1)}, f32[66,32,128]{2,1,0:T(8,128)S(1)}, f32[67,32,128]{2,1,0:T(8,128)S(1)}...) custom-call(f32[3,64,32,128]{3,2,1,0:T(8,128)} %refs_0_.1, ...), custom_call_target="tpu_custom_call" | custom-call | tf_op jit(solution)/shard_map/pallas_call | solution.py:801
  33.4 3.3 %shard_map.156 = (f32[3,64,32,128]{3,2,1,0:T(8,128)}, f32[64,32,128]{2,1,0:T(8,128)}, f32[64,32,128]{2,1,0:T(8,128)}, f32[64,256]{1,0:T(8,128)}, f32[8,64,256]{2,1,0:T(8,128)}) custom-call(f32[64,32,128]{2,1,0:T(8,128)S(1)} %get-tuple-element.17.refs_0_, f32[64,32,128]{2,1,0:T(8,128)S(1)} %get-tuple-element.18.refs_1_, ...), custom_call_target="tpu_custom_call" | custom-call | tf_op jit(solution)/shard_map/pallas_call | solution.py:881

commit v4 on v3

--- a/solution.py
+++ b/solution.py
@@ -1,4 +1,5 @@
 import functools
+import math
 
 import jax
 import jax.numpy as jnp
@@ -41,15 +42,16 @@
     refs = list(refs)
     take = lambda count: [refs.pop(0) for _ in range(count)]
     vel_in, p_in, m_in, b_in, mod_in, rel_in, str_in = take(7)
-    spectra_in, cell_in, cell_row_in, phase_in, listed_in, weights = take(6)
-    vx, vy, vz, p, m, spectra_out, weights_got, rows_out, table, heard, heard_last, phase = take(12)
-    b, mod, rel, stg = take(4)
+    spectra_in, cell_row_in, phase_in, listed_in, weights = take(5)
+    vx, vy, vz, p, m, spectra_out, mixed, rows_out, heard, heard_last, phase = take(11)
+    b, mod, rel, stg, vx_old, vy_old, p_old, b_east = take(8)
     ysend, xsend, csend = take(3)
-    yrecv, xrecv, crecv = (take(STEPS), take(STEPS), take(STEPS - 1))
-    cell, cell_row, listed = take(3)
-    vxh, bxh, hx, vyh, vyx, xj, got, shear, factors = take(9)
+    yrecv, xrecv, crecv = (take(STEPS), take(STEPS), take(STEPS))
+    cell_row, listed, index_made, index = take(4)
+    vxh, bwh, bxh, hx, hx_old, vyh, vyx, xj, got, shear, factors = take(11)
+    hp, hv, hb, weights_got, table, columns, wide = take(7)
     placing, placed, rows_send, rows_group, told, told_last = take(6)
-    in_sem, small_sem, send_sem, recv_sem, far_sem, block_sem, tell_sem, hear_sem = take(8)
+    in_sem, small_sem, send_sem, recv_sem, far_sem, block_sem, tell_sem, hear_sem, index_sem = take(9)
 
     gx, gy = (lax.axis_index("gx"), lax.axis_index("gy"))
     has = [gy > 0, gy < ngy - 1, gx > 0, gx < ngx - 1]
@@ -61,10 +63,10 @@
         at = pl.ds(c * zc, zc)
         moved = pl.ds(c * zc + 1, zc)
         src, dst = [
-            (p_in.at[at], p.at[moved]),
+            (p_in.at[at], p_old.at[moved]),
             (b_in.at[at], b.at[at]),
-            (vel_in.at[0, at], vx.at[at]),
-            (vel_in.at[1, at], vy.at[at]),
+            (vel_in.at[0, at], vx_old.at[at]),
+            (vel_in.at[1, at], vy_old.at[at]),
             (vel_in.at[2, at], vz.at[moved]),
             (rel_in.at[at], rel.at[at]),
             (m_in.at[at], m.at[at]),
@@ -80,7 +82,6 @@
         pltpu.make_async_copy(src, dst, small_sem.at[i])
         for i, (src, dst) in enumerate(
             [
-                (cell_in, cell),
                 (cell_row_in, cell_row),
                 (listed_in, listed),
                 (phase_in, phase),
@@ -114,18 +115,23 @@
 
     barrier = pltpu.get_barrier_semaphore()
 
-    def greet(k, carry):
+    peers = [{"gx": lax.rem(gx + k, ngx)} for k in range(1, ngx)]
+    peers = peers + [{"gy": lax.rem(gy + k, ngy)} for k in range(1, ngy)]
+    peers = peers + [
+        {"gy": lax.rem(gy + ngy + dy, ngy), "gx": lax.rem(gx + ngx + dx, ngx)}
+        for dy in (-1, 1)
+        for dx in (-1, 1)
+    ]
+    for other in peers:
         pl.semaphore_signal(
-            barrier, inc=1, device_id=other_device(k), device_id_type=pl.DeviceIdType.MESH
+            barrier, inc=1, device_id=other, device_id_type=pl.DeviceIdType.MESH
         )
-        return carry
-
-    lax.fori_loop(1, devices, greet, 0)
 
     plane = jnp.zeros((ny, nx), jnp.float32)
-    p[0] = plane
-    p[nz + 1] = plane
-    p[nz + 2] = plane
+    for field in (p_old, p):
+        field[0] = plane
+        field[nz + 1] = plane
+        field[nz + 2] = plane
     vz[0] = plane
     vz[nz + 1] = plane
     b[nz] = plane
@@ -138,9 +144,9 @@
                     yrecv[r][side] = jnp.zeros(yrecv[r].shape[1:], jnp.float32)
                 elif side < 4:
                     xrecv[r][side - 2] = jnp.zeros(xrecv[r].shape[1:], jnp.float32)
-                elif r > 0:
+                else:
                     for c in range(chunks):
-                        crecv[r - 1][c, side - 4] = jnp.zeros((1, nx), jnp.float32)
+                        crecv[r][c, side - 4] = jnp.zeros((1, nx), jnp.float32)
 
     def ends(r, c, side, coming):
         k = side % 4
@@ -156,8 +162,8 @@
             arrives = 2 + there
         else:
             there = k if coming else 3 - k
-            src = csend.at[k // 2, (r - 1) * chunks + c]
-            dst = crecv[r - 1].at[c, there]
+            src = csend.at[k // 2, r * chunks + c]
+            dst = crecv[r].at[c, there]
             arrives = 4 + there
         return pltpu.make_async_remote_copy(
             src_ref=src,
@@ -168,18 +174,15 @@
             device_id_type=pl.DeviceIdType.MESH,
         )
 
-    def sides(r):
-        return range(4) if r == 0 else range(8)
-
     def send(r, c):
-        for side in sides(r):
+        for side in range(8):
 
             @pl.when(has[side])
             def _():
                 ends(r, c, side, False).start()
 
     def receive(r, c):
-        for side in sides(r):
+        for side in range(8):
 
             @pl.when(has[side])
             def _():
@@ -188,18 +191,11 @@
     lane = lax.broadcasted_iota(jnp.int32, (ny, nx), 1)
     row = lax.broadcasted_iota(jnp.int32, (ny, nx), 0)
     quad, lane4 = (quotient(lane, 4), remainder(lane, 4))
-    last_lane, first_lane = (lane == nx - 1, lane == 0)
     last_row, first_row = (row == ny - 1, row == 0)
     west_half = remainder(lax.broadcasted_iota(jnp.int32, (1, nx), 1), 4) < 2
 
     def pack(total, slab, zl):
         return jnp.where(quad == zl, pltpu.roll(slab, 4 * zl + 2, 1), total)
-
-    def d_x(slab, halo, zl):
-        ends = pltpu.roll(halo, nx - 2 - 4 * zl, 1)
-        after = jnp.where(last_lane, ends, pltpu.roll(slab, nx - 1, 1))
-        before = jnp.where(first_lane, ends, pltpu.roll(slab, 1, 1))
-        return after - before
 
     def d_y(slab, south, north):
         after = jnp.where(last_row, north, pltpu.roll(slab, ny - 1, 0))
@@ -215,7 +211,7 @@
             for j in range(BATCH):
                 zl = i * BATCH + j
                 z = c * zc + zl
-                ps, vs, ws, bs = (p[z + 1], vx[z], vy[z], b[z])
+                ps, vs, ws, bs = (p_old[z + 1], vx_old[z], vy_old[z], b[z])
                 pt, vt, bt = (pack(pt, ps, zl), pack(vt, vs, zl), pack(bt, bs, zl))
                 at = pl.ds(zl, 1)
                 ysend[0, c, y_row(0, 0), at, :] = ps[0:1]
@@ -231,8 +227,10 @@
         totals = lax.fori_loop(0, zc // BATCH, edges, (plane, plane, plane))
         for i, total in enumerate(totals):
             xsend[c, x_row(0, i)] = total
+        csend[0, c] = totals[0][0:1]
+        csend[1, c] = totals[0][ny - 1 : ny]
         if c == 0:
-            pl.semaphore_wait(barrier, devices - 1)
+            pl.semaphore_wait(barrier, len(peers))
         send(0, c)
 
     rup_group, slot_dev, variations = weights.shape
@@ -382,32 +380,36 @@
         def joined(i):
             return jnp.where(lane4 < 2, xrecv[r][0, c, i], xrecv[r][1, c, i])
 
-        def swapped(halo):
-            return jnp.where(lane4 == 1, pltpu.roll(halo, nx - 1, 1), pltpu.roll(halo, 1, 1))
-
-        outer, own = (joined(0), xsend[c, x_row(r, 0)])
+        west, east, own = (xrecv[r][0, c, 0], xrecv[r][1, c, 0], xsend[c, x_row(r, 0)])
         if r == 0:
-            vh, bh = (joined(1), joined(2))
-            bxh[c] = bh
+
+            def edge(i):
+                return jnp.where(lane4 == 1, xrecv[0][0, c, i], xsend[c, x_row(0, i)])
+
+            vh, bh = (pltpu.roll(edge(1), 1, 1), pltpu.roll(edge(2), 1, 1))
+            bwh[c] = bh
+            bxh[c] = joined(2)
+            hx_old[c] = jnp.where(
+                lane4 == 1, pltpu.roll(xrecv[0][1, c, 2], nx - 1, 1), xrecv[0][1, c, 1]
+            )
             vyh[0, c] = yrecv[0][0, c, 2]
             vyh[1, c] = yrecv[0][1, c, 2]
+            for side in range(2):
+                hb[side, c] = yrecv[0][side, c, 3]
         else:
-            vh, bh = (vxh[c], bxh[c])
-            corner = crecv[r - 1]
-            xj[c, 7:8, :] = jnp.where(west_half, corner[c, 0], corner[c, 1])
-            xj[c, 8 : 8 + ny, :] = outer
-            xj[c, 8 + ny : 9 + ny, :] = jnp.where(west_half, corner[c, 2], corner[c, 3])
+            vh, bh = (vxh[c], bwh[c])
             if r == 1:
                 vyx[c] = joined(1)
-        slope = jnp.where(
-            lane4 == 1,
-            pltpu.roll(own, nx - 1, 1) - pltpu.roll(outer, 1, 1),
-            pltpu.roll(outer, nx - 1, 1) - pltpu.roll(own, 1, 1),
-        )
-        vh = vh - bh * slope
+                for side in range(2):
+                    hv[side, c] = yrecv[1][side, c, 2]
+        for side in range(2):
+            hp[r % 2, side, c] = yrecv[r][side, c, 1 - side]
+        xj[r % 2, c, 7:8, :] = jnp.where(west_half, crecv[r][c, 0], crecv[r][c, 1])
+        xj[r % 2, c, 8 : 8 + ny, :] = joined(0)
+        xj[r % 2, c, 8 + ny : 9 + ny, :] = jnp.where(west_half, crecv[r][c, 2], crecv[r][c, 3])
+        vh = vh - bh * (own - pltpu.roll(west, 2, 1))
         vxh[c] = vh
-        hx[0, c] = swapped(outer)
-        hx[1, c] = swapped(vh)
+        hx[c] = jnp.where(lane4 < 2, pltpu.roll(east, nx - 2, 1), vh)
         vyh[0, c] = vyh[0, c] - yrecv[0][0, c, 3] * (ysend[0, c, y_row(r, 0)] - yrecv[r][0, c, 0])
         vyh[1, c] = vyh[1, c] - yrecv[0][1, c, 3] * (yrecv[r][1, c, 1] - ysend[1, c, y_row(r, 1)])
 
@@ -419,21 +421,37 @@
             totals = list(totals)
             base = i * BATCH
             z0 = c * zc + base
-            ps = [p[z0 + 1 + j] for j in range(BATCH + 2)]
+            p_from = p_old if first else p
+            ps = [p_from[z0 + 1 + j] for j in range(BATCH + 2)]
             bs = [b[z0 + j] for j in range(BATCH + 1)]
             zs = [vz[z0], vz[z0 + 1]]
-            vs, ws, new_p = ([], [], [])
+            vs, ws, new_p, outer = ([], [], [], [])
             for j in range(BATCH):
                 zl = base + j
                 at = pl.ds(zl, 1)
+                turn = nx - 2 - 4 * zl
                 zs.append(vz[z0 + j + 2] - bs[j + 1] * (ps[j + 2] - ps[j]))
-                vs.append(vx[z0 + j] - bs[j] * d_x(ps[j], hx[0, c], zl))
+                outer.append(pltpu.roll(hx[c], turn, 1))
+                ahead = jnp.where(lane >= nx - 2, outer[j], pltpu.roll(ps[j], nx - 2, 1))
+                if first:
+                    old = pltpu.roll(hx_old[c], turn, 1)
+                    shifted = jnp.where(lane == nx - 1, old, pltpu.roll(bs[j], nx - 1, 1))
+                    b_east[z0 + j] = shifted
+                    speed = pltpu.roll(jnp.where(lane == 0, old, vx_old[z0 + j]), nx - 1, 1)
+                else:
+                    shifted, speed = (b_east[z0 + j], vx[z0 + j])
+                vs.append(speed - shifted * (ahead - ps[j]))
                 south, north = (yrecv[r][0, c, 1, at, :], yrecv[r][1, c, 0, at, :])
-                ws.append(vy[z0 + j] - bs[j] * d_y(ps[j], south, north))
+                side_speed = vy_old[z0 + j] if first else vy[z0 + j]
+                ws.append(side_speed - bs[j] * d_y(ps[j], south, north))
             for j in range(BATCH):
                 zl = base + j
                 at = pl.ds(zl, 1)
-                spread = d_x(vs[j], hx[1, c], zl) + d_y(ws[j], vyh[0, c, at, :], vyh[1, c, at, :])
+                turned = pltpu.roll(vs[j], 2, 1)
+                spread = vs[j] - jnp.where(lane < 2, outer[j], turned)
+                if last:
+                    vs[j] = pltpu.roll(jnp.where(lane == 1, outer[j], turned), nx - 1, 1)
+                spread = spread + d_y(ws[j], vyh[0, c, at, :], vyh[1, c, at, :])
                 spread = spread + (zs[j + 2] - zs[j])
                 mem = m[z0 + j]
                 mem = mem - rel[z0 + j] * (mem + stg[z0 + j] * spread)
@@ -453,9 +471,9 @@
                     ysend[1, c, y_row(n, 0), at, :] = new_p[j][ny - 2 : ny - 1]
                     ysend[1, c, y_row(n, 1), at, :] = new_p[j][ny - 1 : ny]
                 if first:
-                    totals[1] = pack(totals[1], ws[j], zl)
-                    ysend[0, c, y_row(n, 2), at, :] = vs[j][0:1]
-                    ysend[1, c, y_row(n, 2), at, :] = vs[j][ny - 1 : ny]
+                    totals[1] = pack(totals[1], vy_old[z0 + j], zl)
+                    ysend[0, c, y_row(n, 2), at, :] = vx_old[z0 + j, 0:1, :]
+                    ysend[1, c, y_row(n, 2), at, :] = vx_old[z0 + j, ny - 1 : ny, :]
             return tuple(totals)
 
         count = 0 if last else X_PACKS[n]
@@ -463,8 +481,8 @@
         for i, total in enumerate(totals):
             xsend[c, x_row(n, i)] = total
         if not last:
-            csend[0, (n - 1) * chunks + c] = totals[0][0:1]
-            csend[1, (n - 1) * chunks + c] = totals[0][ny - 1 : ny]
+            csend[0, n * chunks + c] = totals[0][0:1]
+            csend[1, n * chunks + c] = totals[0][ny - 1 : ny]
 
     told_lane = lax.broadcasted_iota(jnp.int32, (1, 128), 1)
     in_place = quotient(told_lane, group_rows) == remainder(mine, 128 // group_rows)
@@ -473,42 +491,52 @@
     def masked(keep, values):
         return jnp.where(keep, values, 0.0)
 
-    def gather(first_slot, rows):
+    def flat(ref):
+        return ref.reshape(math.prod(ref.shape[:-1]), ref.shape[-1])
+
+    UP, DOWN, MID, HALO, EDGE, PACK = range(6)
+
+    def make_index():
+        cells = cell_row[...]
+        z, y = (quotient(cells, ny * nx), remainder(quotient(cells, nx), ny))
+        c, zl = (quotient(z, zc), remainder(z, zc))
+        side = jnp.where(y == 0, 0, 1)
+        rows = [
+            z * ny + jnp.minimum(y + 1, ny - 1),
+            z * ny + jnp.maximum(y - 1, 0),
+            z * ny + y,
+            (side * chunks + c) * zc + zl,
+            c * (ny + 16) + y,
+            c * ny + y,
+        ]
+        index_made[...] = jnp.zeros(index_made.shape, jnp.int32)
+        for k, values in enumerate(rows):
+            index_made[k : k + 1, :per_dev] = values
+
+    def gather(*wanted):
+        refs = [(slot, flat(ref), which, shift) for slot, ref, which, shift in wanted]
+
         def body(i, carry):
-            at = cell[i]
-            z, y = (quotient(at, ny * nx), remainder(quotient(at, nx), ny))
+            at = {which: index[which, i] for which in sorted({w[2] for w in refs})}
             out = pl.ds(i, 1)
-            for k, row in enumerate(rows):
-                got[first_slot + k, out, :] = row(z, y)
+            for slot, ref, which, shift in refs:
+                got[slot, out, :] = ref[pl.ds(at[which] + shift, 1), :]
             return carry
 
         lax.fori_loop(0, per_dev, body, 0, unroll=8)
 
-    def row_up(ref, z, y):
-        return ref[z, pl.ds(jnp.minimum(y + 1, ny - 1), 1), :]
-
-    def row_down(ref, z, y):
-        return ref[z, pl.ds(jnp.maximum(y - 1, 0), 1), :]
-
-    def row_halo(ref, index, z, y):
-        side = jnp.where(y == 0, 0, 1)
-        which = 1 - side if index is None else index
-        return ref[side, quotient(z, zc), which, pl.ds(remainder(z, zc), 1), :]
-
-    def row_pack(ref, shift, z, y):
-        return ref[quotient(z, zc), pl.ds(y + shift, 1), :]
-
-    def own_rows(ref, lift):
-        return [lambda z, y: row_up(ref, z + lift, y), lambda z, y: row_down(ref, z + lift, y)]
-
-    def halo_rows(n):
+    B_OWN, P_OWN, V_OWN, P_HALO, V_HALO, B_HALO, OLD_OWN, OLD_HALO = (0, 3, 5, 8, 11, 13, 15, 17)
+
+    def own_rows(slot, ref, shift):
+        return [(slot, ref, UP, shift), (slot + 1, ref, DOWN, shift)]
+
+    def halo_rows(slot, n):
+        edge = xj.at[n % 2]
         return [
-            lambda z, y: row_halo(yrecv[n], None, z, y),
-            lambda z, y: row_pack(xj, 9, z, y),
-            lambda z, y: row_pack(xj, 7, z, y),
+            (slot, hp.at[n % 2], HALO, 0),
+            (slot + 1, edge, EDGE, 9),
+            (slot + 2, edge, EDGE, 7),
         ]
-
-    B_OWN, P_OWN, V_OWN, P_HALO, V_HALO, B_HALO = (0, 3, 5, 8, 11, 13)
 
     def places():
         cells = to_column(cell_row[...].astype(jnp.float32)).astype(jnp.int32)
@@ -533,18 +561,25 @@
                 told_last[k] = spread
         spectra_out[...] = spectra_out[...] + value * phase[n - 1 : n, :]
 
-    def first_shear():
+    def marks():
         cell_x, cell_y, start = places()
         here = patch_lane == cell_x
         up, down = (cell_y < ny - 1, cell_y > 0)
         ahead, behind = (patch_lane == cell_x + 1, patch_lane == cell_x - 1)
         ahead_out = (patch_lane == start + 2) & (cell_x == nx - 1)
         behind_out = (patch_lane == start + 1) & (cell_x == 0)
+        return here, up, down, ahead, behind, ahead_out, behind_out
+
+    def first_shear():
+        here, up, down, ahead, behind, ahead_out, behind_out = marks()
         total = masked(here, jnp.where(up, got[V_OWN], got[V_HALO]))
         total = total - masked(here, jnp.where(down, got[V_OWN + 1], got[V_HALO]))
         total = total + masked(ahead, got[V_OWN + 2]) - masked(behind, got[V_OWN + 2])
         total = total + masked(ahead_out, got[V_HALO + 1]) - masked(behind_out, got[V_HALO + 1])
-        note(1, along(total))
+        shear[...] = jnp.broadcast_to(along(total), shear.shape)
+
+    def make_factors():
+        here, up, down, ahead, behind, ahead_out, behind_out = marks()
         b_up = along(masked(here, jnp.where(up, got[B_OWN], got[B_HALO])))
         b_down = along(masked(here, jnp.where(down, got[B_OWN + 1], got[B_HALO])))
         b_mid, b_out = (got[B_OWN + 2], got[B_HALO + 1])
@@ -558,13 +593,18 @@
         factors[3] = masked(behind_out, b_up + b_behind) - masked(ahead_out, b_up + b_ahead)
         factors[4] = masked(ahead_out, b_down + b_ahead) - masked(behind_out, b_down + b_behind)
 
-    def next_shear(n):
-        rows = [P_OWN, P_OWN + 1, P_HALO, P_HALO + 1, P_HALO + 2]
+    def next_shear(n, own=P_OWN, halo=P_HALO):
+        rows = [own, own + 1, halo, halo + 1, halo + 2]
         total = factors[0] * got[rows[0]]
         for k in range(1, 5):
             total = total + factors[k] * got[rows[k]]
         note(n, shear[:, 0:1] + along(total))
 
+    for small in smalls:
+        small.wait()
+    make_index()
+    index_copy = pltpu.make_async_copy(index_made, index, index_sem.at[0])
+    index_copy.start()
     for c in range(chunks):
         for i in range(4, 9):
             load(i, c).wait()
@@ -582,35 +622,78 @@
         at = pl.ds(pl.multiple_of(gx * group_rows, group_rows), group_rows)
         rows_group[at, :] = rows_send[at, :]
 
+    def mix():
+        slot_count = slot_dev * ngy
+        lines = min(slot_count, 128)
+        depth = min(mixed.shape[1], 512)
+        share = mixed.shape[0] // rup_group
+        begin = pl.multiple_of(lax.rem(gy * share, lanes), share)
+        block = (lines, lines)
+        own_line = lax.broadcasted_iota(jnp.int32, block, 0) == lax.broadcasted_iota(
+            jnp.int32, block, 1
+        )
+        row_at = lax.broadcasted_iota(jnp.int32, (slot_count, depth), 1)
+        for r in range(rup_group):
+            for k in range(slot_count // lines):
+                line = table[r : r + 1, k * lines : (k + 1) * lines].astype(jnp.float32)
+                column = jnp.sum(jnp.where(own_line, line, 0.0), axis=1, keepdims=True)
+                at = pl.ds(k * lines, lines)
+                columns[r, at, :] = jnp.broadcast_to(
+                    column.astype(jnp.int32), (lines, columns.shape[2])
+                )
+
+        def blend(r, k):
+            base = k * depth
+            chosen = jnp.where(row_at + base == columns[r, :, 0:1], 1.0, 0.0).astype(jnp.bfloat16)
+            own = weights_got[:, r].astype(jnp.float32).reshape(slot_count, lanes)
+            spread = lax.dot_general(
+                own.astype(jnp.bfloat16),
+                chosen,
+                (((0,), (0,)), ((), ())),
+                preferred_element_type=jnp.float32,
+            )
+            wide[r] = spread
+            rows = pl.ds(r * share, share)
+            mixed[rows, pl.ds(base, depth)] = wide[r, pl.ds(begin, share), :].astype(jnp.bfloat16)
+
+        for r in range(rup_group):
+            if mixed.shape[1] == depth:
+                blend(r, 0)
+            else:
+
+                @pl.loop(0, mixed.shape[1] // depth)
+                def _(k):
+                    blend(r, k)
+
     def work_after(r):
         if r == 0:
-            for small in smalls:
-                small.wait()
             send_rows()
-            b_rows = own_rows(b, 0) + [lambda z, y: b[z, pl.ds(y, 1), :]]
-            v_rows = own_rows(vx, 0) + [lambda z, y: vy[z, pl.ds(y, 1), :]]
-            gather(B_OWN, b_rows + own_rows(p, 1) + v_rows)
+            index_copy.wait()
+            gather(
+                *own_rows(B_OWN, b, 0),
+                (B_OWN + 2, b, MID, 0),
+                *own_rows(V_OWN, vx_old, 0),
+                (V_OWN + 2, vy_old, MID, 0),
+                (B_HALO, hb, HALO, 0),
+                (B_HALO + 1, bxh, PACK, 0),
+                *own_rows(OLD_OWN, p_old, ny),
+                *halo_rows(OLD_HALO, 0),
+                *own_rows(P_OWN, p, ny),
+            )
+            make_factors()
         elif r == 1:
-            gather(
-                P_HALO,
-                halo_rows(1)
-                + [
-                    lambda z, y: row_halo(yrecv[1], 2, z, y),
-                    lambda z, y: row_pack(vyx, 0, z, y),
-                    lambda z, y: row_halo(yrecv[0], 3, z, y),
-                    lambda z, y: row_pack(bxh, 0, z, y),
-                ],
-            )
+            gather(*halo_rows(P_HALO, 1), (V_HALO, hv, HALO, 0), (V_HALO + 1, vyx, PACK, 0))
             first_shear()
+            next_shear(1, OLD_OWN, OLD_HALO)
             next_shear(2)
-            gather(P_OWN, own_rows(p, 1))
+            gather(*own_rows(P_OWN, p, ny))
         elif r < STEPS - 1:
-            gather(P_HALO, halo_rows(r))
+            gather(*halo_rows(P_HALO, r))
             next_shear(r + 1)
-            gather(P_OWN, own_rows(p, 1))
+            gather(*own_rows(P_OWN, p, ny))
 
     def last_shear():
-        gather(P_HALO, halo_rows(STEPS - 1))
+        gather(*halo_rows(P_HALO, STEPS - 1))
         next_shear(STEPS)
         tell_all(told_last, heard_last, 1)
 
@@ -646,7 +729,8 @@
         jobs[order[place]].append(lambda k=k: weights_to(k).start())
 
     for r in range(STEPS):
-        vz[1] = vz[1] - b[0] * (p[2] - p[0])
+        above = p_old if r == 0 else p
+        vz[1] = vz[1] - b[0] * (above[2] - above[0])
         for c in range(chunks):
             receive(r, c)
             halos(r, c)
@@ -670,6 +754,7 @@
 
     settle(weights_got.at[pl.ds(0, ngy - 1)], far_sem.at[0, 0])
     settle(weights_got, far_sem.at[0, 1])
+    mix()
     settle(rows_group.at[pl.ds(0, (ngx - 1) * group_rows)], far_sem.at[1, 0])
     settle(rows_out.at[pl.ds(0, (ngy - 1) * all_rows)], block_sem.at[0, 1])
     settle(rows_out.at[pl.ds(0, ngy // 2 * all_rows)], block_sem.at[0, 0])
@@ -678,14 +763,12 @@
         settle(ref, hear_sem.at[i])
 
 
-def finish_kernel(dims, *refs):
-    nz, slot_count, share = dims
+def finish_kernel(nz, *refs):
     refs = list(refs)
     take = lambda count: [refs.pop(0) for _ in range(count)]
-    vx, vy, vz, p, m, spectra, weights, rows, table, heard, heard_last, phase = take(12)
+    vx, vy, vz, p, m, spectra, mixed, rows, heard, heard_last, phase = take(11)
     vel_out, p_out, m_out, spectra_out, slip_out = take(5)
-    columns, slots, wide, exact, lines_in, out_sem, slip_sem = take(7)
-    rup_group, lanes = (weights.shape[1], weights.shape[3])
+    slip, exact, lines_in, out_sem, slip_sem = take(5)
     inner = pl.ds(1, nz)
     pairs = [
         (vx, vel_out.at[0]),
@@ -701,20 +784,6 @@
     for store in stores:
         store.start()
 
-    size, depth = (min(rup_group * slot_count, 512), min(rows.shape[0], 512))
-    lines = min(slot_count, 128)
-    square = (lines, lines)
-    eye = lax.broadcasted_iota(jnp.int32, square, 0) == lax.broadcasted_iota(jnp.int32, square, 1)
-    row_at = lax.broadcasted_iota(jnp.int32, (size, depth), 1)
-    start = pl.multiple_of(remainder(lax.axis_index("gy") * share, lanes), share)
-
-    for r in range(rup_group):
-        for k in range(slot_count // lines):
-            line = table[r : r + 1, k * lines : (k + 1) * lines].astype(jnp.float32)
-            column = jnp.sum(jnp.where(eye, line, 0.0), axis=1, keepdims=True).astype(jnp.int32)
-            at = pl.ds(r * slot_count + k * lines, lines)
-            columns[at, :] = jnp.broadcast_to(column, (lines, columns.shape[1]))
-
     count = heard.shape[0]
     per_tile = count * 128 // rows.shape[0]
     lines_in[...] = jnp.zeros(lines_in.shape, jnp.float32)
@@ -722,56 +791,25 @@
         at, of = (pl.ds(t * 128, 128), pl.ds(t * per_tile, per_tile))
         for n in range(STEPS):
             told = heard[of, n] if n < STEPS - 1 else heard_last[of]
-            lines_in[n : n + 1, :] = jnp.sum(told, axis=0)
+            lines_in[n : n + 1, at] = jnp.sum(told, axis=0)
+    for t in range(count // per_tile):
+        at = pl.ds(t * 128, 128)
         change = lax.dot_general(
-            lines_in[...],
+            lines_in[:, at],
             phase[...],
             (((0,), (0,)), ((), ())),
             preferred_element_type=jnp.float32,
             precision=lax.Precision.HIGHEST,
         )
         exact[at, :] = (rows[at, :] + change).astype(jnp.bfloat16)
-
-    def choose(i, carry):
-        at = pl.ds(pl.multiple_of(i * size, size), size)
-        column = columns[at, 0:1]
-
-        def part(k, total):
-            base = pl.multiple_of(k * depth, depth)
-            chosen = jnp.where(row_at + base == column, 1.0, 0.0).astype(jnp.bfloat16)
-            return total + jnp.dot(
-                chosen, exact[pl.ds(base, depth), :], preferred_element_type=jnp.float32
-            )
-
-        total = jnp.zeros((size, rows.shape[1]), jnp.float32)
-        if rows.shape[0] == depth:
-            total = part(0, total)
-        else:
-            total = lax.fori_loop(0, rows.shape[0] // depth, part, total)
-        slots[at, :] = total.astype(jnp.bfloat16)
-        return carry
-
-    if slots.shape[0] == size:
-        choose(0, 0)
-    else:
-        lax.fori_loop(0, slots.shape[0] // size, choose, 0)
-    for r in range(rup_group):
-        own = weights[:, r].astype(jnp.float32).reshape(slot_count, lanes).astype(jnp.bfloat16)
-        wide[r] = lax.dot_general(
-            own,
-            slots[pl.ds(r * slot_count, slot_count), :],
-            (((0,), (0,)), ((), ())),
-            preferred_element_type=jnp.float32,
-        )
-        pltpu.make_async_copy(
-            wide.at[r, pl.ds(start, share)], slip_out.at[r], slip_sem.at[r]
-        ).start()
+    rup_group, share = slip.shape[:2]
+    response = jnp.dot(mixed[...], exact[...], preferred_element_type=jnp.float32)
+    slip[...] = response.reshape(slip.shape)
+    answer = pltpu.make_async_copy(slip, slip_out, slip_sem.at[0])
+    answer.start()
     for store in stores:
         store.wait()
-    for r in range(rup_group):
-        pltpu.make_async_copy(
-            wide.at[r, pl.ds(start, share)], slip_out.at[r], slip_sem.at[r]
-        ).wait()
+    answer.wait()
 
 
 VMEM_LIMIT = 40 * 1024 * 1024
@@ -807,37 +845,47 @@
             field(nz + 3),
             field(nz),
             pltpu.VMEM(spectra.shape, f32),
-            pltpu.VMEM((ngy, rup_group, slot_dev, lanes), jnp.bfloat16),
+            pltpu.VMEM((rup_group * (variations // ngy), ngy * all_rows), jnp.bfloat16),
             pltpu.VMEM((ngy * all_rows, width), f32),
-            pltpu.VMEM((rup_group, max(listed.shape[1], 128)), jnp.int32),
             pltpu.VMEM((ngx * ngy, STEPS - 1, 1, 128), f32),
             pltpu.VMEM((ngx * ngy, 1, 128), f32),
             pltpu.VMEM((8, width), f32),
         ],
-        in_specs=[any_spec] * 13,
-        out_specs=[vmem_spec] * 12,
+        in_specs=[any_spec] * 12,
+        out_specs=[vmem_spec] * 11,
         scratch_shapes=[field(nz + 1), field(nz), field(nz), field(nz)]
+        + [field(nz), field(nz), field(nz + 3), field(nz)]
         + [
             pltpu.VMEM((2, chunks, sum(Y_ROWS), zc, nx), f32),
             pltpu.VMEM((chunks, sum(X_PACKS), ny, nx), f32),
-            pltpu.VMEM((2, (STEPS - 1) * chunks, 1, nx), f32),
+            pltpu.VMEM((2, STEPS * chunks, 1, nx), f32),
         ]
         + [pltpu.VMEM((2, chunks, Y_ROWS[r], zc, nx), f32) for r in rounds]
         + [pltpu.VMEM((2, chunks, X_PACKS[r], ny, nx), f32) for r in rounds]
-        + [pltpu.VMEM((chunks, 4, 1, nx), f32) for r in rounds[1:]]
+        + [pltpu.VMEM((chunks, 4, 1, nx), f32) for r in rounds]
         + [
-            pltpu.SMEM((per_dev,), jnp.int32),
             pltpu.VMEM((1, per_dev), jnp.int32),
             pltpu.VMEM(listed.shape, jnp.int32),
+            pltpu.VMEM((8, max(per_dev, 128)), jnp.int32),
+            pltpu.SMEM((8, max(per_dev, 128)), jnp.int32),
             pltpu.VMEM((chunks, ny, nx), f32),
             pltpu.VMEM((chunks, ny, nx), f32),
-            pltpu.VMEM((2, chunks, ny, nx), f32),
+            pltpu.VMEM((chunks, ny, nx), f32),
+            pltpu.VMEM((chunks, ny, nx), f32),
+            pltpu.VMEM((chunks, ny, nx), f32),
             pltpu.VMEM((2, chunks, zc, nx), f32),
             pltpu.VMEM((chunks, ny, nx), f32),
-            pltpu.VMEM((chunks, ny + 16, nx), f32),
-            pltpu.VMEM((15, per_dev, nx), f32),
+            pltpu.VMEM((2, chunks, ny + 16, nx), f32),
+            pltpu.VMEM((20, per_dev, nx), f32),
             pltpu.VMEM((per_dev, nx), f32),
             pltpu.VMEM((5, per_dev, nx), f32),
+            pltpu.VMEM((2, 2, chunks, zc, nx), f32),
+            pltpu.VMEM((2, chunks, zc, nx), f32),
+            pltpu.VMEM((2, chunks, zc, nx), f32),
+            pltpu.VMEM((ngy, rup_group, slot_dev, lanes), jnp.bfloat16),
+            pltpu.VMEM((rup_group, max(listed.shape[1], 128)), jnp.int32),
+            pltpu.VMEM((rup_group, listed.shape[1], 128), jnp.int32),
+            pltpu.VMEM((rup_group, lanes, min(ngy * all_rows, 512)), f32),
             pltpu.VMEM((all_rows, per_dev), f32),
             pltpu.VMEM((per_dev, max(all_rows, 128)), f32),
             pltpu.VMEM((all_rows, width), f32),
@@ -845,13 +893,14 @@
             pltpu.VMEM((ngx, STEPS - 1, 1, 128), f32),
             pltpu.VMEM((ngx, 1, 128), f32),
             pltpu.SemaphoreType.DMA((9, chunks)),
-            pltpu.SemaphoreType.DMA((5,)),
+            pltpu.SemaphoreType.DMA((4,)),
             pltpu.SemaphoreType.DMA((8,)),
             pltpu.SemaphoreType.DMA((2, chunks, 8)),
             pltpu.SemaphoreType.DMA((2, 2)),
             pltpu.SemaphoreType.DMA((ngy // 2, 2)),
             pltpu.SemaphoreType.DMA((2,)),
             pltpu.SemaphoreType.DMA((2,)),
+            pltpu.SemaphoreType.DMA((1,)),
         ],
         compiler_params=pltpu.CompilerParams(
             collective_id=0, has_side_effects=True, vmem_limit_bytes=VMEM_LIMIT
@@ -859,7 +908,6 @@
     )(
         *[in_hbm(x) for x in (velocity, pressure, memory, buoyancy, modulus, relax, strength)],
         in_hbm(spectra),
-        in_hbm(patch_cell),
         in_hbm(patch_cell.reshape(1, -1)),
         in_hbm(phase_rows(width // 2)),
         in_hbm(listed),
@@ -872,14 +920,12 @@
     width = spectra.shape[1]
     ngy = lax.axis_size("gy")
     rup_group, slot_dev, variations = weights.shape
-    slot_count = slot_dev * ngy
     share = variations // ngy
-    lanes = max(share, 128)
     f32 = jnp.float32
     any_spec = pl.BlockSpec(memory_space=pl.ANY)
     vmem_spec = pl.BlockSpec(memory_space=pltpu.VMEM)
     return pl.pallas_call(
-        functools.partial(finish_kernel, (nz, slot_count, share)),
+        functools.partial(finish_kernel, nz),
         out_shape=[
             jax.ShapeDtypeStruct(velocity.shape, f32),
             jax.ShapeDtypeStruct(pressure.shape, f32),
@@ -890,13 +936,11 @@
         in_specs=[vmem_spec] * len(state),
         out_specs=[any_spec] * 5,
         scratch_shapes=[
-            pltpu.VMEM((rup_group * slot_count, 128), jnp.int32),
-            pltpu.VMEM((rup_group * slot_count, width), jnp.bfloat16),
-            pltpu.VMEM((rup_group, lanes, width), f32),
+            pltpu.VMEM((rup_group, share, width), f32),
             pltpu.VMEM(state[7].shape, jnp.bfloat16),
-            pltpu.VMEM((8, 128), f32),
+            pltpu.VMEM((8, state[7].shape[0]), f32),
             pltpu.SemaphoreType.DMA((6,)),
-            pltpu.SemaphoreType.DMA((rup_group,)),
+            pltpu.SemaphoreType.DMA((1,)),
         ],
         compiler_params=pltpu.CompilerParams(vmem_limit_bytes=VMEM_LIMIT),
     )(*[pltpu.with_memory_space_constraint(x, pltpu.VMEM) for x in state])

time: 36.8 us -> 38.2 us (1.038)
  Pallas kernels: 36 us -> 37.4 us
    pallas_call x1, Pallas kernels: 32.7 us -> 34.5 us  [advance(): pl.pallas_call(functools.partial(step_kernel, dims), out_shape=[field(nz)...]
    pallas_call x1, Pallas kernels: 3.32 us -> 2.87 us  [finish(): pl.pallas_call(functools.partial(finish_kernel, nz), out_shape=[jax.Shape...]
where the time goes in v4:
time: 38.2 us; the launch traced here: 38.1 us
  Pallas kernels  37.4 us (98%)
  between operations  0.64 us (2%)
    pallas_call x1, Pallas kernels, advance(): pl.pallas_call(functools.partial(step_kernel, dims), out_shape=[field(nz)...  34.5 us
    pallas_call x1, Pallas kernels, finish(): pl.pallas_call(functools.partial(finish_kernel, nz), out_shape=[jax.Shape...  2.87 us

profile of v4, /device:TPU:0, one launch (start us, length us, event | category | flops | bytes accessed | tf_op | source)
XLA Modules:
  0.0 38.1 jit_solution(17922637654248740246)
XLA Ops:
  0.6 34.5 %shard_map.155 = (f32[64,32,128]{2,1,0:T(8,128)S(1)}, f32[64,32,128]{2,1,0:T(8,128)S(1)}, f32[66,32,128]{2,1,0:T(8,128)S(1)}, f32[67,32,128]{2,1,0:T(8,128)S(1)}...) custom-call(f32[3,64,32,128]{3,2,1,0:T(8,128)} %refs_0_.1, ...), custom_call_target="tpu_custom_call" | custom-call | tf_op jit(solution)/shard_map/pallas_call | solution.py:839
  35.2 2.9 %shard_map.156 = (f32[3,64,32,128]{3,2,1,0:T(8,128)}, f32[64,32,128]{2,1,0:T(8,128)}, f32[64,32,128]{2,1,0:T(8,128)}, f32[64,256]{1,0:T(8,128)}, f32[8,64,256]{2,1,0:T(8,128)}) custom-call(f32[64,32,128]{2,1,0:T(8,128)S(1)} %get-tuple-element.16.refs_0_, f32[64,32,128]{2,1,0:T(8,128)S(1)} %get-tuple-element.17.refs_1_, ...), custom_call_target="tpu_custom_call" | custom-call | tf_op jit(solution)/shard_map/pallas_call | solution.py:927

commit v5 on v4

--- a/solution.py
+++ b/solution.py
@@ -43,14 +43,14 @@
     take = lambda count: [refs.pop(0) for _ in range(count)]
     vel_in, p_in, m_in, b_in, mod_in, rel_in, str_in = take(7)
     spectra_in, cell_row_in, phase_in, listed_in, weights = take(5)
-    vx, vy, vz, p, m, spectra_out, mixed, rows_out, heard, heard_last, phase = take(11)
+    vx, vy, vz, p, m, spectra_out, mixed, rows_out, heard, phase = take(10)
     b, mod, rel, stg, vx_old, vy_old, p_old, b_east = take(8)
     ysend, xsend, csend = take(3)
     yrecv, xrecv, crecv = (take(STEPS), take(STEPS), take(STEPS))
     cell_row, listed, index_made, index = take(4)
     vxh, bwh, bxh, hx, hx_old, vyh, vyx, xj, got, shear, factors = take(11)
     hp, hv, hb, weights_got, table, columns, wide = take(7)
-    placing, placed, rows_send, rows_group, told, told_last = take(6)
+    placing, placed, rows_send, rows_group, told = take(5)
     in_sem, small_sem, send_sem, recv_sem, far_sem, block_sem, tell_sem, hear_sem, index_sem = take(9)
 
     gx, gy = (lax.axis_index("gx"), lax.axis_index("gy"))
@@ -208,8 +208,8 @@
 
         def edges(i, totals):
             pt, vt, bt = totals
-            for j in range(BATCH):
-                zl = i * BATCH + j
+            for j in range(8):
+                zl = i * 8 + j
                 z = c * zc + zl
                 ps, vs, ws, bs = (p_old[z + 1], vx_old[z], vy_old[z], b[z])
                 pt, vt, bt = (pack(pt, ps, zl), pack(vt, vs, zl), pack(bt, bs, zl))
@@ -224,7 +224,7 @@
                 ysend[1, c, y_row(0, 3), at, :] = bs[ny - 1 : ny]
             return pt, vt, bt
 
-        totals = lax.fori_loop(0, zc // BATCH, edges, (plane, plane, plane))
+        totals = lax.fori_loop(0, zc // 8, edges, (plane, plane, plane))
         for i, total in enumerate(totals):
             xsend[c, x_row(0, i)] = total
         csend[0, c] = totals[0][0:1]
@@ -295,22 +295,22 @@
         block = block_rows(flip(j), h)
         return carry_over(j, h, block, block, flip(1 if j % 2 else j))
 
-    def tell(k, src, dst, i):
+    def tell(k):
         where = other_device(k)
         return pltpu.make_async_remote_copy(
-            src_ref=src.at[where["gx"]],
-            dst_ref=dst.at[mine],
-            send_sem=tell_sem.at[i],
-            recv_sem=hear_sem.at[i],
+            src_ref=told.at[where["gx"]],
+            dst_ref=heard.at[mine],
+            send_sem=tell_sem.at[0],
+            recv_sem=hear_sem.at[0],
             device_id=where,
             device_id_type=pl.DeviceIdType.MESH,
         )
 
-    def tell_all(src, dst, i):
-        pltpu.make_async_copy(src.at[gx], dst.at[mine], hear_sem.at[i]).start()
+    def tell_all():
+        pltpu.make_async_copy(told.at[gx], heard.at[mine], hear_sem.at[0]).start()
 
         def start(k, carry):
-            tell(k, src, dst, i).start()
+            tell(k).start()
             return carry
 
         lax.fori_loop(1, devices, start, 0)
@@ -389,9 +389,8 @@
             vh, bh = (pltpu.roll(edge(1), 1, 1), pltpu.roll(edge(2), 1, 1))
             bwh[c] = bh
             bxh[c] = joined(2)
-            hx_old[c] = jnp.where(
-                lane4 == 1, pltpu.roll(xrecv[0][1, c, 2], nx - 1, 1), xrecv[0][1, c, 1]
-            )
+            hx_old[0, c] = pltpu.roll(xrecv[0][1, c, 2], nx - 1, 1)
+            hx_old[1, c] = pltpu.roll(xrecv[0][1, c, 1], nx - 1, 1)
             vyh[0, c] = yrecv[0][0, c, 2]
             vyh[1, c] = yrecv[0][1, c, 2]
             for side in range(2):
@@ -416,12 +415,11 @@
     def sweep(r, c):
         last, first = (r == STEPS - 1, r == 0)
         n = r + 1
-
-        def body(i, totals):
-            totals = list(totals)
+        p_from, w_from = (p_old, vy_old) if first else (p, vy)
+
+        def body(i, total):
             base = i * BATCH
             z0 = c * zc + base
-            p_from = p_old if first else p
             ps = [p_from[z0 + 1 + j] for j in range(BATCH + 2)]
             bs = [b[z0 + j] for j in range(BATCH + 1)]
             zs = [vz[z0], vz[z0 + 1]]
@@ -433,17 +431,15 @@
                 zs.append(vz[z0 + j + 2] - bs[j + 1] * (ps[j + 2] - ps[j]))
                 outer.append(pltpu.roll(hx[c], turn, 1))
                 ahead = jnp.where(lane >= nx - 2, outer[j], pltpu.roll(ps[j], nx - 2, 1))
+                shifted, speed = (b_east[z0 + j], vx[z0 + j])
                 if first:
-                    old = pltpu.roll(hx_old[c], turn, 1)
-                    shifted = jnp.where(lane == nx - 1, old, pltpu.roll(bs[j], nx - 1, 1))
+                    edges_in = [pltpu.roll(hx_old[k, c], turn, 1) for k in range(2)]
+                    shifted = jnp.where(lane == nx - 1, edges_in[0], shifted)
                     b_east[z0 + j] = shifted
-                    speed = pltpu.roll(jnp.where(lane == 0, old, vx_old[z0 + j]), nx - 1, 1)
-                else:
-                    shifted, speed = (b_east[z0 + j], vx[z0 + j])
+                    speed = jnp.where(lane == nx - 1, edges_in[1], speed)
                 vs.append(speed - shifted * (ahead - ps[j]))
                 south, north = (yrecv[r][0, c, 1, at, :], yrecv[r][1, c, 0, at, :])
-                side_speed = vy_old[z0 + j] if first else vy[z0 + j]
-                ws.append(side_speed - bs[j] * d_y(ps[j], south, north))
+                ws.append(w_from[z0 + j] - bs[j] * d_y(ps[j], south, north))
             for j in range(BATCH):
                 zl = base + j
                 at = pl.ds(zl, 1)
@@ -465,24 +461,34 @@
                 vy[z0 + j] = ws[j]
                 p[z0 + j + 1] = new_p[j]
                 if not last:
-                    totals[0] = pack(totals[0], new_p[j], zl)
+                    total = pack(total, new_p[j], zl)
                     ysend[0, c, y_row(n, 0), at, :] = new_p[j][0:1]
                     ysend[0, c, y_row(n, 1), at, :] = new_p[j][1:2]
                     ysend[1, c, y_row(n, 0), at, :] = new_p[j][ny - 2 : ny - 1]
                     ysend[1, c, y_row(n, 1), at, :] = new_p[j][ny - 1 : ny]
-                if first:
-                    totals[1] = pack(totals[1], vy_old[z0 + j], zl)
-                    ysend[0, c, y_row(n, 2), at, :] = vx_old[z0 + j, 0:1, :]
-                    ysend[1, c, y_row(n, 2), at, :] = vx_old[z0 + j, ny - 1 : ny, :]
-            return tuple(totals)
-
-        count = 0 if last else X_PACKS[n]
-        totals = lax.fori_loop(0, zc // BATCH, body, (plane,) * count)
-        for i, total in enumerate(totals):
-            xsend[c, x_row(n, i)] = total
+            return total
+
+        total = lax.fori_loop(0, zc // BATCH, body, plane)
         if not last:
-            csend[0, n * chunks + c] = totals[0][0:1]
-            csend[1, n * chunks + c] = totals[0][ny - 1 : ny]
+            xsend[c, x_row(n, 0)] = total
+            csend[0, n * chunks + c] = total[0:1]
+            csend[1, n * chunks + c] = total[ny - 1 : ny]
+
+    def shift(c):
+        def body(i, total):
+            for j in range(8):
+                zl = i * 8 + j
+                z = c * zc + zl
+                at = pl.ds(zl, 1)
+                old = vx_old[z]
+                vx[z] = pltpu.roll(old, nx - 1, 1)
+                b_east[z] = pltpu.roll(b[z], nx - 1, 1)
+                total = pack(total, vy_old[z], zl)
+                ysend[0, c, y_row(1, 2), at, :] = old[0:1]
+                ysend[1, c, y_row(1, 2), at, :] = old[ny - 1 : ny]
+            return total
+
+        xsend[c, x_row(1, 1)] = lax.fori_loop(0, zc // 8, body, plane)
 
     told_lane = lax.broadcasted_iota(jnp.int32, (1, 128), 1)
     in_place = quotient(told_lane, group_rows) == remainder(mine, 128 // group_rows)
@@ -555,10 +561,7 @@
             piece = line[:, tile : tile + 128]
             spread = pltpu.roll(piece, remainder(mine * group_rows + (128 - begin % 128), 128), 1)
             spread = jnp.where(in_place, spread, 0.0)
-            if n < STEPS:
-                told[k, n - 1] = spread
-            else:
-                told_last[k] = spread
+            told[k, n - 1] = spread
         spectra_out[...] = spectra_out[...] + value * phase[n - 1 : n, :]
 
     def marks():
@@ -605,6 +608,8 @@
     make_index()
     index_copy = pltpu.make_async_copy(index_made, index, index_sem.at[0])
     index_copy.start()
+    for c in range(chunks):
+        shift(c)
     for c in range(chunks):
         for i in range(4, 9):
             load(i, c).wait()
@@ -667,7 +672,6 @@
 
     def work_after(r):
         if r == 0:
-            send_rows()
             index_copy.wait()
             gather(
                 *own_rows(B_OWN, b, 0),
@@ -695,10 +699,10 @@
     def last_shear():
         gather(*halo_rows(P_HALO, STEPS - 1))
         next_shear(STEPS)
-        tell_all(told_last, heard_last, 1)
+        tell_all()
 
     gaps = [(r, c) for r in range(STEPS - 1) for c in range(chunks)][chunks:]
-    jobs = {gap: [] for gap in gaps + [(STEPS - 1, 0), None]}
+    jobs = {gap: [] for gap in gaps + [None]}
     order = list(jobs)
     pieces = [(j, h) for j in range(2, ngy, 2) for h in range(2)]
 
@@ -718,7 +722,6 @@
         pass_on(j, h).start()
 
     jobs[order[0]].append(enter_rows)
-    jobs[STEPS - 1, 0].append(lambda: tell_all(told, heard, 0))
     for i, (j, h) in enumerate(pieces):
         place = i * len(gaps) // len(pieces)
         jobs[order[place]].append(functools.partial(leave, j, h))
@@ -728,6 +731,7 @@
         place = (k - 1) * len(gaps) // (ngy - 1)
         jobs[order[place]].append(lambda k=k: weights_to(k).start())
 
+    send_rows()
     for r in range(STEPS):
         above = p_old if r == 0 else p
         vz[1] = vz[1] - b[0] * (above[2] - above[0])
@@ -758,15 +762,14 @@
     settle(rows_group.at[pl.ds(0, (ngx - 1) * group_rows)], far_sem.at[1, 0])
     settle(rows_out.at[pl.ds(0, (ngy - 1) * all_rows)], block_sem.at[0, 1])
     settle(rows_out.at[pl.ds(0, ngy // 2 * all_rows)], block_sem.at[0, 0])
-    for i, ref in enumerate([heard, heard_last]):
-        settle(ref.at[pl.ds(1, devices - 1)], tell_sem.at[i])
-        settle(ref, hear_sem.at[i])
+    settle(heard.at[pl.ds(1, devices - 1)], tell_sem.at[0])
+    settle(heard, hear_sem.at[0])
 
 
 def finish_kernel(nz, *refs):
     refs = list(refs)
     take = lambda count: [refs.pop(0) for _ in range(count)]
-    vx, vy, vz, p, m, spectra, mixed, rows, heard, heard_last, phase = take(11)
+    vx, vy, vz, p, m, spectra, mixed, rows, heard, phase = take(10)
     vel_out, p_out, m_out, spectra_out, slip_out = take(5)
     slip, exact, lines_in, out_sem, slip_sem = take(5)
     inner = pl.ds(1, nz)
@@ -790,8 +793,7 @@
     for t in range(count // per_tile):
         at, of = (pl.ds(t * 128, 128), pl.ds(t * per_tile, per_tile))
         for n in range(STEPS):
-            told = heard[of, n] if n < STEPS - 1 else heard_last[of]
-            lines_in[n : n + 1, at] = jnp.sum(told, axis=0)
+            lines_in[n : n + 1, at] = jnp.sum(heard[of, n], axis=0)
     for t in range(count // per_tile):
         at = pl.ds(t * 128, 128)
         change = lax.dot_general(
@@ -847,12 +849,11 @@
             pltpu.VMEM(spectra.shape, f32),
             pltpu.VMEM((rup_group * (variations // ngy), ngy * all_rows), jnp.bfloat16),
             pltpu.VMEM((ngy * all_rows, width), f32),
-            pltpu.VMEM((ngx * ngy, STEPS - 1, 1, 128), f32),
-            pltpu.VMEM((ngx * ngy, 1, 128), f32),
+            pltpu.VMEM((ngx * ngy, STEPS, 1, 128), f32),
             pltpu.VMEM((8, width), f32),
         ],
         in_specs=[any_spec] * 12,
-        out_specs=[vmem_spec] * 11,
+        out_specs=[vmem_spec] * 10,
         scratch_shapes=[field(nz + 1), field(nz), field(nz), field(nz)]
         + [field(nz), field(nz), field(nz + 3), field(nz)]
         + [
@@ -872,7 +873,7 @@
             pltpu.VMEM((chunks, ny, nx), f32),
             pltpu.VMEM((chunks, ny, nx), f32),
             pltpu.VMEM((chunks, ny, nx), f32),
-            pltpu.VMEM((chunks, ny, nx), f32),
+            pltpu.VMEM((2, chunks, ny, nx), f32),
             pltpu.VMEM((2, chunks, zc, nx), f32),
             pltpu.VMEM((chunks, ny, nx), f32),
             pltpu.VMEM((2, chunks, ny + 16, nx), f32),
@@ -890,16 +891,15 @@
             pltpu.VMEM((per_dev, max(all_rows, 128)), f32),
             pltpu.VMEM((all_rows, width), f32),
             pltpu.VMEM((all_rows, width), f32),
-            pltpu.VMEM((ngx, STEPS - 1, 1, 128), f32),
-            pltpu.VMEM((ngx, 1, 128), f32),
+            pltpu.VMEM((ngx, STEPS, 1, 128), f32),
             pltpu.SemaphoreType.DMA((9, chunks)),
             pltpu.SemaphoreType.DMA((4,)),
             pltpu.SemaphoreType.DMA((8,)),
             pltpu.SemaphoreType.DMA((2, chunks, 8)),
             pltpu.SemaphoreType.DMA((2, 2)),
             pltpu.SemaphoreType.DMA((ngy // 2, 2)),
-            pltpu.SemaphoreType.DMA((2,)),
-            pltpu.SemaphoreType.DMA((2,)),
+            pltpu.SemaphoreType.DMA((1,)),
+            pltpu.SemaphoreType.DMA((1,)),
             pltpu.SemaphoreType.DMA((1,)),
         ],
         compiler_params=pltpu.CompilerParams(

time: 38.2 us -> 35.7 us (0.935)
  Pallas kernels: 37.4 us -> 34.9 us
    pallas_call x1, Pallas kernels: 34.5 us -> 32 us  [advance(): pl.pallas_call(functools.partial(step_kernel, dims), out_shape=[field(nz)...]
where the time goes in v5:
time: 35.7 us; the launch traced here: 35.5 us
  Pallas kernels  34.9 us (98%)
  between operations  0.64 us (2%)
    pallas_call x1, Pallas kernels, advance(): pl.pallas_call(functools.partial(step_kernel, dims), out_shape=[field(nz)...  32 us
    pallas_call x1, Pallas kernels, finish(): pl.pallas_call(functools.partial(finish_kernel, nz), out_shape=[jax.Shape...  2.87 us

profile of v5, /device:TPU:0, one launch (start us, length us, event | category | flops | bytes accessed | tf_op | source)
XLA Modules:
  0.0 35.5 jit_solution(14730015830186968148)
XLA Ops:
  0.6 32.0 %shard_map.155 = (f32[64,32,128]{2,1,0:T(8,128)S(1)}, f32[64,32,128]{2,1,0:T(8,128)S(1)}, f32[66,32,128]{2,1,0:T(8,128)S(1)}, f32[67,32,128]{2,1,0:T(8,128)S(1)}...) custom-call(f32[3,64,32,128]{3,2,1,0:T(8,128)} %refs_0_.1, ...), custom_call_target="tpu_custom_call" | custom-call | tf_op jit(solution)/shard_map/pallas_call | solution.py:841
  32.6 2.9 %shard_map.156 = (f32[3,64,32,128]{3,2,1,0:T(8,128)}, f32[64,32,128]{2,1,0:T(8,128)}, f32[64,32,128]{2,1,0:T(8,128)}, f32[64,256]{1,0:T(8,128)}, f32[8,64,256]{2,1,0:T(8,128)}) custom-call(f32[64,32,128]{2,1,0:T(8,128)S(1)} %get-tuple-element.15.refs_0_, f32[64,32,128]{2,1,0:T(8,128)S(1)} %get-tuple-element.16.refs_1_, ...), custom_call_target="tpu_custom_call" | custom-call | tf_op jit(solution)/shard_map/pallas_call | solution.py:927

commit v6 on v5

--- a/solution.py
+++ b/solution.py
@@ -51,7 +51,8 @@
     vxh, bwh, bxh, hx, hx_old, vyh, vyx, xj, got, shear, factors = take(11)
     hp, hv, hb, weights_got, table, columns, wide = take(7)
     placing, placed, rows_send, rows_group, told = take(5)
-    in_sem, small_sem, send_sem, recv_sem, far_sem, block_sem, tell_sem, hear_sem, index_sem = take(9)
+    in_sem, small_sem, send_sem, recv_sem, corner_sem = take(5)
+    far_sem, block_sem, tell_sem, hear_sem, index_sem = take(5)
 
     gx, gy = (lax.axis_index("gx"), lax.axis_index("gy"))
     has = [gy > 0, gy < ngy - 1, gx > 0, gx < ngx - 1]
@@ -59,9 +60,10 @@
     peer = [{"gy": gy - 1}, {"gy": gy + 1}, {"gx": gx - 1}, {"gx": gx + 1}]
     peer = peer + [{**peer[k // 2], **peer[2 + k % 2]} for k in range(4)]
 
-    def load(i, c):
-        at = pl.ds(c * zc, zc)
-        moved = pl.ds(c * zc + 1, zc)
+    def load(i, h):
+        count = nz // 2 if i < 4 else nz
+        at = pl.ds(h * count, count)
+        moved = pl.ds(h * count + 1, count)
         src, dst = [
             (p_in.at[at], p_old.at[moved]),
             (b_in.at[at], b.at[at]),
@@ -73,7 +75,7 @@
             (str_in.at[at], stg.at[at]),
             (mod_in.at[at], mod.at[at]),
         ][i]
-        return pltpu.make_async_copy(src, dst, in_sem.at[i, c])
+        return pltpu.make_async_copy(src, dst, in_sem.at[i + 9 * h])
 
     y_row = lambda r, k: sum(Y_ROWS[:r]) + k
     x_row = lambda r, k: sum(X_PACKS[:r]) + k
@@ -91,12 +93,11 @@
     ]
     for small in smalls:
         small.start()
-    for c in range(chunks):
+    for h in range(2):
         for i in range(4):
-            load(i, c).start()
-    for c in range(chunks):
-        for i in range(4, 9):
-            load(i, c).start()
+            load(i, h).start()
+    for i in range(4, 9):
+        load(i, 0).start()
     devices = ngx * ngy
     me = gx * ngy + gy
     mine = gy * ngx + gx
@@ -145,8 +146,7 @@
                 elif side < 4:
                     xrecv[r][side - 2] = jnp.zeros(xrecv[r].shape[1:], jnp.float32)
                 else:
-                    for c in range(chunks):
-                        crecv[r][c, side - 4] = jnp.zeros((1, nx), jnp.float32)
+                    crecv[r][side - 4] = jnp.zeros(crecv[r].shape[1:], jnp.float32)
 
     def ends(r, c, side, coming):
         k = side % 4
@@ -162,31 +162,38 @@
             arrives = 2 + there
         else:
             there = k if coming else 3 - k
-            src = csend.at[k // 2, r * chunks + c]
-            dst = crecv[r].at[c, there]
+            src, dst = (csend.at[k // 2, r], crecv[r].at[there])
             arrives = 4 + there
         return pltpu.make_async_remote_copy(
             src_ref=src,
             dst_ref=dst,
             send_sem=send_sem.at[side],
-            recv_sem=recv_sem.at[r % 2, c, arrives],
+            recv_sem=recv_sem.at[r % 2, c, arrives] if side < 4 else corner_sem.at[r, there],
             device_id=peer[side],
             device_id_type=pl.DeviceIdType.MESH,
         )
 
     def send(r, c):
-        for side in range(8):
+        for side in range(8 if c == chunks - 1 else 4):
 
             @pl.when(has[side])
             def _():
                 ends(r, c, side, False).start()
 
-    def receive(r, c):
-        for side in range(8):
+    def receive(r, c, sides=range(4)):
+        for side in sides:
 
             @pl.when(has[side])
             def _():
                 ends(r, c, side, True).wait_recv()
+
+    def corners(r):
+        receive(r, chunks - 1, range(4, 8))
+        for c in range(chunks):
+            south = jnp.where(west_half, crecv[r][0, c], crecv[r][1, c])
+            north = jnp.where(west_half, crecv[r][2, c], crecv[r][3, c])
+            xj[r % 2, c, 7:8, :] = south
+            xj[r % 2, c, 8 + ny : 9 + ny, :] = north
 
     lane = lax.broadcasted_iota(jnp.int32, (ny, nx), 1)
     row = lax.broadcasted_iota(jnp.int32, (ny, nx), 0)
@@ -203,8 +210,9 @@
         return after - before
 
     for c in range(chunks):
-        for i in range(4):
-            load(i, c).wait()
+        if c % (chunks // 2) == 0:
+            for i in range(4):
+                load(i, c // (chunks // 2)).wait()
 
         def edges(i, totals):
             pt, vt, bt = totals
@@ -227,8 +235,8 @@
         totals = lax.fori_loop(0, zc // 8, edges, (plane, plane, plane))
         for i, total in enumerate(totals):
             xsend[c, x_row(0, i)] = total
-        csend[0, c] = totals[0][0:1]
-        csend[1, c] = totals[0][ny - 1 : ny]
+        csend[0, 0, c] = totals[0][0:1]
+        csend[1, 0, c] = totals[0][ny - 1 : ny]
         if c == 0:
             pl.semaphore_wait(barrier, len(peers))
         send(0, c)
@@ -403,9 +411,7 @@
                     hv[side, c] = yrecv[1][side, c, 2]
         for side in range(2):
             hp[r % 2, side, c] = yrecv[r][side, c, 1 - side]
-        xj[r % 2, c, 7:8, :] = jnp.where(west_half, crecv[r][c, 0], crecv[r][c, 1])
         xj[r % 2, c, 8 : 8 + ny, :] = joined(0)
-        xj[r % 2, c, 8 + ny : 9 + ny, :] = jnp.where(west_half, crecv[r][c, 2], crecv[r][c, 3])
         vh = vh - bh * (own - pltpu.roll(west, 2, 1))
         vxh[c] = vh
         hx[c] = jnp.where(lane4 < 2, pltpu.roll(east, nx - 2, 1), vh)
@@ -471,8 +477,8 @@
         total = lax.fori_loop(0, zc // BATCH, body, plane)
         if not last:
             xsend[c, x_row(n, 0)] = total
-            csend[0, n * chunks + c] = total[0:1]
-            csend[1, n * chunks + c] = total[ny - 1 : ny]
+            csend[0, n, c] = total[0:1]
+            csend[1, n, c] = total[ny - 1 : ny]
 
     def shift(c):
         def body(i, total):
@@ -608,11 +614,10 @@
     make_index()
     index_copy = pltpu.make_async_copy(index_made, index, index_sem.at[0])
     index_copy.start()
-    for c in range(chunks):
+    for c in range(chunks // 2):
         shift(c)
-    for c in range(chunks):
-        for i in range(4, 9):
-            load(i, c).wait()
+    for i in range(4, 9):
+        load(i, 0).wait()
 
     def send_rows():
         fill_placing()
@@ -671,6 +676,7 @@
                     blend(r, k)
 
     def work_after(r):
+        corners(r)
         if r == 0:
             index_copy.wait()
             gather(
@@ -697,11 +703,12 @@
             gather(*own_rows(P_OWN, p, ny))
 
     def last_shear():
+        corners(STEPS - 1)
         gather(*halo_rows(P_HALO, STEPS - 1))
         next_shear(STEPS)
         tell_all()
 
-    gaps = [(r, c) for r in range(STEPS - 1) for c in range(chunks)][chunks:]
+    gaps = [(r, c) for r in range(STEPS - 1) for c in range(chunks)][chunks + chunks // 2 :]
     jobs = {gap: [] for gap in gaps + [None]}
     order = list(jobs)
     pieces = [(j, h) for j in range(2, ngy, 2) for h in range(2)]
@@ -721,23 +728,24 @@
         block_from(j, h).wait_recv()
         pass_on(j, h).start()
 
+    jobs[0, 0] = [send_rows]
     jobs[order[0]].append(enter_rows)
     for i, (j, h) in enumerate(pieces):
         place = i * len(gaps) // len(pieces)
         jobs[order[place]].append(functools.partial(leave, j, h))
-        after = order[min(place + 2, len(order) - 1)]
+        after = order[min(place + 5, len(order) - 1)]
         jobs[after].append(functools.partial(forward, j, h))
-    for k in range(1, ngy):
-        place = (k - 1) * len(gaps) // (ngy - 1)
-        jobs[order[place]].append(lambda k=k: weights_to(k).start())
-
-    send_rows()
     for r in range(STEPS):
         above = p_old if r == 0 else p
         vz[1] = vz[1] - b[0] * (above[2] - above[0])
         for c in range(chunks):
+            if r == STEPS - 1 and c == 0:
+                for k in range(1, ngy):
+                    weights_to(k).start()
             receive(r, c)
             halos(r, c)
+            if r == 0 and c >= chunks // 2:
+                shift(c)
             if r == STEPS - 1 and c == chunks - 1:
                 last_shear()
             sweep(r, c)
@@ -745,7 +753,8 @@
                 send(r + 1, c)
             for job in jobs.get((r, c), []):
                 job()
-        work_after(r)
+        if r < STEPS - 1:
+            work_after(r)
     for job in jobs[None]:
         job()
     fill_table()
@@ -826,7 +835,7 @@
 ):
     nz, ny, nx = pressure.shape
     per_dev, width = spectra.shape
-    zc = nx // 4
+    zc = nx // 8
     chunks = nz // zc
     ngx, ngy = (lax.axis_size("gx"), lax.axis_size("gy"))
     dims = (nz, ny, nx, chunks, zc, per_dev, ngx, ngy)
@@ -859,11 +868,11 @@
         + [
             pltpu.VMEM((2, chunks, sum(Y_ROWS), zc, nx), f32),
             pltpu.VMEM((chunks, sum(X_PACKS), ny, nx), f32),
-            pltpu.VMEM((2, STEPS * chunks, 1, nx), f32),
+            pltpu.VMEM((2, STEPS, chunks, 1, nx), f32),
         ]
         + [pltpu.VMEM((2, chunks, Y_ROWS[r], zc, nx), f32) for r in rounds]
         + [pltpu.VMEM((2, chunks, X_PACKS[r], ny, nx), f32) for r in rounds]
-        + [pltpu.VMEM((chunks, 4, 1, nx), f32) for r in rounds]
+        + [pltpu.VMEM((4, chunks, 1, nx), f32) for r in rounds]
         + [
             pltpu.VMEM((1, per_dev), jnp.int32),
             pltpu.VMEM(listed.shape, jnp.int32),
@@ -892,10 +901,11 @@
             pltpu.VMEM((all_rows, width), f32),
             pltpu.VMEM((all_rows, width), f32),
             pltpu.VMEM((ngx, STEPS, 1, 128), f32),
-            pltpu.SemaphoreType.DMA((9, chunks)),
+            pltpu.SemaphoreType.DMA((13,)),
             pltpu.SemaphoreType.DMA((4,)),
             pltpu.SemaphoreType.DMA((8,)),
-            pltpu.SemaphoreType.DMA((2, chunks, 8)),
+            pltpu.SemaphoreType.DMA((2, chunks, 4)),
+            pltpu.SemaphoreType.DMA((STEPS, 4)),
             pltpu.SemaphoreType.DMA((2, 2)),
             pltpu.SemaphoreType.DMA((ngy // 2, 2)),
             pltpu.SemaphoreType.DMA((1,)),

time: 35.7 us -> 34.3 us (0.961)
  Pallas kernels: 34.9 us -> 33.5 us
    pallas_call x1, Pallas kernels: 32 us -> 30.7 us  [advance(): pl.pallas_call(functools.partial(step_kernel, dims), out_shape=[field(nz)...]
where the time goes in v6:
time: 34.3 us; the launch traced here: 34.2 us
  Pallas kernels  33.5 us (98%)
  between operations  0.64 us (2%)
    pallas_call x1, Pallas kernels, advance(): pl.pallas_call(functools.partial(step_kernel, dims), out_shape=[field(nz)...  30.7 us
    pallas_call x1, Pallas kernels, finish(): pl.pallas_call(functools.partial(finish_kernel, nz), out_shape=[jax.Shape...  2.87 us

profile of v6, /device:TPU:0, one launch (start us, length us, event | category | flops | bytes accessed | tf_op | source)
XLA Modules:
  0.0 34.2 jit_solution(16978932918047259380)
XLA Ops:
  0.6 30.7 %shard_map.155 = (f32[64,32,128]{2,1,0:T(8,128)S(1)}, f32[64,32,128]{2,1,0:T(8,128)S(1)}, f32[66,32,128]{2,1,0:T(8,128)S(1)}, f32[67,32,128]{2,1,0:T(8,128)S(1)}...) custom-call(f32[3,64,32,128]{3,2,1,0:T(8,128)} %refs_0_.1, ...), custom_call_target="tpu_custom_call" | custom-call | tf_op jit(solution)/shard_map/pallas_call | solution.py:850
  31.3 2.9 %shard_map.156 = (f32[3,64,32,128]{3,2,1,0:T(8,128)}, f32[64,32,128]{2,1,0:T(8,128)}, f32[64,32,128]{2,1,0:T(8,128)}, f32[64,256]{1,0:T(8,128)}, f32[8,64,256]{2,1,0:T(8,128)}) custom-call(f32[64,32,128]{2,1,0:T(8,128)S(1)} %get-tuple-element.15.refs_0_, f32[64,32,128]{2,1,0:T(8,128)S(1)} %get-tuple-element.16.refs_1_, ...), custom_call_target="tpu_custom_call" | custom-call | tf_op jit(solution)/shard_map/pallas_call | solution.py:937

commit v7 on v6

--- a/solution.py
+++ b/solution.py
@@ -61,9 +61,9 @@
     peer = peer + [{**peer[k // 2], **peer[2 + k % 2]} for k in range(4)]
 
     def load(i, h):
-        count = nz // 2 if i < 4 else nz
-        at = pl.ds(h * count, count)
-        moved = pl.ds(h * count + 1, count)
+        cuts = [0, zc, 2 * zc, nz] if i < 4 else [0, nz // 2, nz]
+        at = pl.ds(cuts[h], cuts[h + 1] - cuts[h])
+        moved = pl.ds(cuts[h] + 1, cuts[h + 1] - cuts[h])
         src, dst = [
             (p_in.at[at], p_old.at[moved]),
             (b_in.at[at], b.at[at]),
@@ -75,7 +75,7 @@
             (str_in.at[at], stg.at[at]),
             (mod_in.at[at], mod.at[at]),
         ][i]
-        return pltpu.make_async_copy(src, dst, in_sem.at[i + 9 * h])
+        return pltpu.make_async_copy(src, dst, in_sem.at[i + 9 * h if h < 2 else 18 + i])
 
     y_row = lambda r, k: sum(Y_ROWS[:r]) + k
     x_row = lambda r, k: sum(X_PACKS[:r]) + k
@@ -93,18 +93,15 @@
     ]
     for small in smalls:
         small.start()
-    for h in range(2):
+    for h in range(3):
         for i in range(4):
             load(i, h).start()
-    for i in range(4, 9):
-        load(i, 0).start()
+    for h in range(2):
+        for i in range(4, 9):
+            load(i, h).start()
     devices = ngx * ngy
     me = gx * ngy + gy
     mine = gy * ngx + gx
-
-    def other_device(k):
-        other = lax.rem(me + k, devices)
-        return {"gx": lax.div(other, ngy), "gy": lax.rem(other, ngy)}
 
     def flip(j):
         index = gy
@@ -210,9 +207,9 @@
         return after - before
 
     for c in range(chunks):
-        if c % (chunks // 2) == 0:
+        if c < 3:
             for i in range(4):
-                load(i, c // (chunks // 2)).wait()
+                load(i, c).wait()
 
         def edges(i, totals):
             pt, vt, bt = totals
@@ -303,25 +300,28 @@
         block = block_rows(flip(j), h)
         return carry_over(j, h, block, block, flip(1 if j % 2 else j))
 
-    def tell(k):
-        where = other_device(k)
-        return pltpu.make_async_remote_copy(
-            src_ref=told.at[where["gx"]],
-            dst_ref=heard.at[mine],
-            send_sem=tell_sem.at[0],
-            recv_sem=hear_sem.at[0],
-            device_id=where,
-            device_id_type=pl.DeviceIdType.MESH,
-        )
-
     def tell_all():
         pltpu.make_async_copy(told.at[gx], heard.at[mine], hear_sem.at[0]).start()
-
-        def start(k, carry):
-            tell(k).start()
-            return carry
-
-        lax.fori_loop(1, devices, start, 0)
+        flips = [flip(j) for j in range(ngy)]
+
+        def tell(x, y):
+            pltpu.make_async_remote_copy(
+                src_ref=told.at[x],
+                dst_ref=heard.at[mine],
+                send_sem=tell_sem.at[0],
+                recv_sem=hear_sem.at[0],
+                device_id={"gx": x, "gy": y},
+                device_id_type=pl.DeviceIdType.MESH,
+            ).start()
+
+        for i in range(ngx):
+            x = jnp.where(gx < ngx // 2, ngx - 1 - i, i)
+            for j in range(ngy - 1, 0, -1):
+                tell(x, flips[j])
+
+            @pl.when(x != gx)
+            def _():
+                tell(x, gy)
 
     own_weights = pltpu.make_async_copy(weight_block(gy), weights_got.at[gy], far_sem.at[0, 1])
 
@@ -474,7 +474,9 @@
                     ysend[1, c, y_row(n, 1), at, :] = new_p[j][ny - 1 : ny]
             return total
 
-        total = lax.fori_loop(0, zc // BATCH, body, plane)
+        total = plane
+        for i in range(zc // BATCH):
+            total = body(i, total)
         if not last:
             xsend[c, x_row(n, 0)] = total
             csend[0, n, c] = total[0:1]
@@ -614,7 +616,7 @@
     make_index()
     index_copy = pltpu.make_async_copy(index_made, index, index_sem.at[0])
     index_copy.start()
-    for c in range(chunks // 2):
+    for c in range(2):
         shift(c)
     for i in range(4, 9):
         load(i, 0).wait()
@@ -708,7 +710,7 @@
         next_shear(STEPS)
         tell_all()
 
-    gaps = [(r, c) for r in range(STEPS - 1) for c in range(chunks)][chunks + chunks // 2 :]
+    gaps = [(r, c) for r in range(STEPS - 1) for c in range(chunks)][chunks + 1 :]
     jobs = {gap: [] for gap in gaps + [None]}
     order = list(jobs)
     pieces = [(j, h) for j in range(2, ngy, 2) for h in range(2)]
@@ -728,13 +730,13 @@
         block_from(j, h).wait_recv()
         pass_on(j, h).start()
 
-    jobs[0, 0] = [send_rows]
     jobs[order[0]].append(enter_rows)
     for i, (j, h) in enumerate(pieces):
         place = i * len(gaps) // len(pieces)
         jobs[order[place]].append(functools.partial(leave, j, h))
         after = order[min(place + 5, len(order) - 1)]
         jobs[after].append(functools.partial(forward, j, h))
+    send_rows()
     for r in range(STEPS):
         above = p_old if r == 0 else p
         vz[1] = vz[1] - b[0] * (above[2] - above[0])
@@ -744,8 +746,11 @@
                     weights_to(k).start()
             receive(r, c)
             halos(r, c)
-            if r == 0 and c >= chunks // 2:
+            if r == 0 and c >= 2:
                 shift(c)
+            if r == 0 and c == 1:
+                for i in range(4, 9):
+                    load(i, 1).wait()
             if r == STEPS - 1 and c == chunks - 1:
                 last_shear()
             sweep(r, c)
@@ -901,7 +906,7 @@
             pltpu.VMEM((all_rows, width), f32),
             pltpu.VMEM((all_rows, width), f32),
             pltpu.VMEM((ngx, STEPS, 1, 128), f32),
-            pltpu.SemaphoreType.DMA((13,)),
+            pltpu.SemaphoreType.DMA((22,)),
             pltpu.SemaphoreType.DMA((4,)),
             pltpu.SemaphoreType.DMA((8,)),
             pltpu.SemaphoreType.DMA((2, chunks, 4)),

time: 34.3 us -> 33.4 us (0.974)
  Pallas kernels: 33.5 us -> 32.6 us
    pallas_call x1, Pallas kernels: 30.7 us -> 29.8 us  [advance(): pl.pallas_call(functools.partial(step_kernel, dims), out_shape=[field(nz)...]
where the time goes in v7:
time: 33.4 us; the launch traced here: 33.3 us
  Pallas kernels  32.6 us (98%)
  between operations  0.64 us (2%)
    pallas_call x1, Pallas kernels, advance(): pl.pallas_call(functools.partial(step_kernel, dims), out_shape=[field(nz)...  29.8 us
    pallas_call x1, Pallas kernels, finish(): pl.pallas_call(functools.partial(finish_kernel, nz), out_shape=[jax.Shape...  2.87 us

profile of v7, /device:TPU:0, one launch (start us, length us, event | category | flops | bytes accessed | tf_op | source)
XLA Modules:
  0.0 33.3 jit_solution(15171570946161271125)
XLA Ops:
  0.6 29.8 %shard_map.155 = (f32[64,32,128]{2,1,0:T(8,128)S(1)}, f32[64,32,128]{2,1,0:T(8,128)S(1)}, f32[66,32,128]{2,1,0:T(8,128)S(1)}, f32[67,32,128]{2,1,0:T(8,128)S(1)}...) custom-call(f32[3,64,32,128]{3,2,1,0:T(8,128)} %refs_0_.1, ...), custom_call_target="tpu_custom_call" | custom-call | tf_op jit(solution)/shard_map/pallas_call | solution.py:855
  30.4 2.9 %shard_map.156 = (f32[3,64,32,128]{3,2,1,0:T(8,128)}, f32[64,32,128]{2,1,0:T(8,128)}, f32[64,32,128]{2,1,0:T(8,128)}, f32[64,256]{1,0:T(8,128)}, f32[8,64,256]{2,1,0:T(8,128)}) custom-call(f32[64,32,128]{2,1,0:T(8,128)S(1)} %get-tuple-element.15.refs_0_, f32[64,32,128]{2,1,0:T(8,128)S(1)} %get-tuple-element.16.refs_1_, ...), custom_call_target="tpu_custom_call" | custom-call | tf_op jit(solution)/shard_map/pallas_call | solution.py:942

commit v8 on v7

--- a/solution.py
+++ b/solution.py
@@ -22,7 +22,7 @@
 
 
 Y_ROWS = [4, 3] + [2] * (STEPS - 2)
-X_PACKS = [3, 2] + [1] * (STEPS - 2)
+X_PACKS = [2] + [1] * (STEPS - 1)
 
 
 def quotient(value, size):
@@ -49,7 +49,7 @@
     yrecv, xrecv, crecv = (take(STEPS), take(STEPS), take(STEPS))
     cell_row, listed, index_made, index = take(4)
     vxh, bwh, bxh, hx, hx_old, vyh, vyx, xj, got, shear, factors = take(11)
-    hp, hv, hb, weights_got, table, columns, wide = take(7)
+    hp, hv, hb, vy_pack, weights_got, table, columns, wide = take(8)
     placing, placed, rows_send, rows_group, told = take(5)
     in_sem, small_sem, send_sem, recv_sem, corner_sem = take(5)
     far_sem, block_sem, tell_sem, hear_sem, index_sem = take(5)
@@ -212,12 +212,12 @@
                 load(i, c).wait()
 
         def edges(i, totals):
-            pt, vt, bt = totals
+            pt, bt = totals
             for j in range(8):
                 zl = i * 8 + j
                 z = c * zc + zl
                 ps, vs, ws, bs = (p_old[z + 1], vx_old[z], vy_old[z], b[z])
-                pt, vt, bt = (pack(pt, ps, zl), pack(vt, vs, zl), pack(bt, bs, zl))
+                pt, bt = (pack(pack(pt, ps, zl), vs, zl + zc), pack(bt, bs, zl))
                 at = pl.ds(zl, 1)
                 ysend[0, c, y_row(0, 0), at, :] = ps[0:1]
                 ysend[0, c, y_row(0, 1), at, :] = ps[1:2]
@@ -227,9 +227,9 @@
                 ysend[1, c, y_row(0, 1), at, :] = ps[ny - 1 : ny]
                 ysend[1, c, y_row(0, 2), at, :] = ws[ny - 1 : ny]
                 ysend[1, c, y_row(0, 3), at, :] = bs[ny - 1 : ny]
-            return pt, vt, bt
-
-        totals = lax.fori_loop(0, zc // 8, edges, (plane, plane, plane))
+            return pt, bt
+
+        totals = lax.fori_loop(0, zc // 8, edges, (plane, plane))
         for i, total in enumerate(totals):
             xsend[c, x_row(0, i)] = total
         csend[0, 0, c] = totals[0][0:1]
@@ -394,11 +394,11 @@
             def edge(i):
                 return jnp.where(lane4 == 1, xrecv[0][0, c, i], xsend[c, x_row(0, i)])
 
-            vh, bh = (pltpu.roll(edge(1), 1, 1), pltpu.roll(edge(2), 1, 1))
+            vh, bh = (pltpu.roll(edge(0), 4 * zc + 1, 1), pltpu.roll(edge(1), 1, 1))
             bwh[c] = bh
-            bxh[c] = joined(2)
-            hx_old[0, c] = pltpu.roll(xrecv[0][1, c, 2], nx - 1, 1)
-            hx_old[1, c] = pltpu.roll(xrecv[0][1, c, 1], nx - 1, 1)
+            bxh[c] = joined(1)
+            hx_old[0, c] = pltpu.roll(xrecv[0][1, c, 1], nx - 1, 1)
+            hx_old[1, c] = pltpu.roll(xrecv[0][1, c, 0], nx - 1 - 4 * zc, 1)
             vyh[0, c] = yrecv[0][0, c, 2]
             vyh[1, c] = yrecv[0][1, c, 2]
             for side in range(2):
@@ -406,7 +406,7 @@
         else:
             vh, bh = (vxh[c], bwh[c])
             if r == 1:
-                vyx[c] = joined(1)
+                vyx[c] = pltpu.roll(joined(0), nx - 4 * zc, 1)
                 for side in range(2):
                     hv[side, c] = yrecv[1][side, c, 2]
         for side in range(2):
@@ -474,7 +474,7 @@
                     ysend[1, c, y_row(n, 1), at, :] = new_p[j][ny - 1 : ny]
             return total
 
-        total = plane
+        total = vy_pack[c] if first else plane
         for i in range(zc // BATCH):
             total = body(i, total)
         if not last:
@@ -491,12 +491,12 @@
                 old = vx_old[z]
                 vx[z] = pltpu.roll(old, nx - 1, 1)
                 b_east[z] = pltpu.roll(b[z], nx - 1, 1)
-                total = pack(total, vy_old[z], zl)
+                total = pack(total, vy_old[z], zl + zc)
                 ysend[0, c, y_row(1, 2), at, :] = old[0:1]
                 ysend[1, c, y_row(1, 2), at, :] = old[ny - 1 : ny]
             return total
 
-        xsend[c, x_row(1, 1)] = lax.fori_loop(0, zc // 8, body, plane)
+        vy_pack[c] = lax.fori_loop(0, zc // 8, body, plane)
 
     told_lane = lax.broadcasted_iota(jnp.int32, (1, 128), 1)
     in_place = quotient(told_lane, group_rows) == remainder(mine, 128 // group_rows)
@@ -897,6 +897,7 @@
             pltpu.VMEM((2, 2, chunks, zc, nx), f32),
             pltpu.VMEM((2, chunks, zc, nx), f32),
             pltpu.VMEM((2, chunks, zc, nx), f32),
+            pltpu.VMEM((chunks, ny, nx), f32),
             pltpu.VMEM((ngy, rup_group, slot_dev, lanes), jnp.bfloat16),
             pltpu.VMEM((rup_group, max(listed.shape[1], 128)), jnp.int32),
             pltpu.VMEM((rup_group, listed.shape[1], 128), jnp.int32),

time: 33.4 us -> 32.3 us (0.967)
  Pallas kernels: 32.6 us -> 31.5 us
    pallas_call x1, Pallas kernels: 29.8 us -> 28.7 us  [advance(): pl.pallas_call(functools.partial(step_kernel, dims), out_shape=[field(nz)...]
where the time goes in v8:
time: 32.3 us; the launch traced here: 32.2 us
  Pallas kernels  31.5 us (98%)
  between operations  0.64 us (2%)
    pallas_call x1, Pallas kernels, advance(): pl.pallas_call(functools.partial(step_kernel, dims), out_shape=[field(nz)...  28.7 us
    pallas_call x1, Pallas kernels, finish(): pl.pallas_call(functools.partial(finish_kernel, nz), out_shape=[jax.Shape...  2.87 us

profile of v8, /device:TPU:0, one launch (start us, length us, event | category | flops | bytes accessed | tf_op | source)
XLA Modules:
  0.0 32.2 jit_solution(10582378818399259617)
XLA Ops:
  0.6 28.7 %shard_map.155 = (f32[64,32,128]{2,1,0:T(8,128)S(1)}, f32[64,32,128]{2,1,0:T(8,128)S(1)}, f32[66,32,128]{2,1,0:T(8,128)S(1)}, f32[67,32,128]{2,1,0:T(8,128)S(1)}...) custom-call(f32[3,64,32,128]{3,2,1,0:T(8,128)} %refs_0_.1, ...), custom_call_target="tpu_custom_call" | custom-call | tf_op jit(solution)/shard_map/pallas_call | solution.py:855
  29.3 2.9 %shard_map.156 = (f32[3,64,32,128]{3,2,1,0:T(8,128)}, f32[64,32,128]{2,1,0:T(8,128)}, f32[64,32,128]{2,1,0:T(8,128)}, f32[64,256]{1,0:T(8,128)}, f32[8,64,256]{2,1,0:T(8,128)}) custom-call(f32[64,32,128]{2,1,0:T(8,128)S(1)} %get-tuple-element.15.refs_0_, f32[64,32,128]{2,1,0:T(8,128)S(1)} %get-tuple-element.16.refs_1_, ...), custom_call_target="tpu_custom_call" | custom-call | tf_op jit(solution)/shard_map/pallas_call | solution.py:943

commit v9 on v8

--- a/solution.py
+++ b/solution.py
@@ -61,7 +61,7 @@
     peer = peer + [{**peer[k // 2], **peer[2 + k % 2]} for k in range(4)]
 
     def load(i, h):
-        cuts = [0, zc, 2 * zc, nz] if i < 4 else [0, nz // 2, nz]
+        cuts = [0, zc, nz] if i < 4 else [0, nz // 2, nz]
         at = pl.ds(cuts[h], cuts[h + 1] - cuts[h])
         moved = pl.ds(cuts[h] + 1, cuts[h + 1] - cuts[h])
         src, dst = [
@@ -75,7 +75,7 @@
             (str_in.at[at], stg.at[at]),
             (mod_in.at[at], mod.at[at]),
         ][i]
-        return pltpu.make_async_copy(src, dst, in_sem.at[i + 9 * h if h < 2 else 18 + i])
+        return pltpu.make_async_copy(src, dst, in_sem.at[i + 9 * h])
 
     y_row = lambda r, k: sum(Y_ROWS[:r]) + k
     x_row = lambda r, k: sum(X_PACKS[:r]) + k
@@ -93,7 +93,7 @@
     ]
     for small in smalls:
         small.start()
-    for h in range(3):
+    for h in range(2):
         for i in range(4):
             load(i, h).start()
     for h in range(2):
@@ -207,7 +207,7 @@
         return after - before
 
     for c in range(chunks):
-        if c < 3:
+        if c < 2:
             for i in range(4):
                 load(i, c).wait()
 
@@ -421,16 +421,17 @@
     def sweep(r, c):
         last, first = (r == STEPS - 1, r == 0)
         n = r + 1
+        batch = zc if first else BATCH
         p_from, w_from = (p_old, vy_old) if first else (p, vy)
 
         def body(i, total):
-            base = i * BATCH
+            base = i * batch
             z0 = c * zc + base
-            ps = [p_from[z0 + 1 + j] for j in range(BATCH + 2)]
-            bs = [b[z0 + j] for j in range(BATCH + 1)]
+            ps = [p_from[z0 + 1 + j] for j in range(batch + 2)]
+            bs = [b[z0 + j] for j in range(batch + 1)]
             zs = [vz[z0], vz[z0 + 1]]
             vs, ws, new_p, outer = ([], [], [], [])
-            for j in range(BATCH):
+            for j in range(batch):
                 zl = base + j
                 at = pl.ds(zl, 1)
                 turn = nx - 2 - 4 * zl
@@ -446,7 +447,7 @@
                 vs.append(speed - shifted * (ahead - ps[j]))
                 south, north = (yrecv[r][0, c, 1, at, :], yrecv[r][1, c, 0, at, :])
                 ws.append(w_from[z0 + j] - bs[j] * d_y(ps[j], south, north))
-            for j in range(BATCH):
+            for j in range(batch):
                 zl = base + j
                 at = pl.ds(zl, 1)
                 turned = pltpu.roll(vs[j], 2, 1)
@@ -459,7 +460,7 @@
                 mem = mem - rel[z0 + j] * (mem + stg[z0 + j] * spread)
                 m[z0 + j] = mem
                 new_p.append(ps[j] - mod[z0 + j] * (spread + mem))
-            for j in range(BATCH):
+            for j in range(batch):
                 zl = base + j
                 at = pl.ds(zl, 1)
                 vz[z0 + j + 2] = zs[j + 2]
@@ -475,7 +476,7 @@
             return total
 
         total = vy_pack[c] if first else plane
-        for i in range(zc // BATCH):
+        for i in range(zc // batch):
             total = body(i, total)
         if not last:
             xsend[c, x_row(n, 0)] = total
@@ -907,7 +908,7 @@
             pltpu.VMEM((all_rows, width), f32),
             pltpu.VMEM((all_rows, width), f32),
             pltpu.VMEM((ngx, STEPS, 1, 128), f32),
-            pltpu.SemaphoreType.DMA((22,)),
+            pltpu.SemaphoreType.DMA((18,)),
             pltpu.SemaphoreType.DMA((4,)),
             pltpu.SemaphoreType.DMA((8,)),
             pltpu.SemaphoreType.DMA((2, chunks, 4)),

time: 32.3 us -> 32.1 us (level)
  no operation moved by 1% of the time
where the time goes in v9:
time: 32.1 us; the launch traced here: 32 us
  Pallas kernels  31.3 us (98%)
  between operations  0.64 us (2%)
    pallas_call x1, Pallas kernels, advance(): pl.pallas_call(functools.partial(step_kernel, dims), out_shape=[field(nz)...  28.5 us
    pallas_call x1, Pallas kernels, finish(): pl.pallas_call(functools.partial(finish_kernel, nz), out_shape=[jax.Shape...  2.87 us

profile of v9, /device:TPU:0, one launch (start us, length us, event | category | flops | bytes accessed | tf_op | source)
XLA Modules:
  0.0 32.0 jit_solution(11328595292492724587)
XLA Ops:
  0.6 28.5 %shard_map.155 = (f32[64,32,128]{2,1,0:T(8,128)S(1)}, f32[64,32,128]{2,1,0:T(8,128)S(1)}, f32[66,32,128]{2,1,0:T(8,128)S(1)}, f32[67,32,128]{2,1,0:T(8,128)S(1)}...) custom-call(f32[3,64,32,128]{3,2,1,0:T(8,128)} %refs_0_.1, ...), custom_call_target="tpu_custom_call" | custom-call | tf_op jit(solution)/shard_map/pallas_call | solution.py:856
  29.1 2.9 %shard_map.156 = (f32[3,64,32,128]{3,2,1,0:T(8,128)}, f32[64,32,128]{2,1,0:T(8,128)}, f32[64,32,128]{2,1,0:T(8,128)}, f32[64,256]{1,0:T(8,128)}, f32[8,64,256]{2,1,0:T(8,128)}) custom-call(f32[64,32,128]{2,1,0:T(8,128)S(1)} %get-tuple-element.15.refs_0_, f32[64,32,128]{2,1,0:T(8,128)S(1)} %get-tuple-element.16.refs_1_, ...), custom_call_target="tpu_custom_call" | custom-call | tf_op jit(solution)/shard_map/pallas_call | solution.py:944
